TPU v7x, 256 devices: a whole 4x4x8 slice. The times are simulated.
256 devices in a mesh: batch: 16 (over x, y_hi, core), seq: 16 (over z, y_lo).
Axes of the slice: x: 4, y: 4 (y_hi: 2, y_lo: 2; y = y_hi * 2 + y_lo), z: 8, core: 2. Of those that a mesh axis runs over, the one named last changes fastest.
Arguments:
- dna_features: bfloat16 [131072, 768], P(('batch', 'seq')), parts along dimension 0, may hold values from -6 to 6
- conv_weight: bfloat16 [5, 768, 1536], P(None, None, 'seq'), may hold values from -0.09375 to 0.09375
- conv_bias: float32 [1536], replicated, may hold values from -3 to 3
- norm_gain: float32 [1536], replicated, may hold values from 0.5 to 1.5
- qkv_weight: bfloat16 [3, 1536, 768], P(None, None, 'seq'), may hold values from -0.15625 to 0.15625
- head_scale: float32 [4], replicated, may hold values from 1.5 to 60, as said below
- out_weight: bfloat16 [768, 1536], P(None, 'seq'), may hold values from -0.21875 to 0.21875
Outputs:
- block_out: bfloat16 [65536, 1536], P(('batch', 'seq')), parts along dimension 0
There are 16 independent parts, one for each index of `batch`. A program takes and returns all parts, laid end to end along the dimension named above; an argument that names none is the same for every part. Nothing has to cross between parts.
Inputs may be any that keep to these rules, and one draw needn't show every extreme that they name: `head_scale`: one positive factor per head.
All inputs are finite; a program needn't handle non-finite values.
Results may differ from a plain program's by a relative error of at most 0.017.
The roundings to bfloat16 on the way count: a program that leaves them out, or rounds other values in their place, can miss the bound.
Values may be sent and summed in bfloat16 or wider, within the bound.
No kernel may reach another device: no remote copies, remote signals or barrier semaphores. Data moves between devices by JAX's collectives and lax.ppermute only.
A program may use at most 128 MiB of HBM per device.

v0:
```python
import math

import jax
import jax.numpy as jnp
from jax import lax
from jax.sharding import PartitionSpec as P

HEADS = 4
HEAD_DIM = 192


def extended(block, sides, width):
    for axis, dim in sides:
        count = lax.axis_size(axis)
        forward = [(i, i + 1) for i in range(count - 1)]
        backward = [(target, source) for source, target in forward]
        low = lax.ppermute(
            lax.slice_in_dim(block, block.shape[dim] - width, None, axis=dim), axis, forward
        )
        high = lax.ppermute(lax.slice_in_dim(block, 0, width, axis=dim), axis, backward)
        block = jnp.concatenate([low, block, high], axis=dim)
    return block


def conv_whole(padded, kernel, bias_cols, positions):
    col_count = kernel.shape[2]
    summed = jnp.zeros((positions, col_count), jnp.float32) + bias_cols
    for tap in range(kernel.shape[0]):
        summed = summed + jnp.dot(
            padded[tap : tap + positions], kernel[tap], preferred_element_type=jnp.float32
        )
    return jnp.max(summed.reshape(positions // 2, 2, col_count), axis=1).astype(jnp.bfloat16)


def shards(dna_features, conv_weight, conv_bias, norm_gain, qkv_weight, head_scale, out_weight):
    tap_count = conv_weight.shape[0]
    half_taps = tap_count // 2
    activated = jax.nn.gelu(dna_features.astype(jnp.float32), approximate=True).astype(jnp.bfloat16)
    positions = activated.shape[0]
    padded = extended(activated, (("seq", 0),), half_taps)
    pooled = conv_whole(
        padded, lax.all_gather(conv_weight, "seq", axis=2, tiled=True), conv_bias, positions
    )
    tok_count = pooled.shape[0]
    values32 = pooled.astype(jnp.float32)
    centre = jnp.mean(values32, axis=1, keepdims=True)
    spread = jnp.mean((values32 - centre) ** 2, axis=1, keepdims=True)
    normed = ((values32 - centre) * lax.rsqrt(spread + 1e-05) * norm_gain).astype(jnp.bfloat16)
    projected = jnp.einsum(
        "tc,jcn->jtn",
        normed,
        lax.all_gather(qkv_weight, "seq", axis=2, tiled=True),
        preferred_element_type=jnp.float32,
    ).astype(jnp.bfloat16)
    queries = projected[0].reshape(tok_count, HEADS, HEAD_DIM)
    factor = head_scale / math.sqrt(HEAD_DIM)
    run_max = jnp.full((HEADS, tok_count), -1e30, jnp.float32)
    key_rows = lax.all_gather(projected[1], "seq", axis=0, tiled=True).reshape(-1, HEADS, HEAD_DIM)
    value_rows = lax.all_gather(projected[2], "seq", axis=0, tiled=True).reshape(
        -1, HEADS, HEAD_DIM
    )
    scores = (
        jnp.einsum("thd,nhd->htn", queries, key_rows, preferred_element_type=jnp.float32)
        * factor[:, None, None]
    )
    new_max = jnp.maximum(run_max, jnp.max(scores, axis=2))
    weights = jnp.exp(scores - new_max[:, :, None])
    new_sum = jnp.sum(weights, axis=2)
    new_acc = jnp.einsum(
        "htn,nhd->htd", weights.astype(jnp.bfloat16), value_rows, preferred_element_type=jnp.float32
    )
    heads_out = new_acc / new_sum[:, :, None]
    attended = (
        heads_out.transpose(1, 0, 2).reshape(tok_count, HEADS * HEAD_DIM).astype(jnp.bfloat16)
    )
    base = pooled.astype(jnp.float32)
    return (
        base
        + jnp.dot(
            attended,
            lax.all_gather(out_weight, "seq", axis=1, tiled=True),
            preferred_element_type=jnp.float32,
        )
    ).astype(jnp.bfloat16)


def solution(mesh):
    placed = (
        P(("batch", "seq"), None),
        P(None, None, "seq"),
        P(),
        P(),
        P(None, None, "seq"),
        P(),
        P(None, "seq"),
    )
    return jax.shard_map(
        shards, mesh=mesh, in_specs=placed, out_specs=P(("batch", "seq"), None), check_vma=False
    )
```

profile of v0, /device:TPU:6, one launch (start us, length us, event | category | flops | bytes accessed | tf_op | source)
XLA Modules:
  0.0 799.3 jit_solution(1986249537164564894)
XLA Ops:
  6.5 0.0 all-gather.8.cloned.1.call-start
  6.5 0.7 all-gather.8.cloned.1.call-update
  7.3 0.0 all-gather.10.cloned.1.call-start
  7.3 0.7 all-gather.10.cloned.1.call-update
  8.0 0.0 all-gather.14.cloned.1.call-start
  8.1 1.7 fusion.23
  9.7 3.5 collective-permute-start
  13.2 1.3 collective-permute-start.1
  14.5 0.0 collective-permute-done
  14.5 248.5 %all-gather.8.cloned.1.call-done = bf16[5,768,1536]{1,2,0:T(8,128)(2,1)} async-done(((bf16[5,768,96]{1,2,0:T(8,128)(2,1)}), bf16[5,768,1536]{1,2,0:T(8,128)(2,1)}) %all-gather.8.cloned.1.call-update) | async-done | bytes 11796496 | tf_op jit(solution)/shard_map/all_gather | solution.py:42
  263.0 3.2 fusion.12
  266.3 0.0 slice-start.2
  266.3 0.0 copy-start
  266.3 0.0 collective-permute-done.1
  266.3 3.2 fusion.10
  269.5 0.0 slice-done
  269.5 0.0 slice-done.1
  269.6 0.0 slice-done.2
  269.6 0.0 copy-done
  269.6 0.0 copy-start.1
  269.6 1.5 fusion.11
  271.1 0.0 copy-done.1
  271.1 1.5 fusion.7
  272.6 1.4 fusion.8
  274.1 1.5 reshape.30
  275.6 5.2 reduce_max.18
  280.9 0.2 convert_reduce_fusion
  281.1 0.3 fusion.15
  281.4 141.0 %all-gather.10.cloned.1.call-done = bf16[3,1536,768]{1,2,0:T(8,128)(2,1)} async-done(((bf16[3,1536,48]{1,2,0:T(8,128)(2,1)}), bf16[3,1536,768]{1,2,0:T(8,128)(2,1)}) %all-gather.10.cloned.1.call-update) | async-done | bytes 7077904 | tf_op jit(solution)/shard_map/all_gather | solution.py:52
  422.4 0.0 copy-done.2
  422.4 5.1 fusion.24
  427.6 0.0 copy-start.3
  427.6 1.0 fusion.50
  428.6 0.0 all-gather.14.cloned.1.call-update
  428.6 0.2 all-gather.16.cloned.1.call-start
  428.8 0.3 all-gather.16.cloned.1.call-update
  429.2 0.0 all-gather.12.cloned.1.call-start
  429.2 0.5 all-gather.12.cloned.1.call-update
  429.8 0.2 copy.11
  429.9 139.9 %all-gather.14.cloned.1.call-done = bf16[1,4096,768]{2,1,0:T(8,128)(2,1)} async-done(((bf16[1,256,768]{2,1,0:T(8,128)(2,1)}), bf16[1,4096,768]{2,1,0:T(8,128)(2,1)}) %all-gather.14.cloned.1.call-update) | async-done | bytes 6291472 | tf_op jit(solution)/shard_map/all_gather | solution.py:58
  569.9 8.7 %copy.12 = bf16[1,4096,768]{1,2,0:T(8,128)(2,1)} copy(bf16[1,4096,768]{2,1,0:T(8,128)(2,1)} %all-gather.14.cloned.1.call-done) | data formatting | bytes 12582912 | tf_op jit(solution)/shard_map/all_gather | solution.py:58
  578.6 134.2 %all-gather.16.cloned.1.call-done = bf16[1,4096,768]{2,1,0:T(8,128)(2,1)} async-done(((bf16[1,256,768]{2,1,0:T(8,128)(2,1)}), bf16[1,4096,768]{2,1,0:T(8,128)(2,1)}) %all-gather.16.cloned.1.call-update) | async-done | bytes 6291472 | tf_op jit(solution)/shard_map/all_gather | solution.py:59
  712.8 8.7 %copy.13 = bf16[1,4096,768]{1,2,0:T(8,128)(2,1)} copy(bf16[1,4096,768]{2,1,0:T(8,128)(2,1)} %all-gather.16.cloned.1.call-done) | data formatting | bytes 12582912 | tf_op jit(solution)/shard_map/all_gather | solution.py:59
  721.5 11.1 %multiply_reduce_fusion = (f32[4,256]{1,0:T(4,128)S(1)}, f32[4,256,4096]{2,1,0:T(8,128)}) fusion(f32[4]{0:T(128)S(1)} %broadcast_multiply_fusion.1, bf16[256,4,192]{0,2,1:T(8,128)(2,1)S(1)} %bitcast.41, bf16[4096,4,192]{0,2,1:T(8,128)(2,1)} %bitcast.37), kind=kOutput, calls=%fused_computation.1 | convolution fusion | flops 1619000320 | bytes 23466000 | tf_op jit(solution)/shard_map/thd,nhd->htn/dot_general | solution.py:63
  732.6 8.7 %fusion = f32[4,256]{1,0:T(4,128)S(1)} fusion(f32[4,256,4096]{2,1,0:T(8,128)} %get-tuple-element.11, f32[4,256]{1,0:T(4,128)S(1)} %broadcast_maximum_fusion, f32[4]{0:T(128)S(1)} %broadcast_multiply_fusion.1), kind=kLoop, calls=%fused_computation.2 | loop fusion | flops 12581888 | bytes 16785424 | tf_op jit(solution)/shard_map/reduce_sum | solution.py:68
  741.3 10.8 %fusion.31 = bf16[256,4,192]{0,2,1:T(8,128)(2,1)S(1)} fusion(bf16[4096,4,192]{0,2,1:T(8,128)(2,1)} %bitcast.38, f32[4,256,4096]{2,1,0:T(8,128)} %get-tuple-element.11, f32[4,256]{1,0:T(4,128)S(1)} %broadcast_maximum_fusion, f32[4]{0:T(128)S(1)} %broadcast_multiply_fusion.1, f32[256,4]{0,1:T(4,128)S(1)} %bitcast.42), kind=kOutput, calls=%fused_computation.43 | convolution fusion | flops 1623588864 | bytes 23470096 | tf_op jit(solution)/shard_map/htn,nhd->htd/dot_general | solution.py:69
  752.0 37.4 %all-gather.12.cloned.1.call-done = bf16[768,1536]{0,1:T(8,128)(2,1)} async-done(((bf16[768,96]{0,1:T(8,128)(2,1)}), bf16[768,1536]{0,1:T(8,128)(2,1)}) %all-gather.12.cloned.1.call-update) | async-done | bytes 2359312 | tf_op jit(solution)/shard_map/all_gather | solution.py:81
  789.4 3.4 fusion.9
  (10 shorter events, 0.0 us)
Async XLA Ops:
  6.5 256.5 %all-gather.8.cloned.1.call-start = ((), (), s32[]{:S(2)}) async-start(), calls=%async_computation | async-start | bytes 12533760 | tf_op jit(solution)/shard_map/all_gather | solution.py:42
  7.3 415.2 %all-gather.10.cloned.1.call-start = ((), (), s32[]{:S(2)}) async-start(), calls=%async_computation.1 | async-start | bytes 7520256 | tf_op jit(solution)/shard_map/all_gather | solution.py:52
  8.0 561.9 %all-gather.14.cloned.1.call-start = ((), (), s32[]{:S(2)}) async-start(), calls=%async_computation.3 | async-start | bytes 6684672 | tf_op jit(solution)/shard_map/all_gather | solution.py:58
  9.7 4.8 collective-permute-start
  13.2 253.0 %collective-permute-start.1 = (bf16[2,768]{1,0:T(2,128)(2,1)S(1)}, bf16[2,768]{1,0:T(2,128)(2,1)S(1)}, u32[]{:S(2)}, u32[]{:S(2)}) collective-permute-start(bf16[2,768]{1,0:T(2,128)(2,1)S(1)} %get-tuple-element.9), channel_id=1, source_target_pairs={{1,0},{2,1},{3,2},{4,3},{5,4},{6,5},{7,6},{8,7},{9,8},{10,9},{11,1... | collective-permute-start | bytes 9224 | tf_op jit(solution)/shard_map/ppermute | solution.py:20
  263.0 6.5 slice-start
  263.0 6.5 slice-start.1
  266.3 3.3 slice-start.2
  266.3 3.3 copy-start
  269.6 1.6 copy-start.1
  275.6 146.8 %copy-start.2 = (f32[1536]{0:T(1024)S(1)}, f32[1536]{0:T(1024)}, u32[]{:S(2)}) copy-start(f32[1536]{0:T(1024)} %param.10) | copy-start | bytes 18436
  427.6 2.2 copy-start.3
  428.6 284.2 %all-gather.16.cloned.1.call-start = ((), (), s32[]{:S(2)}) async-start(), calls=%async_computation.4 | async-start | bytes 6684672 | tf_op jit(solution)/shard_map/all_gather | solution.py:59
  429.2 360.3 %all-gather.12.cloned.1.call-start = ((), (), s32[]{:S(2)}) async-start(), calls=%async_computation.2 | async-start | bytes 2506752 | tf_op jit(solution)/shard_map/all_gather | solution.py:81
Sparse Core Ops, SparseCore 0:
  9.1 253.8 all-gather.7
  264.8 157.5 all-gather.9
  428.7 141.1 all-gather.13
  571.5 141.2 all-gather.15
  714.4 74.9 all-gather.11
where the time goes:
time: 800 us; the launch traced here: 799 us
  waiting for transfers between devices  703 us (88%)
  matrix products  41.3 us (5%)
  local copies, waits for them, and re-layouts  20.1 us (3%)
  other arithmetic  16.2 us (2%)
  between operations  13.3 us (2%)
    all_gather x1, waiting for transfers between devices, shards(): lax.all_gather(conv_weight, 'seq', axis=2, tiled=True)  248 us
    all_gather x1, waiting for transfers between devices, shards(): lax.all_gather(qkv_weight, 'seq', axis=2, tiled=True)  141 us
    all_gather x1, waiting for transfers between devices, shards(): lax.all_gather(projected[1], 'seq', axis=0, tiled=True)  140 us
    all_gather x1, waiting for transfers between devices, shards(): lax.all_gather(projected[2], 'seq', axis=0, tiled=True)  134 us
    all_gather x1, waiting for transfers between devices, shards(): lax.all_gather(out_weight, 'seq', axis=1, tiled=True)  37.4 us
  transfers between devices with their start and end apart: 7, of which 5 were waited for; matrix products, arithmetic and copies ran while one was open for 9% of the time, Pallas kernels for 0%

commit v1 on v0

v1 whole, which is shorter than its diff:
```python
import math

import jax
import jax.numpy as jnp
import numpy as np
from jax import lax
from jax.experimental import pallas as pl
from jax.experimental.pallas import tpu as pltpu
from jax.sharding import PartitionSpec as P

HEADS = 4
HEAD_DIM = 192
AXES = ("batch", "seq")
F32 = jnp.float32
BF16 = jnp.bfloat16
DELTAS = (0, 1, -1, 2)
SLOTS = [(a, b) for b in range(4) for a in range(4)]
BYTES = 8_000_000
VMEM_BYTES = 60 * 1024 * 1024


def place(index):
    low, z = index % 2, (index // 2) % 8
    core, high, x = (index // 16) % 2, (index // 32) % 2, index // 64
    return x, 2 * high + low, z, core


def flat(x, y, z, core):
    x, y, z = x % 4, y % 4, z % 8
    return (((x * 2 + y // 2) * 2 + core) * 8 + z) * 2 + y % 2


def send(value, target, name):
    pairs = [(i, flat(*target(*place(i)))) for i in range(256)]
    with jax.named_scope(name):
        return lax.ppermute(value, AXES, pairs)


SPREAD = {
    (0, 0): ((3, 1, 0, 2), (0, 2, 1, 3), (2, 0, 3, 1), (1, 3, 2, 0)),
    (0, 1): ((2, 3, 0, 1), (0, 2, 1, 3), (3, 1, 2, 0), (1, 0, 3, 2)),
    (1, 0): ((1, 0, 3, 2), (0, 2, 1, 3), (3, 1, 2, 0), (2, 3, 0, 1)),
    (1, 1): ((2, 1, 3, 0), (0, 2, 1, 3), (3, 0, 2, 1), (1, 3, 0, 2)),
}


def origin_z(x, z, core):
    return SPREAD[core, z // 4][x % 4][z % 4]


def spread_z(x, y, z, core):
    (target,) = [i for i in range(4) if origin_z(x, 4 * core + i, z // 4) == z % 4]
    return x, y, 4 * core + target, z // 4


def first(step):
    return lambda x, y, z, core: (x + step, y, z, core) if core == 0 else (x, y + step, z, core)


def second(step):
    return lambda x, y, z, core: (x, y + step, z, core) if core == 0 else (x + step, y, z, core)


def other_core(x, y, z, core):
    return x, y, z, 1 - core


def other_low(x, y, z, core):
    return x, y ^ 1, z, core


def after(value, *others):
    zero = sum((o[(0,) * o.ndim].astype(F32) * 0.0 for o in others), F32(0.0))
    return value + zero.astype(value.dtype)


def stacked(blocks):
    out = jnp.zeros((len(blocks), *blocks[0].shape), blocks[0].dtype)
    for at, block in enumerate(blocks):
        out = lax.dynamic_update_slice(out, block[None], (at,) + (0,) * block.ndim)
    return out


def gather_first(block):
    return [block] + [send(block, first(step), "weights_first") for step in (1, -1, 2)]


ROWS, CORE, SENDS, HEAD, STEPS, OTHER, FROM = 0, 16, 17, 25, 26, 30, 46


def slot_rows(x, y, z, core):
    rows = []
    for a, b in SLOTS:
        along, across = (DELTAS[a], DELTAS[b]) if core == 0 else (DELTAS[b], DELTAS[a])
        px, py = (x - along) % 4, (y - across) % 4
        rows.append(origin_z(px, z, core) * 4 + (py % 2) * 2 + py // 2)
    return rows


def shift(m, core, parity):
    return (2, -2, 0, 4)[m] + core - parity


def to_head(m):
    return lambda x, y, z, core: (x, y, (z + shift(m, core, z % 2)) % 8, z % 2)


BACK = {
    (0, 0): ((1, 2, 3, 0), (3, 0, 1, 2), (0, 3, 2, 1), (2, 1, 0, 3)),
    (0, 1): ((2, 3, 0, 1), (0, 1, 2, 3), (1, 2, 3, 0), (3, 0, 1, 2)),
    (1, 0): ((0, 1, 3, 2), (3, 2, 1, 0), (2, 3, 0, 1), (1, 0, 2, 3)),
    (1, 1): ((2, 3, 0, 1), (0, 1, 2, 3), (3, 0, 1, 2), (1, 2, 3, 0)),
}


def back_z(n, z, core):
    return 2 * BACK[(z // 2) % 2, core][n][2 * (z // 4) + z % 2] + core


def to_tokens(n):
    return lambda x, y, z, core: (x, y, back_z(n, z, core), (z // 2) % 2)


def integers(index):
    x, y, z, core = place(index)
    row = slot_rows(x, y, z, core) + [core]
    for m in range(4):
        target = (z + shift(m, core, z % 2)) % 8
        row += [0 if (target // 2) % 2 == core else 1, target // 4]
    row.append(2 * (z % 2) + z // 4)
    source = {(z - shift(m, z % 2, core)) % 8: m for m in range(4)}
    row += [source[back_z(n, z, core)] for n in range(4)]
    row += slot_rows(x, y, z, 1 - core)
    for n in range(4):
        (origin,) = [
            a for a in range(8) if (a // 2) % 2 == core and back_z(n, a, z % 2) == z
        ]
        row.append(2 * (origin % 2) + origin // 4)
    return row


TABLE = np.array([integers(i) for i in range(256)], np.int32)


def nt(a, b):
    return lax.dot_general(a, b, (((1,), (1,)), ((), ())), preferred_element_type=F32)


def acts_kernel(own, other, out):
    for which, window in enumerate((own, other)):
        for odd in range(2):
            row = lax.broadcasted_iota(jnp.int32, (272, 528), 0)
            col = lax.broadcasted_iota(jnp.int32, (272, 528), 1)
            pick = jnp.where(col == 2 * row + odd, 1.0, 0.0).astype(BF16)
            rows = jnp.dot(pick, window[...], preferred_element_type=F32)
            for step in range(3):
                out[2 * step + odd, pl.ds(256 * which, 256), :] = rows[step : step + 256].astype(BF16)


def conv_kernel(base, table, acts, bias, *refs):
    *groups, out, weights, sems = refs
    groups = groups[-3:] if base == 0 else groups[-2:]
    copies = [[] for _ in range(5)]
    for tap in range(5):
        at = 0
        for group in groups:
            for slot in range(group.shape[0]):
                copy = pltpu.make_async_copy(
                    group.at[slot, tap], weights.at[tap, at], sems.at[tap, at]
                )
                copy.start()
                copies[tap].append(copy)
                at += 1
    for tap in range(5):
        for copy in copies[tap]:
            copy.wait()

    def block(number, _):
        even = odd = None
        for tap in range(5):
            w = weights[tap, pl.ds(4 * number, 4)].reshape(192, 768)
            e, o = nt(acts[tap], w), nt(acts[tap + 1], w)
            even = e if even is None else even + e
            odd = o if odd is None else odd + o
        at = base + 4 * number
        shift = jnp.concatenate([bias[table[ROWS + at + i]] for i in range(4)], axis=1)
        pooled = (jnp.maximum(even, odd) + shift).T.astype(BF16)
        out[pl.ds(4 * number, 4)] = pooled.reshape(4, 48, 512)
        return 0

    lax.fori_loop(0, weights.shape[1] // 4, block, 0)


def project_kernel(table, ma, mb, ta, tb, gain, g0, g1, g2, g3, g4, out, last, tokens, weights, normed, sems):
    at = 0
    copies = []
    for group in (g0, g1, g2, g3, g4):
        for slot in range(group.shape[0]):
            row = table[ROWS + at]
            for source, target in (
                (group.at[slot, pl.ds(0, 3)], weights.at[:, row % 2, row // 2]),
                (group.at[slot, 3], last.at[row]),
            ):
                copy = pltpu.make_async_copy(source, target, sems.at[len(copies)])
                copy.start()
                copies.append(copy)
            at += 1
    core = table[CORE]
    for at in range(16):
        a, b = (ma, at) if at < 12 else (mb, at - 12)
        tokens[core, table[ROWS + at]] = a[b]
        a = ta if at < 12 else tb
        row = table[OTHER + at]
        tokens[1 - core, row, :, :256] = a[b, :, 256:]
        tokens[1 - core, row, :, 256:] = a[b, :, :256]

    def norm(part, _):
        cols = pl.ds(pl.multiple_of(256 * part, 256), 256)
        values = [tokens[half, :, :, cols].astype(F32).reshape(768, 256) for half in range(2)]
        centre = sum(jnp.sum(v, axis=0, keepdims=True) for v in values) / 1536.0
        values = [v - centre for v in values]
        spread = sum(jnp.sum(v * v, axis=0, keepdims=True) for v in values) / 1536.0
        rate = lax.rsqrt(spread + 1e-05)
        for half in range(2):
            normed[part, half] = (values[half] * rate * gain[half]).astype(BF16)
        return 0

    lax.fori_loop(0, 2, norm, 0)
    for copy in copies:
        copy.wait()

    def one(m, _):
        part, head = table[SENDS + 2 * m], table[SENDS + 1 + 2 * m]
        total = None
        for half in range(2):
            w = weights[:, half, pl.ds(4 * head, 4)].reshape(576, 768)
            term = jnp.dot(w, normed[part, half], preferred_element_type=F32)
            total = term if total is None else total + term
        out[m] = total.astype(BF16).reshape(3, 192, 256)
        return 0

    lax.fori_loop(0, 4, one, 0)


def scores_of(query, groups, scores, scale):
    top = None
    for at, group in enumerate(groups):
        keys = jnp.concatenate([group[i, 0] for i in range(group.shape[0])], axis=1)
        s = jnp.dot(query, keys, preferred_element_type=F32) * scale
        scores[at, :, : s.shape[1]] = s
        t = jnp.max(s, axis=1, keepdims=True)
        top = t if top is None else jnp.maximum(top, t)
    return top


def sums_of(top, groups, scores):
    total = acc = None
    for at, group in enumerate(groups):
        values = jnp.concatenate([group[i, 1] for i in range(group.shape[0])], axis=1)
        p = jnp.exp(scores[at, :, : values.shape[1]] - top)
        t = jnp.sum(p, axis=1, keepdims=True)
        o = nt(p.astype(BF16), values)
        total = t if total is None else total + t
        acc = o if acc is None else acc + o
    return total, acc


def attend_kernel(table, factor, queries, g0, g1, g2, g3, tops, totals, accs, scores):
    scale = factor[table[HEAD]] * (1 / math.sqrt(HEAD_DIM))

    def one(part, _):
        groups = (g0, g1, g2, g3)
        top = scores_of(queries[part].T, groups, scores, scale)
        total, acc = sums_of(top, groups, scores)
        tops[part] = jnp.broadcast_to(top, (256, 128))
        totals[part] = jnp.broadcast_to(total, (256, 128))
        accs[part] = acc
        return 0

    lax.fori_loop(0, 4, one, 0)


def finish_kernel(base, table, factor, *refs):
    queries, g0, g1, g2, g3, tops, totals, accs, out, scores = refs[-10:]
    scale = factor[table[HEAD]] * (1 / math.sqrt(HEAD_DIM))

    def one(step, _):
        part = table[STEPS + base[0] + step]
        groups = (g0, g1, g2, g3)
        before = tops[part, :, :1]
        top = jnp.maximum(before, scores_of(queries[part].T, groups, scores, scale))
        total, acc = sums_of(top, groups, scores)
        keep = jnp.exp(before - top)
        total = total + totals[part, :, :1] * keep
        acc = acc + accs[part] * keep
        out[step] = (acc / total).astype(BF16).T
        return 0

    lax.fori_loop(0, 2, one, 0)


def base_kernel(tokens, out):
    for half in range(2):
        out[:, 768 * half : 768 * half + 768] = tokens[half, :, :, :256].reshape(768, 256).T


def out_kernel(table, h0, h1, h2, h3, base, mine, theirs, out, weights, attended, sems):
    core = table[CORE]
    copies = []
    for side, (group, which) in enumerate(((mine, core), (theirs, 1 - core))):
        copy = pltpu.make_async_copy(group, weights.at[which], sems.at[side])
        copy.start()
        copies.append(copy)
    for number, head in enumerate((h0, h1, h2, h3)):
        attended[table[FROM + number]] = head[...].T
    rows = jnp.concatenate([attended[h] for h in range(4)], axis=1)
    for copy in copies:
        copy.wait()
    for half in range(2):
        lanes = slice(768 * half, 768 * half + 768)
        w = weights[half].reshape(768, 768)
        out[:, lanes] = (base[:, lanes].astype(F32) + nt(rows, w)).astype(BF16)


SMEM = pl.BlockSpec(memory_space=pltpu.SMEM)
VMEM = pl.BlockSpec(memory_space=pltpu.VMEM)
ANY = pl.BlockSpec(memory_space=pl.ANY)


def call(kernel, ins, outs, scratch, flops, *args):
    kernel_name = getattr(kernel, '__name__', 'kernel').replace('<lambda>', 'conv_kernel')
    return pl.pallas_call(
        kernel,
        out_shape=outs,
        in_specs=ins,
        out_specs=jax.tree.map(lambda _: VMEM, outs),
        scratch_shapes=scratch,
        compiler_params=pltpu.CompilerParams(vmem_limit_bytes=VMEM_BYTES),
        cost_estimate=pl.CostEstimate(flops=flops, bytes_accessed=BYTES, transcendentals=0),
        name=kernel_name,
    )(*args)


def shape(*dims, dtype=BF16):
    return jax.ShapeDtypeStruct(dims, dtype)


def shards(dna_features, conv_weight, conv_bias, norm_gain, qkv_weight, head_scale, out_weight):
    batch, seq = lax.axis_index("batch"), lax.axis_index("seq")
    core, high = batch % 2, (batch // 2) % 2
    table = lax.dynamic_index_in_dim(TABLE, batch * 16 + seq, 0, keepdims=False)

    taps = lax.dynamic_slice_in_dim(conv_weight.transpose(0, 2, 1), 48 * high, 48, axis=1)
    qkv = lax.dynamic_slice_in_dim(qkv_weight.transpose(0, 2, 1), 768 * high, 768, axis=2)
    last = lax.dynamic_slice_in_dim(out_weight.T, 48 * high, 48, axis=0)
    block = jnp.concatenate([taps, qkv[1:], qkv[:1], last[None]], axis=0)
    features = after(dna_features, block)
    block = send(block, spread_z, "weights_z")

    activated = jax.nn.gelu(features.astype(F32), approximate=True).astype(BF16)
    forward = [(16 * b + i, 16 * b + i + 1) for b in range(16) for i in range(15)]
    backward = [(t, s) for s, t in forward]
    before = lax.ppermute(activated[-2:], AXES, forward)
    behind = lax.ppermute(activated[:2], AXES, backward)
    padded = jnp.concatenate([before, activated, behind, jnp.zeros((12, 768), BF16)], axis=0)
    acts = call(
        acts_kernel,
        [VMEM] * 2,
        shape(6, 512, 768),
        [],
        1_000_000_000,
        padded,
        send(padded, other_core, "acts_core"),
    )

    pieces = gather_first(block)
    stack = stacked([after(pieces[0][:5], acts)] + [p[:5] for p in pieces[1:]])
    low, high_stack = [send(stack, second(step), "conv_second") for step in (1, -1)]
    far = (
        send(low[:2], second(1), "conv_far"),
        send(high_stack[2:], second(-1), "conv_far"),
    )
    qkv_stack = stacked([after(pieces[0][5:], low, high_stack)] + [p[5:] for p in pieces[1:]])
    qkv_near = [send(qkv_stack, second(step), "qkv_second") for step in (1, -1)]
    qkv_groups = (
        qkv_stack,
        *qkv_near,
        send(qkv_near[0][:2], second(1), "qkv_far"),
        send(qkv_near[1][2:], second(-1), "qkv_far"),
    )
    bias = lax.dynamic_slice_in_dim(conv_bias, 768 * core, 768).reshape(16, 1, 48)

    def conv(base, groups, *earlier):
        count = sum(g.shape[0] for g in groups)
        return call(
            lambda *refs: conv_kernel(base, *refs),
            [SMEM, VMEM, VMEM] + [ANY] * (len(groups) + len(earlier)),
            shape(count, 48, 512),
            [pltpu.VMEM((5, count, 48, 768), BF16), pltpu.SemaphoreType.DMA((5, count))],
            375_000_000 * count,
            table,
            acts,
            bias,
            *earlier,
            *groups,
        )

    mine = [conv(0, (stack, low, high_stack))]
    mine.append(conv(12, far, mine[0]))
    theirs = [send(m, other_core, "pooled_core") for m in mine]
    blocks, last, tokens = call(
        project_kernel,
        [SMEM] + [VMEM] * 5 + [ANY] * 5,
        [shape(4, 3, 192, 256), shape(16, 48, 768), shape(2, 16, 48, 512)],
        [
            pltpu.VMEM((3, 2, 8, 48, 768), BF16),
            pltpu.VMEM((2, 2, 768, 256), BF16),
            pltpu.SemaphoreType.DMA((32,)),
        ],
        1_800_000_000,
        table,
        *mine,
        *theirs,
        norm_gain.reshape(2, 768, 1),
        *qkv_groups,
    )

    own = [send(blocks[m], to_head(m), "qkv_z") for m in range(2)]
    later = after(blocks, *own)
    first_keys = jnp.stack([o[:2] for o in own])
    own += [send(later[m], to_head(m), "qkv_z_later") for m in range(2, 4)]
    second_keys = jnp.stack([o[:2] for o in own[2:]])
    queries = jnp.stack([o[2] for o in own])

    def shared(keys, *earlier):
        far = send(keys, other_low, "keys_y")
        return keys, send(keys, other_core, "keys_core"), far, send(after(far, *earlier), other_core, "keys_y_core")

    partial = call(
        attend_kernel,
        [SMEM, SMEM] + [VMEM] * 5,
        [
            shape(4, 256, 128, dtype=F32),
            shape(4, 256, 128, dtype=F32),
            shape(4, 256, 192, dtype=F32),
        ],
        [pltpu.VMEM((4, 256, 512), F32)],
        1_600_000_000,
        table,
        head_scale,
        queries,
        *shared(first_keys),
    )
    base = call(base_kernel, [VMEM], shape(256, 1536), [], 1_000_000, tokens)
    other_last = send(after(last, queries), other_core, "out_core")
    late = (queries, *shared(second_keys, partial[0]), *partial)
    heads = []
    for number in range(2):
        heads.append(
            call(
                finish_kernel,
                [SMEM, SMEM, SMEM] + [VMEM] * (8 + number),
                shape(2, 192, 256),
                [pltpu.VMEM((4, 256, 512), F32)],
                800_000_000,
                jnp.full((1,), 2 * number, jnp.int32),
                table,
                head_scale,
                *heads,
                *late,
            )
        )
    back = [send(heads[n // 2][n % 2], to_tokens(n), "heads_back") for n in range(4)]
    return call(
        out_kernel,
        [SMEM] + [VMEM] * 5 + [ANY] * 2,
        shape(256, 1536),
        [
            pltpu.VMEM((2, 16, 48, 768), BF16),
            pltpu.VMEM((4, 256, 192), BF16),
            pltpu.SemaphoreType.DMA((2,)),
        ],
        600_000_000,
        table,
        *back,
        base,
        last,
        other_last,
    )


def solution(mesh):
    placed = (
        P(AXES, None),
        P(None, None, "seq"),
        P(),
        P(),
        P(None, None, "seq"),
        P(),
        P(None, "seq"),
    )
    return jax.shard_map(
        shards, mesh=mesh, in_specs=placed, out_specs=P(AXES, None), check_vma=False
    )
```

time: 800 us -> 227 us (0.28)
  waiting for transfers between devices: 703 us -> 69.9 us
  Pallas kernels: 0 us -> 60.7 us
  starting transfers between devices: 5.11 us -> 53.1 us
  matrix products: 41.3 us -> 0 us
  other arithmetic: 16.2 us -> 4.28 us
  local copies, waits for them, and re-layouts: 20.1 us -> 29 us
    all_gather x5 -> x0, waiting for transfers between devices: 701 us -> none  [the longest x1 248 us: shards(): lax.all_gather(conv_weight, 'seq', axis=2, tiled=True)]
    ppermute x2 -> x32, waiting for transfers between devices: 0.01 us -> 69.9 us  [the longest x30 69.9 us: send(): return lax.ppermute(value, AXES, pairs)]
    pallas_call x0 -> x9, Pallas kernels: none -> 60.7 us  [call(): pl.pallas_call(kernel, out_shape=outs, in_specs=ins, out_specs=jax.tree.m...]
    ppermute x2 -> x32, starting transfers between devices: 4.77 us -> 53.1 us  [the longest x30 47.3 us: send(): return lax.ppermute(value, AXES, pairs)]
    dot_general x9 -> x0, matrix products: 41.3 us -> none  [the longest x1 11.1 us: shards(): jnp.einsum('thd,nhd->htn', queries, key_rows, preferred_element_type=jnp....]
    all_gather x2 -> x0, local copies, waits for them, and re-layouts: 17.4 us -> none  [the longest x1 8.7 us: shards(): lax.all_gather(projected[1], 'seq', axis=0, tiled=True)]
    reduce_sum x3 -> x0, other arithmetic: 9.23 us -> none  [the longest x1 8.7 us: shards(): new_sum = jnp.sum(weights, axis=2)]
    slice x3 -> x18, local copies, waits for them, and re-layouts: 1.17 us -> 10.3 us  [the longest x7 5.08 us: after(): zero = sum((o[(0,) * o.ndim].astype(F32) * 0.0 for o in others), F32(0.0))]
  transfers between devices with their start and end apart: 7 -> 32, of which waited for: 5 -> 9; matrix products, arithmetic and copies ran while one was open for 9% -> 8% of each run, Pallas kernels for 0% -> 21%
where the time goes in v1:
time: 227 us; the launch traced here: 223 us
  waiting for transfers between devices  69.9 us (31%)
  Pallas kernels  60.7 us (27%)
  starting transfers between devices  53.1 us (23%)
  local copies, waits for them, and re-layouts  29 us (13%)
  between operations  5.89 us (3%)
  other arithmetic  4.28 us (2%)
    ppermute x30, waiting for transfers between devices, send(): return lax.ppermute(value, AXES, pairs)  69.9 us
    pallas_call x9, Pallas kernels, call(): pl.pallas_call(kernel, out_shape=outs, in_specs=ins, out_specs=jax.tree.m...  60.7 us
    ppermute x30, starting transfers between devices, send(): return lax.ppermute(value, AXES, pairs)  47.3 us
    dynamic_update_slice x8, local copies, waits for them, and re-layouts, stacked(): out = lax.dynamic_update_slice(out, block[None], (at,) + (0,) * block.ndim)  6.16 us
    unnamed x58, local copies, waits for them, and re-layouts  5.82 us
    slice x7, local copies, waits for them, and re-layouts, after(): zero = sum((o[(0,) * o.ndim].astype(F32) * 0.0 for o in others), F32(0.0))  5.08 us
    ppermute x1, starting transfers between devices, shards(): before = lax.ppermute(activated[-2:], AXES, forward)  4.55 us
  transfers between devices with their start and end apart: 32, of which 9 were waited for; matrix products, arithmetic and copies ran while one was open for 8% of the time, Pallas kernels for 21%

profile of v1, /device:TPU:6, one launch (start us, length us, event | category | flops | bytes accessed | tf_op | source)
XLA Modules:
  0.0 223.0 jit_solution(8753358255813629205)
XLA Ops:
  0.0 1.1 copy-done
  2.3 1.7 fusion.5
  4.1 1.3 collective-permute-start.1
  5.4 4.5 %collective-permute-start = (bf16[2,768]{1,0:T(2,128)(2,1)S(1)}, bf16[2,768]{1,0:T(2,128)(2,1)S(1)}, u32[]{:S(2)}, u32[]{:S(2)}) collective-permute-start(bf16[2,768]{1,0:T(2,128)(2,1)S(1)} %get-tuple-element.21), channel_id=1, source_target_pairs={{0,1},{1,2},{2,3},{3,4},{4,5},{5,6},{6,7},{7,8},{8,9},{9,10},{10,1... | collective-permute-start | bytes 9224 | tf_op jit(solution)/shard_map/ppermute | solution.py:363
  10.1 6.5 %collective-permute-start.3 = (bf16[9,48,768]{2,1,0:T(8,128)(2,1)S(1)}, bf16[9,48,768]{2,1,0:T(8,128)(2,1)S(1)}, u32[]{:S(2)}, u32[]{:S(2)}) collective-permute-start(bf16[9,48,768]{2,1,0:T(8,128)(2,1)S(1)} %pad_maximum_fusion), channel_id=1, source_target_pairs={{0,4},{1,5},{2,2},{3,3},{4,6},{5,7},{6,0},{7,1},{8,18},{9,19},{10,... | collective-permute-start | bytes 1990664 | tf_op jit(solution)/shard_map/weights_z/ppermute | solution.py:36
  17.1 2.3 %collective-permute-start.2 = (bf16[528,768]{1,0:T(8,128)(2,1)S(1)}, bf16[528,768]{1,0:T(8,128)(2,1)S(1)}, u32[]{:S(2)}, u32[]{:S(2)}) collective-permute-start(bf16[528,768]{1,0:T(8,128)(2,1)S(1)} %maximum_maximum_fusion.own), channel_id=1, source_target_pairs={{0,16},{1,17},{2,18},{3,19},{4,20},{5,21},{6,22},{7,23},{8,24},{9,... | collective-permute-start | bytes 2433032 | tf_op jit(solution)/shard_map/acts_core/ppermute | solution.py:36
  19.4 12.1 %collective-permute-done.3 = bf16[9,48,768]{2,1,0:T(8,128)(2,1)S(1)} collective-permute-done((bf16[9,48,768]{2,1,0:T(8,128)(2,1)S(1)}, bf16[9,48,768]{2,1,0:T(8,128)(2,1)S(1)}, u32[]{:S(2)}, u32[]{:S(2)}) %collective-permute-start.3) | collective-permute-done | bytes 663584 | tf_op jit(solution)/shard_map/weights_z/ppermute | solution.py:36
  31.5 1.6 collective-permute-start.4
  33.5 1.1 collective-permute-start.6
  35.5 5.2 %acts_kernel.1.refs_1_ = bf16[6,512,768]{2,1,0:T(8,128)(2,1)} custom-call(bf16[528,768]{1,0:T(8,128)(2,1)} %copy-done.5, bf16[528,768]{1,0:T(8,128)(2,1)} %copy-done.12), custom_call_target="tpu_custom_call" | custom-call | flops 1000000000 | bytes 8000000 | tf_op jit(solution)/shard_map/acts_kernel/pallas_call | solution.py:332
  40.7 1.2 slice.167
  42.7 1.0 fusion.8
  43.7 8.5 %collective-permute-done.5 = bf16[9,48,768]{2,1,0:T(8,128)(2,1)} collective-permute-done((bf16[9,48,768]{2,1,0:T(8,128)(2,1)S(1)}, bf16[9,48,768]{2,1,0:T(8,128)(2,1)}, u32[]{:S(2)}, u32[]{:S(2)}) %collective-permute-start.5) | collective-permute-done | bytes 663584 | tf_op jit(solution)/shard_map/weights_first/ppermute | solution.py:36
  52.2 1.0 fusion.7
  53.2 1.0 fusion.6.refs_3_
  54.3 3.6 %collective-permute-start.7 = (bf16[4,5,48,768]{3,2,1,0:T(8,128)(2,1)S(1)}, bf16[4,5,48,768]{3,2,1,0:T(8,128)(2,1)S(1)}, u32[]{:S(2)}, u32[]{:S(2)}) collective-permute-start(bf16[4,5,48,768]{3,2,1,0:T(8,128)(2,1)S(1)} %fusion.6.refs_3_), channel_id=1, source_target_pairs={{0,1},{1,32},{2,3},{3,34},{4,5},{5,36},{6,7},{7,38},{8,9},{9,40},{... | collective-permute-start | bytes 4423688 | tf_op jit(solution)/shard_map/conv_second/ppermute | solution.py:36
  57.9 1.5 collective-permute-start.8
  59.4 17.3 %collective-permute-done.7.refs_4_ = bf16[4,5,48,768]{3,2,1,0:T(8,128)(2,1)S(1)} collective-permute-done((bf16[4,5,48,768]{3,2,1,0:T(8,128)(2,1)S(1)}, bf16[4,5,48,768]{3,2,1,0:T(8,128)(2,1)S(1)}, u32[]{:S(2)}, u32[]{:S(2)}) %collective-permute-start.7) | collective-permute-done | bytes 1474592 | tf_op jit(solution)/shard_map/conv_second/ppermute | solution.py:36
  80.1 1.0 fusion.11
  81.1 1.0 fusion.10.g0
  83.0 2.4 %collective-permute-start.14 = (bf16[4,4,48,768]{3,2,1,0:T(8,128)(2,1)S(1)}, bf16[4,4,48,768]{3,2,1,0:T(8,128)(2,1)}, u32[]{:S(2)}, u32[]{:S(2)}) collective-permute-start(bf16[4,4,48,768]{3,2,1,0:T(8,128)(2,1)S(1)} %fusion.10.g0), channel_id=1, source_target_pairs={{0,33},{1,0},{2,35},{3,2},{4,37},{5,4},{6,39},{7,6},{8,41},{9,8},{... | collective-permute-start | bytes 3538952 | tf_op jit(solution)/shard_map/qkv_second/ppermute | solution.py:36
  86.2 2.1 slice.171
  89.3 3.2 %collective-permute-start.10 = (bf16[2,5,48,768]{3,2,1,0:T(8,128)(2,1)}, bf16[2,5,48,768]{3,2,1,0:T(8,128)(2,1)}, u32[]{:S(2)}, u32[]{:S(2)}) collective-permute-start(bf16[2,5,48,768]{3,2,1,0:T(8,128)(2,1)} %slice.172), channel_id=1, source_target_pairs={{0,33},{1,0},{2,35},{3,2},{4,37},{5,4},{6,39},{7,6},{8,41},{9,8},{... | collective-permute-start | bytes 2211848 | tf_op jit(solution)/shard_map/conv_far/ppermute | solution.py:36
  92.5 1.2 fusion.14.refs_0_.table
  93.7 12.8 %conv_kernel.2.refs_3_.ma = bf16[12,48,512]{2,1,0:T(8,128)(2,1)} custom-call(s32[50]{0:T(128)} %fusion.14.refs_0_.table, bf16[6,512,768]{2,1,0:T(8,128)(2,1)} %acts_kernel.1.refs_1_, f32[16,1,48]{2,1,0:T(1,128)} %reshape.37.refs_2_, bf16[4,5,48,768]{3,2,1,0:T(8,128)(2,1)} %copy-done.10, bf16[4,5,48,768]{3,2,1,0:T(8,128)(2,1)} %copy-done.15, ...), custom_call_target="tpu_custom_call" | custom-call | flops 4499999744 | bytes 8000000 | tf_op jit(solution)/shard_map/conv_kernel/pallas_call | solution.py:332
  107.7 1.1 slice.180
  108.8 3.3 %collective-permute-start.16 = (bf16[2,4,48,768]{3,2,1,0:T(8,128)(2,1)S(1)}, bf16[2,4,48,768]{3,2,1,0:T(8,128)(2,1)S(1)}, u32[]{:S(2)}, u32[]{:S(2)}) collective-permute-start(bf16[2,4,48,768]{3,2,1,0:T(8,128)(2,1)S(1)} %slice.180), channel_id=1, source_target_pairs={{0,33},{1,0},{2,35},{3,2},{4,37},{5,4},{6,39},{7,6},{8,41},{9,8},{... | collective-permute-start | bytes 1769480 | tf_op jit(solution)/shard_map/qkv_far/ppermute | solution.py:36
  112.1 6.9 %conv_kernel.3.mb = bf16[4,48,512]{2,1,0:T(8,128)(2,1)} custom-call(s32[50]{0:T(128)} %fusion.14.refs_0_.table, bf16[6,512,768]{2,1,0:T(8,128)(2,1)} %acts_kernel.1.refs_1_, f32[16,1,48]{2,1,0:T(1,128)} %reshape.37.refs_2_, bf16[12,48,512]{2,1,0:T(8,128)(2,1)} %conv_kernel.2.refs_3_.ma, bf16[2,5,48,768]{3,2,1,0:T(8,128)(2,1)} %collective-permute-done.9.refs_4_, ...), custom_call_target="tpu_custom_call" | custom-call | flops 1500000000 | bytes 8000000 | tf_op jit(solution)/shard_map/conv_kernel/pallas_call | solution.py:332
  119.1 1.5 reshape.39.gain
  122.3 8.3 %project_kernel.1 = (bf16[4,3,192,256]{3,2,1,0:T(8,128)(2,1)}, bf16[16,48,768]{2,1,0:T(8,128)(2,1)}, bf16[2,16,48,512]{3,2,1,0:T(8,128)(2,1)}) custom-call(s32[50]{0:T(128)} %fusion.14.refs_0_.table, bf16[12,48,512]{2,1,0:T(8,128)(2,1)} %conv_kernel.2.refs_3_.ma, bf16[4,48,512]{2,1,0:T(8,128)(2,1)} %conv_kernel.3.mb, ...), custom_call_target="tpu_custom_call" | custom-call | flops 1800000000 | bytes 8000000 | tf_op jit(solution)/shard_map/project_kernel/pallas_call | solution.py:332
  130.6 1.2 slice_bitcast_fusion.8
  132.2 3.8 %collective-permute-start.18 = (bf16[3,192,256]{2,1,0:T(8,128)(2,1)S(1)}, bf16[3,192,256]{2,1,0:T(8,128)(2,1)S(1)}, u32[]{:S(2)}, u32[]{:S(2)}) collective-permute-start(bf16[3,192,256]{2,1,0:T(8,128)(2,1)S(1)} %get-tuple-element.19), channel_id=1, source_target_pairs={{0,12},{1,13},{2,28},{3,29},{4,0},{5,1},{6,16},{7,17},{8,4},{9,5},... | collective-permute-start | bytes 884744 | tf_op jit(solution)/shard_map/qkv_z/ppermute | solution.py:36
  136.0 12.2 %collective-permute-done.17 = bf16[3,192,256]{2,1,0:T(8,128)(2,1)S(1)} collective-permute-done((bf16[3,192,256]{2,1,0:T(8,128)(2,1)S(1)}, bf16[3,192,256]{2,1,0:T(8,128)(2,1)S(1)}, u32[]{:S(2)}, u32[]{:S(2)}) %collective-permute-start.17) | collective-permute-done | bytes 294944 | tf_op jit(solution)/shard_map/qkv_z/ppermute | solution.py:36
  148.8 2.9 %collective-permute-done.18 = bf16[3,192,256]{2,1,0:T(8,128)(2,1)S(1)} collective-permute-done((bf16[3,192,256]{2,1,0:T(8,128)(2,1)S(1)}, bf16[3,192,256]{2,1,0:T(8,128)(2,1)S(1)}, u32[]{:S(2)}, u32[]{:S(2)}) %collective-permute-start.18) | collective-permute-done | bytes 294944 | tf_op jit(solution)/shard_map/qkv_z/ppermute | solution.py:36
  153.6 2.4 %collective-permute-start.20 = (bf16[3,192,256]{2,1,0:T(8,128)(2,1)S(1)}, bf16[3,192,256]{2,1,0:T(8,128)(2,1)S(1)}, u32[]{:S(2)}, u32[]{:S(2)}) collective-permute-start(bf16[3,192,256]{2,1,0:T(8,128)(2,1)S(1)} %get-tuple-element.18), channel_id=1, source_target_pairs={{0,8},{1,9},{2,24},{3,25},{4,12},{5,13},{6,28},{7,29},{8,0},{9,1},... | collective-permute-start | bytes 884744 | tf_op jit(solution)/shard_map/qkv_z_later/ppermute | solution.py:36
  156.8 2.3 %collective-permute-start.23 = (bf16[2,2,192,256]{3,2,1,0:T(8,128)(2,1)S(1)}, bf16[2,2,192,256]{3,2,1,0:T(8,128)(2,1)S(1)}, u32[]{:S(2)}, u32[]{:S(2)}) collective-permute-start(bf16[2,2,192,256]{3,2,1,0:T(8,128)(2,1)S(1)} %pad_maximum_fusion.3.g0), channel_id=1, source_target_pairs={{0,16},{1,17},{2,18},{3,19},{4,20},{5,21},{6,22},{7,23},{8,24},{9,... | collective-permute-start | bytes 1179656 | tf_op jit(solution)/shard_map/keys_core/ppermute | solution.py:36
  159.7 12.2 %collective-permute-done.20 = bf16[3,192,256]{2,1,0:T(8,128)(2,1)S(1)} collective-permute-done((bf16[3,192,256]{2,1,0:T(8,128)(2,1)S(1)}, bf16[3,192,256]{2,1,0:T(8,128)(2,1)S(1)}, u32[]{:S(2)}, u32[]{:S(2)}) %collective-permute-start.20) | collective-permute-done | bytes 294944 | tf_op jit(solution)/shard_map/qkv_z_later/ppermute | solution.py:36
  172.3 1.1 broadcast_add_fusion
  175.6 8.2 %attend_kernel.1 = (f32[4,256,128]{2,1,0:T(8,128)}, f32[4,256,128]{2,1,0:T(8,128)}, f32[4,256,192]{2,1,0:T(8,128)}) custom-call(s32[50]{0:T(128)} %fusion.14.refs_0_.table, f32[4]{0:T(128)} %factor.5, bf16[4,192,256]{2,1,0:T(8,128)(2,1)} %pad_maximum_fusion.1.queries.refs_0_.refs_1_, bf16[2,2,192,256]{3,2,1,0:T(8,128)(2,1)} %copy-done.14, ...), custom_call_target="tpu_custom_call" | custom-call | flops 1600000000 | bytes 8000000 | tf_op jit(solution)/shard_map/attend_kernel/pallas_call | solution.py:332
  183.8 1.2 slice.155
  186.3 1.3 collective-permute-done.26.refs_4_.refs_5_
  188.4 6.0 %finish_kernel.2.refs_0_ = bf16[2,192,256]{2,1,0:T(8,128)(2,1)} custom-call(s32[1]{0:T(128)} %constant.66.clone.1.base, s32[50]{0:T(128)} %fusion.14.refs_0_.table, f32[4]{0:T(128)} %factor.5, bf16[4,192,256]{2,1,0:T(8,128)(2,1)} %pad_maximum_fusion.1.queries.refs_0_.refs_1_, bf16[2,2,192,256]{3,2,1,0:T(8,128)(2,1)} %copy-done.3, ...), custom_call_target="tpu_custom_call" | custom-call | flops 800000000 | bytes 8000000 | tf_op jit(solution)/shard_map/finish_kernel/pallas_call | solution.py:332
  195.5 4.3 %collective-permute-start.28 = (bf16[192,256]{1,0:T(8,128)(2,1)S(1)}, bf16[192,256]{1,0:T(8,128)(2,1)S(1)}, u32[]{:S(2)}, u32[]{:S(2)}) collective-permute-start(bf16[192,256]{1,0:T(8,128)(2,1)S(1)} %get-tuple-element.27), channel_id=1, source_target_pairs={{0,12},{1,13},{2,0},{3,1},{4,28},{5,29},{6,24},{7,25},{8,4},{9,5},... | collective-permute-start | bytes 294920 | tf_op jit(solution)/shard_map/heads_back/ppermute | solution.py:36
  199.8 6.1 %finish_kernel.3 = bf16[2,192,256]{2,1,0:T(8,128)(2,1)} custom-call(s32[1]{0:T(128)} %constant.82.clone.1.base, s32[50]{0:T(128)} %fusion.14.refs_0_.table, f32[4]{0:T(128)} %factor.5, bf16[2,192,256]{2,1,0:T(8,128)(2,1)} %finish_kernel.2.refs_0_, bf16[4,192,256]{2,1,0:T(8,128)(2,1)} %pad_maximum_fusion.1.queries.refs_0_.refs_1_, ...), custom_call_target="tpu_custom_call" | custom-call | flops 800000000 | bytes 8000000 | tf_op jit(solution)/shard_map/finish_kernel/pallas_call | solution.py:332
  207.5 4.1 %collective-permute-start.30 = (bf16[192,256]{1,0:T(8,128)(2,1)S(1)}, bf16[192,256]{1,0:T(8,128)(2,1)S(1)}, u32[]{:S(2)}, u32[]{:S(2)}) collective-permute-start(bf16[192,256]{1,0:T(8,128)(2,1)S(1)} %get-tuple-element.25), channel_id=1, source_target_pairs={{0,8},{1,9},{2,4},{3,5},{4,20},{5,21},{6,16},{7,17},{8,0},{9,1},{1... | collective-permute-start | bytes 294920 | tf_op jit(solution)/shard_map/heads_back/ppermute | solution.py:36
  211.6 2.6 %base_kernel.1.base = bf16[256,1536]{1,0:T(8,128)(2,1)} custom-call(bf16[2,16,48,512]{3,2,1,0:T(8,128)(2,1)} %get-tuple-element.15.tokens), custom_call_target="tpu_custom_call" | custom-call | flops 1000000 | bytes 8000000 | tf_op jit(solution)/shard_map/base_kernel/pallas_call | solution.py:332
  214.3 3.2 %collective-permute-done.30.h3 = bf16[192,256]{1,0:T(8,128)(2,1)S(1)} collective-permute-done((bf16[192,256]{1,0:T(8,128)(2,1)S(1)}, bf16[192,256]{1,0:T(8,128)(2,1)S(1)}, u32[]{:S(2)}, u32[]{:S(2)}) %collective-permute-start.30) | collective-permute-done | bytes 98336 | tf_op jit(solution)/shard_map/heads_back/ppermute | solution.py:36
  218.1 4.7 %out_kernel.1 = bf16[256,1536]{1,0:T(8,128)(2,1)} custom-call(s32[50]{0:T(128)} %fusion.14.refs_0_.table, bf16[192,256]{1,0:T(8,128)(2,1)} %copy-done.20, bf16[192,256]{1,0:T(8,128)(2,1)} %copy-done.21, bf16[192,256]{1,0:T(8,128)(2,1)} %copy-done.22, bf16[192,256]{1,0:T(8,128)(2,1)} %copy-done.23, bf16[256,1536]{1,0:T(8,128)(2,1)} %base_kernel.1.base, ...), custom_call_target="tpu_custom_call" | custom-call | flops 600000000 | bytes 8000000 | tf_op jit(solution)/shard_map/out_kernel/pallas_call | solution.py:332
  (137 shorter events, 19.7 us)
Async XLA Ops:
  0.0 9.9 %copy-start.19 = (bf16[3,1536,48]{1,2,0:T(8,128)(2,1)S(1)}, bf16[3,1536,48]{1,2,0:T(8,128)(2,1)}, u32[]{:S(2)}) copy-start(bf16[3,1536,48]{1,2,0:T(8,128)(2,1)} %param.12) | copy-start | bytes 1327108
  1.1 8.9 %copy-start.24 = (bf16[768,96]{0,1:T(8,128)(2,1)S(1)}, bf16[768,96]{0,1:T(8,128)(2,1)}, u32[]{:S(2)}) copy-start(bf16[768,96]{0,1:T(8,128)(2,1)} %param.14) | copy-start | bytes 442372
  4.1 12.7 %collective-permute-start.1 = (bf16[2,768]{1,0:T(2,128)(2,1)S(1)}, bf16[2,768]{1,0:T(2,128)(2,1)S(1)}, u32[]{:S(2)}, u32[]{:S(2)}) collective-permute-start(bf16[2,768]{1,0:T(2,128)(2,1)S(1)} %get-tuple-element.22), channel_id=1, source_target_pairs={{1,0},{2,1},{3,2},{4,3},{5,4},{6,5},{7,6},{8,7},{9,8},{10,9},{11,1... | collective-permute-start | bytes 9224 | tf_op jit(solution)/shard_map/ppermute | solution.py:364
  5.4 11.4 %collective-permute-start = (bf16[2,768]{1,0:T(2,128)(2,1)S(1)}, bf16[2,768]{1,0:T(2,128)(2,1)S(1)}, u32[]{:S(2)}, u32[]{:S(2)}) collective-permute-start(bf16[2,768]{1,0:T(2,128)(2,1)S(1)} %get-tuple-element.21), channel_id=1, source_target_pairs={{0,1},{1,2},{2,3},{3,4},{4,5},{5,6},{6,7},{7,8},{8,9},{9,10},{10,1... | collective-permute-start | bytes 9224 | tf_op jit(solution)/shard_map/ppermute | solution.py:363
  10.1 21.3 %collective-permute-start.3 = (bf16[9,48,768]{2,1,0:T(8,128)(2,1)S(1)}, bf16[9,48,768]{2,1,0:T(8,128)(2,1)S(1)}, u32[]{:S(2)}, u32[]{:S(2)}) collective-permute-start(bf16[9,48,768]{2,1,0:T(8,128)(2,1)S(1)} %pad_maximum_fusion), channel_id=1, source_target_pairs={{0,4},{1,5},{2,2},{3,3},{4,6},{5,7},{6,0},{7,1},{8,18},{9,19},{10,... | collective-permute-start | bytes 1990664 | tf_op jit(solution)/shard_map/weights_z/ppermute | solution.py:36
  17.1 17.5 %copy-start.5 = (bf16[528,768]{1,0:T(8,128)(2,1)}, bf16[528,768]{1,0:T(8,128)(2,1)S(1)}, u32[]{:S(2)}) copy-start(bf16[528,768]{1,0:T(8,128)(2,1)S(1)} %maximum_maximum_fusion.own) | copy-start | bytes 2433028
  17.1 17.5 %collective-permute-start.2 = (bf16[528,768]{1,0:T(8,128)(2,1)S(1)}, bf16[528,768]{1,0:T(8,128)(2,1)S(1)}, u32[]{:S(2)}, u32[]{:S(2)}) collective-permute-start(bf16[528,768]{1,0:T(8,128)(2,1)S(1)} %maximum_maximum_fusion.own), channel_id=1, source_target_pairs={{0,16},{1,17},{2,18},{3,19},{4,20},{5,21},{6,22},{7,23},{8,24},{9,... | collective-permute-start | bytes 2433032 | tf_op jit(solution)/shard_map/acts_core/ppermute | solution.py:36
  31.5 11.2 %collective-permute-start.4 = (bf16[9,48,768]{2,1,0:T(8,128)(2,1)S(1)}, bf16[9,48,768]{2,1,0:T(8,128)(2,1)}, u32[]{:S(2)}, u32[]{:S(2)}) collective-permute-start(bf16[9,48,768]{2,1,0:T(8,128)(2,1)S(1)} %collective-permute-done.3), channel_id=1, source_target_pairs={{0,64},{1,65},{2,66},{3,67},{4,68},{5,69},{6,70},{7,71},{8,72},{9,... | collective-permute-start | bytes 1990664 | tf_op jit(solution)/shard_map/weights_first/ppermute | solution.py:36
  33.1 19.1 %collective-permute-start.5 = (bf16[9,48,768]{2,1,0:T(8,128)(2,1)S(1)}, bf16[9,48,768]{2,1,0:T(8,128)(2,1)}, u32[]{:S(2)}, u32[]{:S(2)}) collective-permute-start(bf16[9,48,768]{2,1,0:T(8,128)(2,1)S(1)} %collective-permute-done.3), channel_id=1, source_target_pairs={{0,192},{1,193},{2,194},{3,195},{4,196},{5,197},{6,198},{7,199},{8... | collective-permute-start | bytes 1990664 | tf_op jit(solution)/shard_map/weights_first/ppermute | solution.py:36
  33.5 19.7 %collective-permute-start.6 = (bf16[9,48,768]{2,1,0:T(8,128)(2,1)S(1)}, bf16[9,48,768]{2,1,0:T(8,128)(2,1)}, u32[]{:S(2)}, u32[]{:S(2)}) collective-permute-start(bf16[9,48,768]{2,1,0:T(8,128)(2,1)S(1)} %collective-permute-done.3), channel_id=1, source_target_pairs={{0,128},{1,129},{2,130},{3,131},{4,132},{5,133},{6,134},{7,135},{8... | collective-permute-start | bytes 1990664 | tf_op jit(solution)/shard_map/weights_first/ppermute | solution.py:36
  54.2 26.9 %copy-start.10 = (bf16[4,5,48,768]{3,2,1,0:T(8,128)(2,1)}, bf16[4,5,48,768]{3,2,1,0:T(8,128)(2,1)S(1)}, u32[]{:S(2)}) copy-start(bf16[4,5,48,768]{3,2,1,0:T(8,128)(2,1)S(1)} %fusion.6.refs_3_) | copy-start | bytes 4423684
  54.3 22.4 %collective-permute-start.7 = (bf16[4,5,48,768]{3,2,1,0:T(8,128)(2,1)S(1)}, bf16[4,5,48,768]{3,2,1,0:T(8,128)(2,1)S(1)}, u32[]{:S(2)}, u32[]{:S(2)}) collective-permute-start(bf16[4,5,48,768]{3,2,1,0:T(8,128)(2,1)S(1)} %fusion.6.refs_3_), channel_id=1, source_target_pairs={{0,1},{1,32},{2,3},{3,34},{4,5},{5,36},{6,7},{7,38},{8,9},{9,40},{... | collective-permute-start | bytes 4423688 | tf_op jit(solution)/shard_map/conv_second/ppermute | solution.py:36
  57.9 19.4 %collective-permute-start.8 = (bf16[4,5,48,768]{3,2,1,0:T(8,128)(2,1)S(1)}, bf16[4,5,48,768]{3,2,1,0:T(8,128)(2,1)S(1)}, u32[]{:S(2)}, u32[]{:S(2)}) collective-permute-start(bf16[4,5,48,768]{3,2,1,0:T(8,128)(2,1)S(1)} %fusion.6.refs_3_), channel_id=1, source_target_pairs={{0,33},{1,0},{2,35},{3,2},{4,37},{5,4},{6,39},{7,6},{8,41},{9,8},{... | collective-permute-start | bytes 4423688 | tf_op jit(solution)/shard_map/conv_second/ppermute | solution.py:36
  76.7 2.3 %copy-start.15 = (bf16[4,5,48,768]{3,2,1,0:T(8,128)(2,1)}, bf16[4,5,48,768]{3,2,1,0:T(8,128)(2,1)S(1)}, u32[]{:S(2)}) copy-start(bf16[4,5,48,768]{3,2,1,0:T(8,128)(2,1)S(1)} %collective-permute-done.7.refs_4_) | copy-start | bytes 4423684
  79.1 6.4 %copy-start.26 = (f32[1536]{0:T(1024)S(1)}, f32[1536]{0:T(1024)}, u32[]{:S(2)}) copy-start(f32[1536]{0:T(1024)} %param.10) | copy-start | bytes 18436
  82.1 7.1 %copy-start.2 = (bf16[4,4,48,768]{3,2,1,0:T(8,128)(2,1)}, bf16[4,4,48,768]{3,2,1,0:T(8,128)(2,1)S(1)}, u32[]{:S(2)}) copy-start(bf16[4,4,48,768]{3,2,1,0:T(8,128)(2,1)S(1)} %fusion.10.g0) | copy-start | bytes 3538948
  82.1 24.5 %collective-permute-start.13 = (bf16[4,4,48,768]{3,2,1,0:T(8,128)(2,1)S(1)}, bf16[4,4,48,768]{3,2,1,0:T(8,128)(2,1)S(1)}, u32[]{:S(2)}, u32[]{:S(2)}) collective-permute-start(bf16[4,4,48,768]{3,2,1,0:T(8,128)(2,1)S(1)} %fusion.10.g0), channel_id=1, source_target_pairs={{0,1},{1,32},{2,3},{3,34},{4,5},{5,36},{6,7},{7,38},{8,9},{9,40},{... | collective-permute-start | bytes 3538952 | tf_op jit(solution)/shard_map/qkv_second/ppermute | solution.py:36
  83.0 24.6 %collective-permute-start.14 = (bf16[4,4,48,768]{3,2,1,0:T(8,128)(2,1)S(1)}, bf16[4,4,48,768]{3,2,1,0:T(8,128)(2,1)}, u32[]{:S(2)}, u32[]{:S(2)}) collective-permute-start(bf16[4,4,48,768]{3,2,1,0:T(8,128)(2,1)S(1)} %fusion.10.g0), channel_id=1, source_target_pairs={{0,33},{1,0},{2,35},{3,2},{4,37},{5,4},{6,39},{7,6},{8,41},{9,8},{... | collective-permute-start | bytes 3538952 | tf_op jit(solution)/shard_map/qkv_second/ppermute | solution.py:36
  88.3 23.8 %collective-permute-start.9 = (bf16[2,5,48,768]{3,2,1,0:T(8,128)(2,1)}, bf16[2,5,48,768]{3,2,1,0:T(8,128)(2,1)}, u32[]{:S(2)}, u32[]{:S(2)}) collective-permute-start(bf16[2,5,48,768]{3,2,1,0:T(8,128)(2,1)} %slice.171), channel_id=1, source_target_pairs={{0,1},{1,32},{2,3},{3,34},{4,5},{5,36},{6,7},{7,38},{8,9},{9,40},{... | collective-permute-start | bytes 2211848 | tf_op jit(solution)/shard_map/conv_far/ppermute | solution.py:36
  89.3 22.9 %collective-permute-start.10 = (bf16[2,5,48,768]{3,2,1,0:T(8,128)(2,1)}, bf16[2,5,48,768]{3,2,1,0:T(8,128)(2,1)}, u32[]{:S(2)}, u32[]{:S(2)}) collective-permute-start(bf16[2,5,48,768]{3,2,1,0:T(8,128)(2,1)} %slice.172), channel_id=1, source_target_pairs={{0,33},{1,0},{2,35},{3,2},{4,37},{5,4},{6,39},{7,6},{8,41},{9,8},{... | collective-permute-start | bytes 2211848 | tf_op jit(solution)/shard_map/conv_far/ppermute | solution.py:36
  106.6 14.1 %collective-permute-start.11 = (bf16[12,48,512]{2,1,0:T(8,128)(2,1)}, bf16[12,48,512]{2,1,0:T(8,128)(2,1)}, u32[]{:S(2)}, u32[]{:S(2)}) collective-permute-start(bf16[12,48,512]{2,1,0:T(8,128)(2,1)} %conv_kernel.2.refs_3_.ma), channel_id=1, source_target_pairs={{0,16},{1,17},{2,18},{3,19},{4,20},{5,21},{6,22},{7,23},{8,24},{9,... | collective-permute-start | bytes 1769480 | tf_op jit(solution)/shard_map/pooled_core/ppermute | solution.py:36
  106.7 12.3 %copy-start.6 = (bf16[4,4,48,768]{3,2,1,0:T(8,128)(2,1)}, bf16[4,4,48,768]{3,2,1,0:T(8,128)(2,1)S(1)}, u32[]{:S(2)}) copy-start(bf16[4,4,48,768]{3,2,1,0:T(8,128)(2,1)S(1)} %collective-permute-done.13.g1) | copy-start | bytes 3538948
  107.7 13.1 %collective-permute-start.15 = (bf16[2,4,48,768]{3,2,1,0:T(8,128)(2,1)}, bf16[2,4,48,768]{3,2,1,0:T(8,128)(2,1)}, u32[]{:S(2)}, u32[]{:S(2)}) collective-permute-start(bf16[2,4,48,768]{3,2,1,0:T(8,128)(2,1)} %slice.179), channel_id=1, source_target_pairs={{0,1},{1,32},{2,3},{3,34},{4,5},{5,36},{6,7},{7,38},{8,9},{9,40},{... | collective-permute-start | bytes 1769480 | tf_op jit(solution)/shard_map/qkv_far/ppermute | solution.py:36
  108.8 10.4 %copy-start.25 = (f32[1536]{0:T(1024)S(1)}, f32[1536]{0:T(1024)}, u32[]{:S(2)}) copy-start(f32[1536]{0:T(1024)} %param.11) | copy-start | bytes 18436
  108.8 12.0 %collective-permute-start.16 = (bf16[2,4,48,768]{3,2,1,0:T(8,128)(2,1)S(1)}, bf16[2,4,48,768]{3,2,1,0:T(8,128)(2,1)S(1)}, u32[]{:S(2)}, u32[]{:S(2)}) collective-permute-start(bf16[2,4,48,768]{3,2,1,0:T(8,128)(2,1)S(1)} %slice.180), channel_id=1, source_target_pairs={{0,33},{1,0},{2,35},{3,2},{4,37},{5,4},{6,39},{7,6},{8,41},{9,8},{... | collective-permute-start | bytes 1769480 | tf_op jit(solution)/shard_map/qkv_far/ppermute | solution.py:36
  119.0 1.7 collective-permute-start.12
  130.6 22.8 %copy-start.7 = (bf16[4,3,192,256]{3,2,1,0:T(8,128)(2,1)S(1)}, bf16[4,3,192,256]{3,2,1,0:T(8,128)(2,1)}, u32[]{:S(2)}) copy-start(bf16[4,3,192,256]{3,2,1,0:T(8,128)(2,1)} %get-tuple-element.11) | copy-start | bytes 3538948
  131.8 16.4 %collective-permute-start.17 = (bf16[3,192,256]{2,1,0:T(8,128)(2,1)S(1)}, bf16[3,192,256]{2,1,0:T(8,128)(2,1)S(1)}, u32[]{:S(2)}, u32[]{:S(2)}) collective-permute-start(bf16[3,192,256]{2,1,0:T(8,128)(2,1)S(1)} %get-tuple-element.20), channel_id=1, source_target_pairs={{0,4},{1,5},{2,20},{3,21},{4,8},{5,9},{6,24},{7,25},{8,12},{9,13},... | collective-permute-start | bytes 884744 | tf_op jit(solution)/shard_map/qkv_z/ppermute | solution.py:36
  132.2 19.5 %collective-permute-start.18 = (bf16[3,192,256]{2,1,0:T(8,128)(2,1)S(1)}, bf16[3,192,256]{2,1,0:T(8,128)(2,1)S(1)}, u32[]{:S(2)}, u32[]{:S(2)}) collective-permute-start(bf16[3,192,256]{2,1,0:T(8,128)(2,1)S(1)} %get-tuple-element.19), channel_id=1, source_target_pairs={{0,12},{1,13},{2,28},{3,29},{4,0},{5,1},{6,16},{7,17},{8,4},{9,5},... | collective-permute-start | bytes 884744 | tf_op jit(solution)/shard_map/qkv_z/ppermute | solution.py:36
  153.6 18.4 %collective-permute-start.20 = (bf16[3,192,256]{2,1,0:T(8,128)(2,1)S(1)}, bf16[3,192,256]{2,1,0:T(8,128)(2,1)S(1)}, u32[]{:S(2)}, u32[]{:S(2)}) collective-permute-start(bf16[3,192,256]{2,1,0:T(8,128)(2,1)S(1)} %get-tuple-element.18), channel_id=1, source_target_pairs={{0,8},{1,9},{2,24},{3,25},{4,12},{5,13},{6,28},{7,29},{8,0},{9,1},... | collective-permute-start | bytes 884744 | tf_op jit(solution)/shard_map/qkv_z_later/ppermute | solution.py:36
  156.0 16.0 %collective-permute-start.19 = (bf16[3,192,256]{2,1,0:T(8,128)(2,1)S(1)}, bf16[3,192,256]{2,1,0:T(8,128)(2,1)S(1)}, u32[]{:S(2)}, u32[]{:S(2)}) collective-permute-start(bf16[3,192,256]{2,1,0:T(8,128)(2,1)S(1)} %get-tuple-element.17), channel_id=1, source_target_pairs={{0,0},{1,1},{2,16},{3,17},{4,4},{5,5},{6,20},{7,21},{8,8},{9,9},{1... | collective-permute-start | bytes 884744 | tf_op jit(solution)/shard_map/qkv_z_later/ppermute | solution.py:36
  156.7 15.6 %copy-start.1 = (bf16[16,48,768]{2,1,0:T(8,128)(2,1)S(1)}, bf16[16,48,768]{2,1,0:T(8,128)(2,1)}, u32[]{:S(2)}) copy-start(bf16[16,48,768]{2,1,0:T(8,128)(2,1)} %get-tuple-element.16.mine) | copy-start | bytes 3538948
  156.8 16.6 %copy-start.14 = (bf16[2,2,192,256]{3,2,1,0:T(8,128)(2,1)}, bf16[2,2,192,256]{3,2,1,0:T(8,128)(2,1)S(1)}, u32[]{:S(2)}) copy-start(bf16[2,2,192,256]{3,2,1,0:T(8,128)(2,1)S(1)} %pad_maximum_fusion.3.g0) | copy-start | bytes 1179652
  156.8 18.1 %collective-permute-start.23 = (bf16[2,2,192,256]{3,2,1,0:T(8,128)(2,1)S(1)}, bf16[2,2,192,256]{3,2,1,0:T(8,128)(2,1)S(1)}, u32[]{:S(2)}, u32[]{:S(2)}) collective-permute-start(bf16[2,2,192,256]{3,2,1,0:T(8,128)(2,1)S(1)} %pad_maximum_fusion.3.g0), channel_id=1, source_target_pairs={{0,16},{1,17},{2,18},{3,19},{4,20},{5,21},{6,22},{7,23},{8,24},{9,... | collective-permute-start | bytes 1179656 | tf_op jit(solution)/shard_map/keys_core/ppermute | solution.py:36
  159.0 13.1 %collective-permute-start.24 = (bf16[2,2,192,256]{3,2,1,0:T(8,128)(2,1)S(1)}, bf16[2,2,192,256]{3,2,1,0:T(8,128)(2,1)S(1)}, u32[]{:S(2)}, u32[]{:S(2)}) collective-permute-start(bf16[2,2,192,256]{3,2,1,0:T(8,128)(2,1)S(1)} %pad_maximum_fusion.3.g0), channel_id=1, source_target_pairs={{0,1},{1,0},{2,3},{3,2},{4,5},{5,4},{6,7},{7,6},{8,9},{9,8},{10,11... | collective-permute-start | bytes 1179656 | tf_op jit(solution)/shard_map/keys_y/ppermute | solution.py:36
  172.0 13.6 %collective-permute-start.22 = (bf16[2,2,192,256]{3,2,1,0:T(8,128)(2,1)S(1)}, bf16[2,2,192,256]{3,2,1,0:T(8,128)(2,1)S(1)}, u32[]{:S(2)}, u32[]{:S(2)}) collective-permute-start(bf16[2,2,192,256]{3,2,1,0:T(8,128)(2,1)S(1)} %pad_maximum_fusion.2.refs_1_.refs_2_), channel_id=1, source_target_pairs={{0,1},{1,0},{2,3},{3,2},{4,5},{5,4},{6,7},{7,6},{8,9},{9,8},{10,11... | collective-permute-start | bytes 1179656 | tf_op jit(solution)/shard_map/keys_y/ppermute | solution.py:36
  172.2 2.7 %collective-permute-start.25 = (bf16[2,2,192,256]{3,2,1,0:T(8,128)(2,1)S(1)}, bf16[2,2,192,256]{3,2,1,0:T(8,128)(2,1)}, u32[]{:S(2)}, u32[]{:S(2)}) collective-permute-start(bf16[2,2,192,256]{3,2,1,0:T(8,128)(2,1)S(1)} %collective-permute-done.24.g2), channel_id=1, source_target_pairs={{0,16},{1,17},{2,18},{3,19},{4,20},{5,21},{6,22},{7,23},{8,24},{9,... | collective-permute-start | bytes 1179656 | tf_op jit(solution)/shard_map/keys_y_core/ppermute | solution.py:36
  173.4 40.8 %collective-permute-start.31 = (bf16[16,48,768]{2,1,0:T(8,128)(2,1)}, bf16[16,48,768]{2,1,0:T(8,128)(2,1)S(1)}, u32[]{:S(2)}, u32[]{:S(2)}) collective-permute-start(bf16[16,48,768]{2,1,0:T(8,128)(2,1)} %broadcast_add_fusion), channel_id=1, source_target_pairs={{0,16},{1,17},{2,18},{3,19},{4,20},{5,21},{6,22},{7,23},{8,24},{9,... | collective-permute-start | bytes 3538952 | tf_op jit(solution)/shard_map/out_core/ppermute | solution.py:36
  173.9 12.4 %collective-permute-start.21 = (bf16[2,2,192,256]{3,2,1,0:T(8,128)(2,1)S(1)}, bf16[2,2,192,256]{3,2,1,0:T(8,128)(2,1)S(1)}, u32[]{:S(2)}, u32[]{:S(2)}) collective-permute-start(bf16[2,2,192,256]{3,2,1,0:T(8,128)(2,1)S(1)} %pad_maximum_fusion.2.refs_1_.refs_2_), channel_id=1, source_target_pairs={{0,16},{1,17},{2,18},{3,19},{4,20},{5,21},{6,22},{7,23},{8,24},{9,... | collective-permute-start | bytes 1179656 | tf_op jit(solution)/shard_map/keys_core/ppermute | solution.py:36
  185.7 1.9 collective-permute-start.26
  195.4 18.8 %collective-permute-start.27 = (bf16[192,256]{1,0:T(8,128)(2,1)S(1)}, bf16[192,256]{1,0:T(8,128)(2,1)S(1)}, u32[]{:S(2)}, u32[]{:S(2)}) collective-permute-start(bf16[192,256]{1,0:T(8,128)(2,1)S(1)} %get-tuple-element.28), channel_id=1, source_target_pairs={{0,4},{1,5},{2,8},{3,9},{4,16},{5,17},{6,20},{7,21},{8,12},{9,13},... | collective-permute-start | bytes 294920 | tf_op jit(solution)/shard_map/heads_back/ppermute | solution.py:36
  195.5 18.7 %collective-permute-start.28 = (bf16[192,256]{1,0:T(8,128)(2,1)S(1)}, bf16[192,256]{1,0:T(8,128)(2,1)S(1)}, u32[]{:S(2)}, u32[]{:S(2)}) collective-permute-start(bf16[192,256]{1,0:T(8,128)(2,1)S(1)} %get-tuple-element.27), channel_id=1, source_target_pairs={{0,12},{1,13},{2,0},{3,1},{4,28},{5,29},{6,24},{7,25},{8,4},{9,5},... | collective-permute-start | bytes 294920 | tf_op jit(solution)/shard_map/heads_back/ppermute | solution.py:36
  206.9 7.4 %collective-permute-start.29 = (bf16[192,256]{1,0:T(8,128)(2,1)S(1)}, bf16[192,256]{1,0:T(8,128)(2,1)S(1)}, u32[]{:S(2)}, u32[]{:S(2)}) collective-permute-start(bf16[192,256]{1,0:T(8,128)(2,1)S(1)} %get-tuple-element.26), channel_id=1, source_target_pairs={{0,0},{1,1},{2,12},{3,13},{4,24},{5,25},{6,28},{7,29},{8,8},{9,9},... | collective-permute-start | bytes 294920 | tf_op jit(solution)/shard_map/heads_back/ppermute | solution.py:36
  207.5 9.9 %collective-permute-start.30 = (bf16[192,256]{1,0:T(8,128)(2,1)S(1)}, bf16[192,256]{1,0:T(8,128)(2,1)S(1)}, u32[]{:S(2)}, u32[]{:S(2)}) collective-permute-start(bf16[192,256]{1,0:T(8,128)(2,1)S(1)} %get-tuple-element.25), channel_id=1, source_target_pairs={{0,8},{1,9},{2,4},{3,5},{4,20},{5,21},{6,16},{7,17},{8,0},{9,1},{1... | collective-permute-start | bytes 294920 | tf_op jit(solution)/shard_map/heads_back/ppermute | solution.py:36
  214.2 3.3 %copy-start.11 = (bf16[16,48,768]{2,1,0:T(8,128)(2,1)}, bf16[16,48,768]{2,1,0:T(8,128)(2,1)S(1)}, u32[]{:S(2)}) copy-start(bf16[16,48,768]{2,1,0:T(8,128)(2,1)S(1)} %collective-permute-done.31.theirs) | copy-start | bytes 3538948
  214.2 3.2 %copy-start.20 = (bf16[192,256]{1,0:T(8,128)(2,1)}, bf16[192,256]{1,0:T(8,128)(2,1)S(1)}, u32[]{:S(2)}) copy-start(bf16[192,256]{1,0:T(8,128)(2,1)S(1)} %collective-permute-done.27.h0) | copy-start | bytes 294916
  214.2 3.2 %copy-start.21 = (bf16[192,256]{1,0:T(8,128)(2,1)}, bf16[192,256]{1,0:T(8,128)(2,1)S(1)}, u32[]{:S(2)}) copy-start(bf16[192,256]{1,0:T(8,128)(2,1)S(1)} %collective-permute-done.28.h1) | copy-start | bytes 294916
  214.3 3.2 %copy-start.22 = (bf16[192,256]{1,0:T(8,128)(2,1)}, bf16[192,256]{1,0:T(8,128)(2,1)S(1)}, u32[]{:S(2)}) copy-start(bf16[192,256]{1,0:T(8,128)(2,1)S(1)} %collective-permute-done.29.h2) | copy-start | bytes 294916
  (13 other events, 16.8 us)

commit v2 on v1

--- a/solution.py
+++ b/solution.py
@@ -76,8 +76,8 @@
 
 def stacked(blocks):
     out = jnp.zeros((len(blocks), *blocks[0].shape), blocks[0].dtype)
-    for at, block in enumerate(blocks):
-        out = lax.dynamic_update_slice(out, block[None], (at,) + (0,) * block.ndim)
+    for at in reversed(range(len(blocks))):
+        out = lax.dynamic_update_slice(out, blocks[at][None], (at,) + (0,) * blocks[at].ndim)
     return out
 
 
@@ -148,50 +148,53 @@
 
 def acts_kernel(own, other, out):
     for which, window in enumerate((own, other)):
-        for odd in range(2):
-            row = lax.broadcasted_iota(jnp.int32, (272, 528), 0)
-            col = lax.broadcasted_iota(jnp.int32, (272, 528), 1)
-            pick = jnp.where(col == 2 * row + odd, 1.0, 0.0).astype(BF16)
-            rows = jnp.dot(pick, window[...], preferred_element_type=F32)
-            for step in range(3):
-                out[2 * step + odd, pl.ds(256 * which, 256), :] = rows[step : step + 256].astype(BF16)
+        columns = window[...].T
+
+        def one(number, _):
+            row = lax.broadcasted_iota(jnp.int32, (528, 256), 0)
+            col = lax.broadcasted_iota(jnp.int32, (528, 256), 1)
+            pick = jnp.where(row == 2 * col + number, 1.0, 0.0).astype(BF16)
+            picked = jnp.dot(columns, pick, preferred_element_type=F32)
+            out[number, :, 256 * which : 256 * which + 256] = picked.astype(BF16)
+            return 0
+
+        lax.fori_loop(0, 6, one, 0)
 
 
 def conv_kernel(base, table, acts, bias, *refs):
     *groups, out, weights, sems = refs
     groups = groups[-3:] if base == 0 else groups[-2:]
-    copies = [[] for _ in range(5)]
-    for tap in range(5):
-        at = 0
-        for group in groups:
-            for slot in range(group.shape[0]):
+    copies = []
+    at = 0
+    for group in groups:
+        for slot in range(group.shape[0]):
+            for tap in range(5):
                 copy = pltpu.make_async_copy(
-                    group.at[slot, tap], weights.at[tap, at], sems.at[tap, at]
+                    group.at[slot, tap],
+                    weights.at[at, :, pl.ds(768 * tap, 768)],
+                    sems.at[at, tap],
                 )
                 copy.start()
-                copies[tap].append(copy)
-                at += 1
-    for tap in range(5):
-        for copy in copies[tap]:
-            copy.wait()
+                copies.append(copy)
+            at += 1
+    count = at
+    shift = jnp.concatenate([bias[table[ROWS + base + i]] for i in range(count)], axis=0)
+    for copy in copies:
+        copy.wait()
 
     def block(number, _):
-        even = odd = None
-        for tap in range(5):
-            w = weights[tap, pl.ds(4 * number, 4)].reshape(192, 768)
-            e, o = nt(acts[tap], w), nt(acts[tap + 1], w)
-            even = e if even is None else even + e
-            odd = o if odd is None else odd + o
-        at = base + 4 * number
-        shift = jnp.concatenate([bias[table[ROWS + at + i]] for i in range(4)], axis=1)
-        pooled = (jnp.maximum(even, odd) + shift).T.astype(BF16)
-        out[pl.ds(4 * number, 4)] = pooled.reshape(4, 48, 512)
+        cols = pl.ds(pl.multiple_of(256 * number, 256), 256)
+        w = weights[...].reshape(48 * count, 3840)
+        even = jnp.dot(w, acts[0:5, :, cols].reshape(3840, 256), preferred_element_type=F32)
+        odd = jnp.dot(w, acts[1:6, :, cols].reshape(3840, 256), preferred_element_type=F32)
+        pooled = (jnp.maximum(even, odd) + shift).astype(BF16)
+        out[:, :, cols] = pooled.reshape(count, 48, 256)
         return 0
 
-    lax.fori_loop(0, weights.shape[1] // 4, block, 0)
-
-
-def project_kernel(table, ma, mb, ta, tb, gain, g0, g1, g2, g3, g4, out, last, tokens, weights, normed, sems):
+    lax.fori_loop(0, 2, block, 0)
+
+
+def project_kernel(table, ma, mb, ta, tb, gain, g0, g1, g2, g3, g4, out, query, last, tokens, weights, normed, sems):
     at = 0
     copies = []
     for group in (g0, g1, g2, g3, g4):
@@ -236,28 +239,30 @@
             w = weights[:, half, pl.ds(4 * head, 4)].reshape(576, 768)
             term = jnp.dot(w, normed[part, half], preferred_element_type=F32)
             total = term if total is None else total + term
-        out[m] = total.astype(BF16).reshape(3, 192, 256)
+        out[m] = total[:384].astype(BF16).reshape(2, 192, 256)
+        query[m] = total[384:].astype(BF16)
         return 0
 
     lax.fori_loop(0, 4, one, 0)
 
 
-def scores_of(query, groups, scores, scale):
+def scores_of(query, groups, scores):
     top = None
     for at, group in enumerate(groups):
         keys = jnp.concatenate([group[i, 0] for i in range(group.shape[0])], axis=1)
-        s = jnp.dot(query, keys, preferred_element_type=F32) * scale
+        s = jnp.dot(query, keys, preferred_element_type=F32)
         scores[at, :, : s.shape[1]] = s
         t = jnp.max(s, axis=1, keepdims=True)
         top = t if top is None else jnp.maximum(top, t)
     return top
 
 
-def sums_of(top, groups, scores):
+def sums_of(top, groups, scores, scale):
+    top = top * scale
     total = acc = None
     for at, group in enumerate(groups):
         values = jnp.concatenate([group[i, 1] for i in range(group.shape[0])], axis=1)
-        p = jnp.exp(scores[at, :, : values.shape[1]] - top)
+        p = jnp.exp2(scores[at, :, : values.shape[1]] * scale - top)
         t = jnp.sum(p, axis=1, keepdims=True)
         o = nt(p.astype(BF16), values)
         total = t if total is None else total + t
@@ -265,13 +270,13 @@
     return total, acc
 
 
-def attend_kernel(table, factor, queries, g0, g1, g2, g3, tops, totals, accs, scores):
-    scale = factor[table[HEAD]] * (1 / math.sqrt(HEAD_DIM))
+def attend_kernel(table, factor, queries, g0, g1, tops, totals, accs, scores):
+    scale = factor[table[HEAD]] * (math.log2(math.e) / math.sqrt(HEAD_DIM))
 
     def one(part, _):
-        groups = (g0, g1, g2, g3)
-        top = scores_of(queries[part].T, groups, scores, scale)
-        total, acc = sums_of(top, groups, scores)
+        groups = (g0, g1)
+        top = scores_of(queries[part].T, groups, scores)
+        total, acc = sums_of(top, groups, scores, scale)
         tops[part] = jnp.broadcast_to(top, (256, 128))
         totals[part] = jnp.broadcast_to(total, (256, 128))
         accs[part] = acc
@@ -280,23 +285,22 @@
     lax.fori_loop(0, 4, one, 0)
 
 
-def finish_kernel(base, table, factor, *refs):
-    queries, g0, g1, g2, g3, tops, totals, accs, out, scores = refs[-10:]
-    scale = factor[table[HEAD]] * (1 / math.sqrt(HEAD_DIM))
+def finish_kernel(table, factor, queries, g0, g1, tops, totals, accs, out, scores):
+    scale = factor[table[HEAD]] * (math.log2(math.e) / math.sqrt(HEAD_DIM))
 
     def one(step, _):
-        part = table[STEPS + base[0] + step]
-        groups = (g0, g1, g2, g3)
+        part = table[STEPS + step]
+        groups = (g0, g1)
         before = tops[part, :, :1]
-        top = jnp.maximum(before, scores_of(queries[part].T, groups, scores, scale))
-        total, acc = sums_of(top, groups, scores)
-        keep = jnp.exp(before - top)
+        top = jnp.maximum(before, scores_of(queries[part].T, groups, scores))
+        total, acc = sums_of(top, groups, scores, scale)
+        keep = jnp.exp2((before - top) * scale)
         total = total + totals[part, :, :1] * keep
         acc = acc + accs[part] * keep
         out[step] = (acc / total).astype(BF16).T
         return 0
 
-    lax.fori_loop(0, 2, one, 0)
+    lax.fori_loop(0, 4, one, 0)
 
 
 def base_kernel(tokens, out):
@@ -304,22 +308,15 @@
         out[:, 768 * half : 768 * half + 768] = tokens[half, :, :, :256].reshape(768, 256).T
 
 
-def out_kernel(table, h0, h1, h2, h3, base, mine, theirs, out, weights, attended, sems):
+def out_kernel(table, h0, h1, h2, h3, base, mine, theirs, out, attended):
     core = table[CORE]
-    copies = []
-    for side, (group, which) in enumerate(((mine, core), (theirs, 1 - core))):
-        copy = pltpu.make_async_copy(group, weights.at[which], sems.at[side])
-        copy.start()
-        copies.append(copy)
     for number, head in enumerate((h0, h1, h2, h3)):
-        attended[table[FROM + number]] = head[...].T
-    rows = jnp.concatenate([attended[h] for h in range(4)], axis=1)
-    for copy in copies:
-        copy.wait()
-    for half in range(2):
-        lanes = slice(768 * half, 768 * half + 768)
-        w = weights[half].reshape(768, 768)
-        out[:, lanes] = (base[:, lanes].astype(F32) + nt(rows, w)).astype(BF16)
+        attended[table[FROM + number]] = head[...]
+    rows = attended[...].reshape(768, 256).T
+    for which, weights in ((core, mine), (1 - core, theirs)):
+        lanes = pl.ds(pl.multiple_of(768 * which, 768), 768)
+        mixed = nt(rows, weights[...].reshape(768, 768))
+        out[:, lanes] = (base[:, lanes].astype(F32) + mixed).astype(BF16)
 
 
 SMEM = pl.BlockSpec(memory_space=pltpu.SMEM)
@@ -366,7 +363,7 @@
     acts = call(
         acts_kernel,
         [VMEM] * 2,
-        shape(6, 512, 768),
+        shape(6, 768, 512),
         [],
         1_000_000_000,
         padded,
@@ -388,7 +385,7 @@
         send(qkv_near[0][:2], second(1), "qkv_far"),
         send(qkv_near[1][2:], second(-1), "qkv_far"),
     )
-    bias = lax.dynamic_slice_in_dim(conv_bias, 768 * core, 768).reshape(16, 1, 48)
+    bias = lax.dynamic_slice_in_dim(conv_bias, 768 * core, 768).reshape(16, 48, 1)
 
     def conv(base, groups, *earlier):
         count = sum(g.shape[0] for g in groups)
@@ -396,7 +393,7 @@
             lambda *refs: conv_kernel(base, *refs),
             [SMEM, VMEM, VMEM] + [ANY] * (len(groups) + len(earlier)),
             shape(count, 48, 512),
-            [pltpu.VMEM((5, count, 48, 768), BF16), pltpu.SemaphoreType.DMA((5, count))],
+            [pltpu.VMEM((count, 48, 3840), BF16), pltpu.SemaphoreType.DMA((count, 5))],
             375_000_000 * count,
             table,
             acts,
@@ -408,10 +405,15 @@
     mine = [conv(0, (stack, low, high_stack))]
     mine.append(conv(12, far, mine[0]))
     theirs = [send(m, other_core, "pooled_core") for m in mine]
-    blocks, last, tokens = call(
+    blocks, query, last, tokens = call(
         project_kernel,
         [SMEM] + [VMEM] * 5 + [ANY] * 5,
-        [shape(4, 3, 192, 256), shape(16, 48, 768), shape(2, 16, 48, 512)],
+        [
+            shape(4, 2, 192, 256),
+            shape(4, 192, 256),
+            shape(16, 48, 768),
+            shape(2, 16, 48, 512),
+        ],
         [
             pltpu.VMEM((3, 2, 8, 48, 768), BF16),
             pltpu.VMEM((2, 2, 768, 256), BF16),
@@ -425,61 +427,50 @@
         *qkv_groups,
     )
 
-    own = [send(blocks[m], to_head(m), "qkv_z") for m in range(2)]
-    later = after(blocks, *own)
-    first_keys = jnp.stack([o[:2] for o in own])
-    own += [send(later[m], to_head(m), "qkv_z_later") for m in range(2, 4)]
-    second_keys = jnp.stack([o[:2] for o in own[2:]])
-    queries = jnp.stack([o[2] for o in own])
-
-    def shared(keys, *earlier):
-        far = send(keys, other_low, "keys_y")
-        return keys, send(keys, other_core, "keys_core"), far, send(after(far, *earlier), other_core, "keys_y_core")
+    keys = jnp.stack([send(blocks[m], to_head(m), "keys_z") for m in range(4)])
+    far = send(keys, other_low, "keys_y")
+    near = send(keys, other_core, "keys_core")
+    query = after(query, keys)
+    queries = jnp.stack([send(query[m], to_head(m), "queries_z") for m in range(4)])
 
     partial = call(
         attend_kernel,
-        [SMEM, SMEM] + [VMEM] * 5,
+        [SMEM, SMEM] + [VMEM] * 3,
         [
             shape(4, 256, 128, dtype=F32),
             shape(4, 256, 128, dtype=F32),
             shape(4, 256, 192, dtype=F32),
         ],
-        [pltpu.VMEM((4, 256, 512), F32)],
+        [pltpu.VMEM((2, 256, 1024), F32)],
         1_600_000_000,
         table,
         head_scale,
         queries,
-        *shared(first_keys),
+        keys,
+        near,
     )
     base = call(base_kernel, [VMEM], shape(256, 1536), [], 1_000_000, tokens)
     other_last = send(after(last, queries), other_core, "out_core")
-    late = (queries, *shared(second_keys, partial[0]), *partial)
-    heads = []
-    for number in range(2):
-        heads.append(
-            call(
-                finish_kernel,
-                [SMEM, SMEM, SMEM] + [VMEM] * (8 + number),
-                shape(2, 192, 256),
-                [pltpu.VMEM((4, 256, 512), F32)],
-                800_000_000,
-                jnp.full((1,), 2 * number, jnp.int32),
-                table,
-                head_scale,
-                *heads,
-                *late,
-            )
-        )
-    back = [send(heads[n // 2][n % 2], to_tokens(n), "heads_back") for n in range(4)]
+    far_near = send(after(far, partial[0]), other_core, "keys_y_core")
+    heads = call(
+        finish_kernel,
+        [SMEM, SMEM] + [VMEM] * 6,
+        shape(4, 192, 256),
+        [pltpu.VMEM((2, 256, 1024), F32)],
+        1_600_000_000,
+        table,
+        head_scale,
+        queries,
+        far,
+        far_near,
+        *partial,
+    )
+    back = [send(heads[n], to_tokens(n), "heads_back") for n in range(4)]
     return call(
         out_kernel,
-        [SMEM] + [VMEM] * 5 + [ANY] * 2,
+        [SMEM] + [VMEM] * 7,
         shape(256, 1536),
-        [
-            pltpu.VMEM((2, 16, 48, 768), BF16),
-            pltpu.VMEM((4, 256, 192), BF16),
-            pltpu.SemaphoreType.DMA((2,)),
-        ],
+        [pltpu.VMEM((4, 192, 256), BF16)],
         600_000_000,
         table,
         *back,

time: 227 us -> 213 us (0.938); the launches traced: 223 us -> 212 us
  waiting for transfers between devices: 69.9 us -> 63.1 us
    ppermute x30 -> x31, waiting for transfers between devices: 69.9 us -> 59 us  [send(): return lax.ppermute(value, AXES, pairs)]
    ppermute x1, waiting for transfers between devices: 0.01 us -> 4.1 us  [shards(): behind = lax.ppermute(activated[:2], AXES, backward)]
    dynamic_update_slice x8 -> x6, local copies, waits for them, and re-layouts: 6.16 us -> 2.22 us  [stacked(): lax.dynamic_update_slice(out, blocks[at][None], (at,) + (0,) * blocks[at]...]
    unnamed x58 -> x50, local copies, waits for them, and re-layouts: 5.82 us -> 4.27 us
    ppermute x30 -> x31, starting transfers between devices: 47.3 us -> 48.7 us  [send(): return lax.ppermute(value, AXES, pairs)]
    pallas_call x9 -> x8, Pallas kernels: 60.7 us -> 60.9 us  [call(): pl.pallas_call(kernel, out_shape=outs, in_specs=ins, out_specs=jax.tree.m...]
  transfers between devices with their start and end apart: 32 -> 33, of which waited for: 9 -> 16; matrix products, arithmetic and copies ran while one was open for 8% -> 9% of each run, Pallas kernels for 21% -> 23%
where the time goes in v2:
time: 213 us; the launch traced here: 212 us
  waiting for transfers between devices  63.1 us (30%)
  Pallas kernels  60.9 us (29%)
  starting transfers between devices  53.4 us (25%)
  local copies, waits for them, and re-layouts  27.2 us (13%)
  between operations  5.13 us (2%)
  other arithmetic  2.18 us (1%)
    pallas_call x8, Pallas kernels, call(): pl.pallas_call(kernel, out_shape=outs, in_specs=ins, out_specs=jax.tree.m...  60.9 us
    ppermute x31, waiting for transfers between devices, send(): return lax.ppermute(value, AXES, pairs)  59 us
    ppermute x31, starting transfers between devices, send(): return lax.ppermute(value, AXES, pairs)  48.7 us
    slice x7, local copies, waits for them, and re-layouts, after(): zero = sum((o[(0,) * o.ndim].astype(F32) * 0.0 for o in others), F32(0.0))  5.23 us
    unnamed x50, local copies, waits for them, and re-layouts  4.27 us
  transfers between devices with their start and end apart: 33, of which 16 were waited for; matrix products, arithmetic and copies ran while one was open for 9% of the time, Pallas kernels for 23%

profile of v2, /device:TPU:6, one launch (start us, length us, event | category | flops | bytes accessed | tf_op | source)
XLA Modules:
  0.0 211.9 jit_solution(13781930688584784784)
XLA Ops:
  0.0 1.1 dynamic-slice_bitcast_fusion.1
  2.2 6.5 %collective-permute-start.3 = (bf16[9,48,768]{2,1,0:T(8,128)(2,1)S(1)}, bf16[9,48,768]{2,1,0:T(8,128)(2,1)S(1)}, u32[]{:S(2)}, u32[]{:S(2)}) collective-permute-start(bf16[9,48,768]{2,1,0:T(8,128)(2,1)S(1)} %pad_maximum_fusion.1), channel_id=1, source_target_pairs={{0,4},{1,5},{2,2},{3,3},{4,6},{5,7},{6,0},{7,1},{8,18},{9,19},{10,... | collective-permute-start | bytes 1990664 | tf_op jit(solution)/shard_map/weights_z/ppermute | solution.py:36
  10.5 3.5 %collective-permute-start = (bf16[2,768]{1,0:T(2,128)(2,1)S(1)}, bf16[2,768]{1,0:T(2,128)(2,1)S(1)}, u32[]{:S(2)}, u32[]{:S(2)}) collective-permute-start(bf16[2,768]{1,0:T(2,128)(2,1)S(1)} %get-tuple-element.23), channel_id=1, source_target_pairs={{0,1},{1,2},{2,3},{3,4},{4,5},{5,6},{6,7},{7,8},{8,9},{9,10},{10,1... | collective-permute-start | bytes 9224 | tf_op jit(solution)/shard_map/ppermute | solution.py:360
  14.0 1.3 collective-permute-start.1
  15.4 4.1 %collective-permute-done.1 = bf16[2,768]{1,0:T(2,128)(2,1)S(1)} collective-permute-done((bf16[2,768]{1,0:T(2,128)(2,1)S(1)}, bf16[2,768]{1,0:T(2,128)(2,1)S(1)}, u32[]{:S(2)}, u32[]{:S(2)}) %collective-permute-start.1) | collective-permute-done | bytes 3104 | tf_op jit(solution)/shard_map/ppermute | solution.py:361
  20.7 2.9 %collective-permute-done.3 = bf16[9,48,768]{2,1,0:T(8,128)(2,1)S(1)} collective-permute-done((bf16[9,48,768]{2,1,0:T(8,128)(2,1)S(1)}, bf16[9,48,768]{2,1,0:T(8,128)(2,1)S(1)}, u32[]{:S(2)}, u32[]{:S(2)}) %collective-permute-start.3) | collective-permute-done | bytes 663584 | tf_op jit(solution)/shard_map/weights_z/ppermute | solution.py:36
  23.6 2.9 %collective-permute-start.5 = (bf16[9,48,768]{2,1,0:T(8,128)(2,1)S(1)}, bf16[9,48,768]{2,1,0:T(8,128)(2,1)S(1)}, u32[]{:S(2)}, u32[]{:S(2)}) collective-permute-start(bf16[9,48,768]{2,1,0:T(8,128)(2,1)S(1)} %collective-permute-done.3), channel_id=1, source_target_pairs={{0,192},{1,193},{2,194},{3,195},{4,196},{5,197},{6,198},{7,199},{8... | collective-permute-start | bytes 1990664 | tf_op jit(solution)/shard_map/weights_first/ppermute | solution.py:36
  27.8 10.1 %acts_kernel.1.refs_1_ = bf16[6,768,512]{2,1,0:T(8,128)(2,1)} custom-call(bf16[528,768]{1,0:T(8,128)(2,1)} %copy-done.3, bf16[528,768]{1,0:T(8,128)(2,1)} %copy-done.7), custom_call_target="tpu_custom_call" | custom-call | flops 1000000000 | bytes 8000000 | tf_op jit(solution)/shard_map/acts_kernel/pallas_call | solution.py:329
  37.9 1.2 slice.149
  39.8 1.0 slice_bitcast_fusion.2
  40.9 1.7 collective-permute-done.5
  42.6 1.0 fusion.8
  43.7 5.0 %collective-permute-start.8 = (bf16[4,5,48,768]{3,2,1,0:T(8,128)(2,1)S(1)}, bf16[4,5,48,768]{3,2,1,0:T(8,128)(2,1)S(1)}, u32[]{:S(2)}, u32[]{:S(2)}) collective-permute-start(bf16[4,5,48,768]{3,2,1,0:T(8,128)(2,1)S(1)} %fusion.7.refs_3_), channel_id=1, source_target_pairs={{0,33},{1,0},{2,35},{3,2},{4,37},{5,4},{6,39},{7,6},{8,41},{9,8},{... | collective-permute-start | bytes 4423688 | tf_op jit(solution)/shard_map/conv_second/ppermute | solution.py:36
  50.8 14.8 %collective-permute-done.8.refs_5_ = bf16[4,5,48,768]{3,2,1,0:T(8,128)(2,1)S(1)} collective-permute-done((bf16[4,5,48,768]{3,2,1,0:T(8,128)(2,1)S(1)}, bf16[4,5,48,768]{3,2,1,0:T(8,128)(2,1)S(1)}, u32[]{:S(2)}, u32[]{:S(2)}) %collective-permute-start.8) | collective-permute-done | bytes 1474592 | tf_op jit(solution)/shard_map/conv_second/ppermute | solution.py:36
  66.2 3.1 %collective-permute-done.7.refs_4_ = bf16[4,5,48,768]{3,2,1,0:T(8,128)(2,1)S(1)} collective-permute-done((bf16[4,5,48,768]{3,2,1,0:T(8,128)(2,1)S(1)}, bf16[4,5,48,768]{3,2,1,0:T(8,128)(2,1)S(1)}, u32[]{:S(2)}, u32[]{:S(2)}) %collective-permute-start.7) | collective-permute-done | bytes 1474592 | tf_op jit(solution)/shard_map/conv_second/ppermute | solution.py:36
  71.9 1.4 collective-permute-start.13
  73.4 1.0 reshape.35.refs_2_
  74.4 2.1 %slice.151 = bf16[2,5,48,768]{3,2,1,0:T(8,128)(2,1)} slice(bf16[4,5,48,768]{3,2,1,0:T(8,128)(2,1)} %copy-done.13), slice={[2:4], [0:5], [0:48], [0:768]} | slice | bytes 1474560 | tf_op jit(solution)/shard_map/slice | solution.py:378
  76.6 1.8 collective-permute-start.10
  79.5 1.3 fusion.14.refs_0_.table
  80.8 11.0 %conv_kernel.2.refs_3_.ma = bf16[12,48,512]{2,1,0:T(8,128)(2,1)} custom-call(s32[50]{0:T(128)} %fusion.14.refs_0_.table, bf16[6,768,512]{2,1,0:T(8,128)(2,1)} %acts_kernel.1.refs_1_, f32[16,48,1]{2,1,0:T(8,128)} %reshape.35.refs_2_, bf16[4,5,48,768]{3,2,1,0:T(8,128)(2,1)} %copy-done.5, bf16[4,5,48,768]{3,2,1,0:T(8,128)(2,1)} %copy-done.14, ...), custom_call_target="tpu_custom_call" | custom-call | flops 4499999744 | bytes 8000000 | tf_op jit(solution)/shard_map/conv_kernel/pallas_call | solution.py:329
  92.9 3.0 %collective-permute-start.16 = (bf16[2,4,48,768]{3,2,1,0:T(8,128)(2,1)}, bf16[2,4,48,768]{3,2,1,0:T(8,128)(2,1)}, u32[]{:S(2)}, u32[]{:S(2)}) collective-permute-start(bf16[2,4,48,768]{3,2,1,0:T(8,128)(2,1)} %slice.159), channel_id=1, source_target_pairs={{0,33},{1,0},{2,35},{3,2},{4,37},{5,4},{6,39},{7,6},{8,41},{9,8},{... | collective-permute-start | bytes 1769480 | tf_op jit(solution)/shard_map/qkv_far/ppermute | solution.py:36
  95.9 1.1 slice.158
  97.3 6.6 %conv_kernel.3.mb = bf16[4,48,512]{2,1,0:T(8,128)(2,1)} custom-call(s32[50]{0:T(128)} %fusion.14.refs_0_.table, bf16[6,768,512]{2,1,0:T(8,128)(2,1)} %acts_kernel.1.refs_1_, f32[16,48,1]{2,1,0:T(8,128)} %reshape.35.refs_2_, bf16[12,48,512]{2,1,0:T(8,128)(2,1)} %conv_kernel.2.refs_3_.ma, bf16[2,5,48,768]{3,2,1,0:T(8,128)(2,1)} %collective-permute-done.9.refs_4_, ...), custom_call_target="tpu_custom_call" | custom-call | flops 1500000000 | bytes 8000000 | tf_op jit(solution)/shard_map/conv_kernel/pallas_call | solution.py:329
  104.0 1.5 reshape.36.gain
  105.6 2.6 %collective-permute-done.15.g3 = bf16[2,4,48,768]{3,2,1,0:T(8,128)(2,1)S(1)} collective-permute-done((bf16[2,4,48,768]{3,2,1,0:T(8,128)(2,1)S(1)}, bf16[2,4,48,768]{3,2,1,0:T(8,128)(2,1)S(1)}, u32[]{:S(2)}, u32[]{:S(2)}) %collective-permute-start.15) | collective-permute-done | bytes 589856 | tf_op jit(solution)/shard_map/qkv_far/ppermute | solution.py:36
  109.0 8.7 %project_kernel.1 = (bf16[4,2,192,256]{3,2,1,0:T(8,128)(2,1)}, bf16[4,192,256]{2,1,0:T(8,128)(2,1)}, bf16[16,48,768]{2,1,0:T(8,128)(2,1)}, bf16[2,16,48,512]{3,2,1,0:T(8,128)(2,1)}) custom-call(s32[50]{0:T(128)} %fusion.14.refs_0_.table, bf16[12,48,512]{2,1,0:T(8,128)(2,1)} %conv_kernel.2.refs_3_.ma, bf16[4,48,512]{2,1,0:T(8,128)(2,1)} %conv_kernel.3.mb, ...), custom_call_target="tpu_custom_call" | custom-call | flops 1800000000 | bytes 8000000 | tf_op jit(solution)/shard_map/project_kernel/pallas_call | solution.py:329
  117.8 1.3 slice_bitcast_fusion.8
  119.1 2.5 %collective-permute-start.17 = (bf16[2,192,256]{2,1,0:T(8,128)(2,1)S(1)}, bf16[2,192,256]{2,1,0:T(8,128)(2,1)S(1)}, u32[]{:S(2)}, u32[]{:S(2)}) collective-permute-start(bf16[2,192,256]{2,1,0:T(8,128)(2,1)S(1)} %get-tuple-element.22), channel_id=1, source_target_pairs={{0,4},{1,5},{2,20},{3,21},{4,8},{5,9},{6,24},{7,25},{8,12},{9,13},... | collective-permute-start | bytes 589832 | tf_op jit(solution)/shard_map/keys_z/ppermute | solution.py:36
  121.7 2.4 %collective-permute-start.22 = (bf16[2,192,256]{2,1,0:T(8,128)(2,1)S(1)}, bf16[2,192,256]{2,1,0:T(8,128)(2,1)S(1)}, u32[]{:S(2)}, u32[]{:S(2)}) collective-permute-start(bf16[2,192,256]{2,1,0:T(8,128)(2,1)S(1)} %get-tuple-element.19), channel_id=1, source_target_pairs={{0,12},{1,13},{2,28},{3,29},{4,0},{5,1},{6,16},{7,17},{8,4},{9,5},... | collective-permute-start | bytes 589832 | tf_op jit(solution)/shard_map/keys_z/ppermute | solution.py:36
  124.0 4.5 %collective-permute-start.24 = (bf16[2,192,256]{2,1,0:T(8,128)(2,1)S(1)}, bf16[2,192,256]{2,1,0:T(8,128)(2,1)S(1)}, u32[]{:S(2)}, u32[]{:S(2)}) collective-permute-start(bf16[2,192,256]{2,1,0:T(8,128)(2,1)S(1)} %get-tuple-element.20), channel_id=1, source_target_pairs={{0,8},{1,9},{2,24},{3,25},{4,12},{5,13},{6,28},{7,29},{8,0},{9,1},... | collective-permute-start | bytes 589832 | tf_op jit(solution)/shard_map/keys_z/ppermute | solution.py:36
  129.3 4.2 %collective-permute-done.17 = bf16[2,192,256]{2,1,0:T(8,128)(2,1)S(1)} collective-permute-done((bf16[2,192,256]{2,1,0:T(8,128)(2,1)S(1)}, bf16[2,192,256]{2,1,0:T(8,128)(2,1)S(1)}, u32[]{:S(2)}, u32[]{:S(2)}) %collective-permute-start.17) | collective-permute-done | bytes 196640 | tf_op jit(solution)/shard_map/keys_z/ppermute | solution.py:36
  134.1 3.6 %collective-permute-done.22 = bf16[2,192,256]{2,1,0:T(8,128)(2,1)S(1)} collective-permute-done((bf16[2,192,256]{2,1,0:T(8,128)(2,1)S(1)}, bf16[2,192,256]{2,1,0:T(8,128)(2,1)S(1)}, u32[]{:S(2)}, u32[]{:S(2)}) %collective-permute-start.22) | collective-permute-done | bytes 196640 | tf_op jit(solution)/shard_map/keys_z/ppermute | solution.py:36
  137.6 6.8 %collective-permute-done.24 = bf16[2,192,256]{2,1,0:T(8,128)(2,1)S(1)} collective-permute-done((bf16[2,192,256]{2,1,0:T(8,128)(2,1)S(1)}, bf16[2,192,256]{2,1,0:T(8,128)(2,1)S(1)}, u32[]{:S(2)}, u32[]{:S(2)}) %collective-permute-start.24) | collective-permute-done | bytes 196640 | tf_op jit(solution)/shard_map/keys_z/ppermute | solution.py:36
  145.5 2.5 %collective-permute-start.21 = (bf16[192,256]{1,0:T(8,128)(2,1)S(1)}, bf16[192,256]{1,0:T(8,128)(2,1)S(1)}, u32[]{:S(2)}, u32[]{:S(2)}) collective-permute-start(bf16[192,256]{1,0:T(8,128)(2,1)S(1)} %get-tuple-element.30), channel_id=1, source_target_pairs={{0,8},{1,9},{2,24},{3,25},{4,12},{5,13},{6,28},{7,29},{8,0},{9,1},... | collective-permute-start | bytes 294920 | tf_op jit(solution)/shard_map/queries_z/ppermute | solution.py:36
  148.7 6.7 %collective-permute-done.18 = bf16[192,256]{1,0:T(8,128)(2,1)S(1)} collective-permute-done((bf16[192,256]{1,0:T(8,128)(2,1)S(1)}, bf16[192,256]{1,0:T(8,128)(2,1)S(1)}, u32[]{:S(2)}, u32[]{:S(2)}) %collective-permute-start.18) | collective-permute-done | bytes 98336 | tf_op jit(solution)/shard_map/queries_z/ppermute | solution.py:36
  156.7 4.7 %collective-permute-done.19 = bf16[192,256]{1,0:T(8,128)(2,1)S(1)} collective-permute-done((bf16[192,256]{1,0:T(8,128)(2,1)S(1)}, bf16[192,256]{1,0:T(8,128)(2,1)S(1)}, u32[]{:S(2)}, u32[]{:S(2)}) %collective-permute-start.19) | collective-permute-done | bytes 98336 | tf_op jit(solution)/shard_map/queries_z/ppermute | solution.py:36
  163.1 8.7 %attend_kernel.1 = (f32[4,256,128]{2,1,0:T(8,128)}, f32[4,256,128]{2,1,0:T(8,128)}, f32[4,256,192]{2,1,0:T(8,128)}) custom-call(s32[50]{0:T(128)} %fusion.14.refs_0_.table, f32[4]{0:T(128)} %factor.3, bf16[4,192,256]{2,1,0:T(8,128)(2,1)} %pad_maximum_fusion.2.queries, bf16[4,2,192,256]{3,2,1,0:T(8,128)(2,1)} %copy-done.10, bf16[4,2,192,256]{3,2,1,0:T(8,128)(2,1)} %copy-done.23), custom_call_target="tpu_custom_call" | custom-call | flops 1600000000 | bytes 8000000 | tf_op jit(solution)/shard_map/attend_kernel/pallas_call | solution.py:329
  171.8 1.3 slice.134
  173.8 2.6 %collective-permute-start.27 = (bf16[4,2,192,256]{3,2,1,0:T(8,128)(2,1)S(1)}, bf16[4,2,192,256]{3,2,1,0:T(8,128)(2,1)S(1)}, u32[]{:S(2)}, u32[]{:S(2)}) collective-permute-start(bf16[4,2,192,256]{3,2,1,0:T(8,128)(2,1)S(1)} %broadcast_add_fusion.1), channel_id=1, source_target_pairs={{0,16},{1,17},{2,18},{3,19},{4,20},{5,21},{6,22},{7,23},{8,24},{9,... | collective-permute-start | bytes 2359304 | tf_op jit(solution)/shard_map/keys_y_core/ppermute | solution.py:36
  177.1 1.2 collective-permute-done.27.g1
  179.2 9.4 %finish_kernel.1 = bf16[4,192,256]{2,1,0:T(8,128)(2,1)} custom-call(s32[50]{0:T(128)} %fusion.14.refs_0_.table, f32[4]{0:T(128)} %factor.3, bf16[4,192,256]{2,1,0:T(8,128)(2,1)} %pad_maximum_fusion.2.queries, bf16[4,2,192,256]{3,2,1,0:T(8,128)(2,1)} %copy-done.9, bf16[4,2,192,256]{3,2,1,0:T(8,128)(2,1)} %copy-done.24, ...), custom_call_target="tpu_custom_call" | custom-call | flops 1600000000 | bytes 8000000 | tf_op jit(solution)/shard_map/finish_kernel/pallas_call | solution.py:329
  188.6 1.1 slice_bitcast_fusion.10
  190.9 7.5 %collective-permute-start.29 = (bf16[192,256]{1,0:T(8,128)(2,1)S(1)}, bf16[192,256]{1,0:T(8,128)(2,1)S(1)}, u32[]{:S(2)}, u32[]{:S(2)}) collective-permute-start(bf16[192,256]{1,0:T(8,128)(2,1)S(1)} %get-tuple-element.27), channel_id=1, source_target_pairs={{0,12},{1,13},{2,0},{3,1},{4,28},{5,29},{6,24},{7,25},{8,4},{9,5},... | collective-permute-start | bytes 294920 | tf_op jit(solution)/shard_map/heads_back/ppermute | solution.py:36
  198.5 2.5 %base_kernel.1.base = bf16[256,1536]{1,0:T(8,128)(2,1)} custom-call(bf16[2,16,48,512]{3,2,1,0:T(8,128)(2,1)} %get-tuple-element.17.tokens), custom_call_target="tpu_custom_call" | custom-call | flops 1000000 | bytes 8000000 | tf_op jit(solution)/shard_map/base_kernel/pallas_call | solution.py:329
  201.1 1.5 collective-permute-done.29.h1
  202.6 4.9 %collective-permute-done.28.h0 = bf16[192,256]{1,0:T(8,128)(2,1)S(1)} collective-permute-done((bf16[192,256]{1,0:T(8,128)(2,1)S(1)}, bf16[192,256]{1,0:T(8,128)(2,1)S(1)}, u32[]{:S(2)}, u32[]{:S(2)}) %collective-permute-start.28) | collective-permute-done | bytes 98336 | tf_op jit(solution)/shard_map/heads_back/ppermute | solution.py:36
  208.2 3.8 %out_kernel.1 = bf16[256,1536]{1,0:T(8,128)(2,1)} custom-call(s32[50]{0:T(128)} %fusion.14.refs_0_.table, bf16[192,256]{1,0:T(8,128)(2,1)} %copy-done.20, bf16[192,256]{1,0:T(8,128)(2,1)} %copy-done.19, bf16[192,256]{1,0:T(8,128)(2,1)} %copy-done.18, bf16[192,256]{1,0:T(8,128)(2,1)} %copy-done.17, bf16[256,1536]{1,0:T(8,128)(2,1)} %base_kernel.1.base, ...), custom_call_target="tpu_custom_call" | custom-call | flops 600000000 | bytes 8000000 | tf_op jit(solution)/shard_map/out_kernel/pallas_call | solution.py:329
  (120 shorter events, 20.7 us)
Async XLA Ops:
  0.0 9.9 %copy-start.8 = (bf16[512,768]{1,0:T(8,128)(2,1)S(1)}, bf16[512,768]{1,0:T(8,128)(2,1)}, u32[]{:S(2)}) copy-start(bf16[512,768]{1,0:T(8,128)(2,1)} %param.8) | copy-start | bytes 2359300
  2.2 21.4 %collective-permute-start.3 = (bf16[9,48,768]{2,1,0:T(8,128)(2,1)S(1)}, bf16[9,48,768]{2,1,0:T(8,128)(2,1)S(1)}, u32[]{:S(2)}, u32[]{:S(2)}) collective-permute-start(bf16[9,48,768]{2,1,0:T(8,128)(2,1)S(1)} %pad_maximum_fusion.1), channel_id=1, source_target_pairs={{0,4},{1,5},{2,2},{3,3},{4,6},{5,7},{6,0},{7,1},{8,18},{9,19},{10,... | collective-permute-start | bytes 1990664 | tf_op jit(solution)/shard_map/weights_z/ppermute | solution.py:36
  10.5 4.9 %collective-permute-start = (bf16[2,768]{1,0:T(2,128)(2,1)S(1)}, bf16[2,768]{1,0:T(2,128)(2,1)S(1)}, u32[]{:S(2)}, u32[]{:S(2)}) collective-permute-start(bf16[2,768]{1,0:T(2,128)(2,1)S(1)} %get-tuple-element.23), channel_id=1, source_target_pairs={{0,1},{1,2},{2,3},{3,4},{4,5},{5,6},{6,7},{7,8},{8,9},{9,10},{10,1... | collective-permute-start | bytes 9224 | tf_op jit(solution)/shard_map/ppermute | solution.py:360
  14.0 5.5 %collective-permute-start.1 = (bf16[2,768]{1,0:T(2,128)(2,1)S(1)}, bf16[2,768]{1,0:T(2,128)(2,1)S(1)}, u32[]{:S(2)}, u32[]{:S(2)}) collective-permute-start(bf16[2,768]{1,0:T(2,128)(2,1)S(1)} %get-tuple-element.24), channel_id=1, source_target_pairs={{1,0},{2,1},{3,2},{4,3},{5,4},{6,5},{7,6},{8,7},{9,8},{10,9},{11,1... | collective-permute-start | bytes 9224 | tf_op jit(solution)/shard_map/ppermute | solution.py:361
  19.8 7.1 %copy-start.3 = (bf16[528,768]{1,0:T(8,128)(2,1)}, bf16[528,768]{1,0:T(8,128)(2,1)S(1)}, u32[]{:S(2)}) copy-start(bf16[528,768]{1,0:T(8,128)(2,1)S(1)} %maximum_maximum_fusion.own) | copy-start | bytes 2433028
  19.8 7.1 %collective-permute-start.2 = (bf16[528,768]{1,0:T(8,128)(2,1)S(1)}, bf16[528,768]{1,0:T(8,128)(2,1)S(1)}, u32[]{:S(2)}, u32[]{:S(2)}) collective-permute-start(bf16[528,768]{1,0:T(8,128)(2,1)S(1)} %maximum_maximum_fusion.own), channel_id=1, source_target_pairs={{0,16},{1,17},{2,18},{3,19},{4,20},{5,21},{6,22},{7,23},{8,24},{9,... | collective-permute-start | bytes 2433032 | tf_op jit(solution)/shard_map/acts_core/ppermute | solution.py:36
  23.6 16.2 %collective-permute-start.4 = (bf16[9,48,768]{2,1,0:T(8,128)(2,1)S(1)}, bf16[9,48,768]{2,1,0:T(8,128)(2,1)}, u32[]{:S(2)}, u32[]{:S(2)}) collective-permute-start(bf16[9,48,768]{2,1,0:T(8,128)(2,1)S(1)} %collective-permute-done.3), channel_id=1, source_target_pairs={{0,128},{1,129},{2,130},{3,131},{4,132},{5,133},{6,134},{7,135},{8... | collective-permute-start | bytes 1990664 | tf_op jit(solution)/shard_map/weights_first/ppermute | solution.py:36
  23.6 19.0 %collective-permute-start.5 = (bf16[9,48,768]{2,1,0:T(8,128)(2,1)S(1)}, bf16[9,48,768]{2,1,0:T(8,128)(2,1)S(1)}, u32[]{:S(2)}, u32[]{:S(2)}) collective-permute-start(bf16[9,48,768]{2,1,0:T(8,128)(2,1)S(1)} %collective-permute-done.3), channel_id=1, source_target_pairs={{0,192},{1,193},{2,194},{3,195},{4,196},{5,197},{6,198},{7,199},{8... | collective-permute-start | bytes 1990664 | tf_op jit(solution)/shard_map/weights_first/ppermute | solution.py:36
  26.5 16.1 %collective-permute-start.6 = (bf16[9,48,768]{2,1,0:T(8,128)(2,1)S(1)}, bf16[9,48,768]{2,1,0:T(8,128)(2,1)}, u32[]{:S(2)}, u32[]{:S(2)}) collective-permute-start(bf16[9,48,768]{2,1,0:T(8,128)(2,1)S(1)} %collective-permute-done.3), channel_id=1, source_target_pairs={{0,64},{1,65},{2,66},{3,67},{4,68},{5,69},{6,70},{7,71},{8,72},{9,... | collective-permute-start | bytes 1990664 | tf_op jit(solution)/shard_map/weights_first/ppermute | solution.py:36
  43.7 7.1 %copy-start.5 = (bf16[4,5,48,768]{3,2,1,0:T(8,128)(2,1)}, bf16[4,5,48,768]{3,2,1,0:T(8,128)(2,1)S(1)}, u32[]{:S(2)}) copy-start(bf16[4,5,48,768]{3,2,1,0:T(8,128)(2,1)S(1)} %fusion.7.refs_3_) | copy-start | bytes 4423684
  43.7 21.9 %collective-permute-start.8 = (bf16[4,5,48,768]{3,2,1,0:T(8,128)(2,1)S(1)}, bf16[4,5,48,768]{3,2,1,0:T(8,128)(2,1)S(1)}, u32[]{:S(2)}, u32[]{:S(2)}) collective-permute-start(bf16[4,5,48,768]{3,2,1,0:T(8,128)(2,1)S(1)} %fusion.7.refs_3_), channel_id=1, source_target_pairs={{0,33},{1,0},{2,35},{3,2},{4,37},{5,4},{6,39},{7,6},{8,41},{9,8},{... | collective-permute-start | bytes 4423688 | tf_op jit(solution)/shard_map/conv_second/ppermute | solution.py:36
  48.7 20.6 %collective-permute-start.7 = (bf16[4,5,48,768]{3,2,1,0:T(8,128)(2,1)S(1)}, bf16[4,5,48,768]{3,2,1,0:T(8,128)(2,1)S(1)}, u32[]{:S(2)}, u32[]{:S(2)}) collective-permute-start(bf16[4,5,48,768]{3,2,1,0:T(8,128)(2,1)S(1)} %fusion.7.refs_3_), channel_id=1, source_target_pairs={{0,1},{1,32},{2,3},{3,34},{4,5},{5,36},{6,7},{7,38},{8,9},{9,40},{... | collective-permute-start | bytes 4423688 | tf_op jit(solution)/shard_map/conv_second/ppermute | solution.py:36
  49.7 23.6 %copy-start.22 = (f32[1536]{0:T(1024)S(1)}, f32[1536]{0:T(1024)}, u32[]{:S(2)}) copy-start(f32[1536]{0:T(1024)} %param.10) | copy-start | bytes 18436
  65.6 5.6 %copy-start.13 = (bf16[4,5,48,768]{3,2,1,0:T(8,128)(2,1)}, bf16[4,5,48,768]{3,2,1,0:T(8,128)(2,1)S(1)}, u32[]{:S(2)}) copy-start(bf16[4,5,48,768]{3,2,1,0:T(8,128)(2,1)S(1)} %collective-permute-done.8.refs_5_) | copy-start | bytes 4423684
  71.2 8.1 %copy-start.2 = (bf16[4,4,48,768]{3,2,1,0:T(8,128)(2,1)}, bf16[4,4,48,768]{3,2,1,0:T(8,128)(2,1)S(1)}, u32[]{:S(2)}) copy-start(bf16[4,4,48,768]{3,2,1,0:T(8,128)(2,1)S(1)} %fusion.11.g0) | copy-start | bytes 3538948
  71.2 20.7 %collective-permute-start.14 = (bf16[4,4,48,768]{3,2,1,0:T(8,128)(2,1)S(1)}, bf16[4,4,48,768]{3,2,1,0:T(8,128)(2,1)S(1)}, u32[]{:S(2)}, u32[]{:S(2)}) collective-permute-start(bf16[4,4,48,768]{3,2,1,0:T(8,128)(2,1)S(1)} %fusion.11.g0), channel_id=1, source_target_pairs={{0,33},{1,0},{2,35},{3,2},{4,37},{5,4},{6,39},{7,6},{8,41},{9,8},{... | collective-permute-start | bytes 3538952 | tf_op jit(solution)/shard_map/qkv_second/ppermute | solution.py:36
  71.9 24.0 %collective-permute-start.13 = (bf16[4,4,48,768]{3,2,1,0:T(8,128)(2,1)S(1)}, bf16[4,4,48,768]{3,2,1,0:T(8,128)(2,1)}, u32[]{:S(2)}, u32[]{:S(2)}) collective-permute-start(bf16[4,4,48,768]{3,2,1,0:T(8,128)(2,1)S(1)} %fusion.11.g0), channel_id=1, source_target_pairs={{0,1},{1,32},{2,3},{3,34},{4,5},{5,36},{6,7},{7,38},{8,9},{9,40},{... | collective-permute-start | bytes 3538952 | tf_op jit(solution)/shard_map/qkv_second/ppermute | solution.py:36
  76.6 20.6 %collective-permute-start.10 = (bf16[2,5,48,768]{3,2,1,0:T(8,128)(2,1)}, bf16[2,5,48,768]{3,2,1,0:T(8,128)(2,1)}, u32[]{:S(2)}, u32[]{:S(2)}) collective-permute-start(bf16[2,5,48,768]{3,2,1,0:T(8,128)(2,1)} %slice.151), channel_id=1, source_target_pairs={{0,33},{1,0},{2,35},{3,2},{4,37},{5,4},{6,39},{7,6},{8,41},{9,8},{... | collective-permute-start | bytes 2211848 | tf_op jit(solution)/shard_map/conv_far/ppermute | solution.py:36
  79.3 18.0 %collective-permute-start.9 = (bf16[2,5,48,768]{3,2,1,0:T(8,128)(2,1)}, bf16[2,5,48,768]{3,2,1,0:T(8,128)(2,1)}, u32[]{:S(2)}, u32[]{:S(2)}) collective-permute-start(bf16[2,5,48,768]{3,2,1,0:T(8,128)(2,1)} %slice.150), channel_id=1, source_target_pairs={{0,1},{1,32},{2,3},{3,34},{4,5},{5,36},{6,7},{7,38},{8,9},{9,40},{... | collective-permute-start | bytes 2211848 | tf_op jit(solution)/shard_map/conv_far/ppermute | solution.py:36
  91.8 13.7 %collective-permute-start.11 = (bf16[12,48,512]{2,1,0:T(8,128)(2,1)}, bf16[12,48,512]{2,1,0:T(8,128)(2,1)}, u32[]{:S(2)}, u32[]{:S(2)}) collective-permute-start(bf16[12,48,512]{2,1,0:T(8,128)(2,1)} %conv_kernel.2.refs_3_.ma), channel_id=1, source_target_pairs={{0,16},{1,17},{2,18},{3,19},{4,20},{5,21},{6,22},{7,23},{8,24},{9,... | collective-permute-start | bytes 1769480 | tf_op jit(solution)/shard_map/pooled_core/ppermute | solution.py:36
  91.9 12.0 %copy-start.4 = (bf16[4,4,48,768]{3,2,1,0:T(8,128)(2,1)}, bf16[4,4,48,768]{3,2,1,0:T(8,128)(2,1)S(1)}, u32[]{:S(2)}) copy-start(bf16[4,4,48,768]{3,2,1,0:T(8,128)(2,1)S(1)} %collective-permute-done.14.g2) | copy-start | bytes 3538948
  92.9 12.8 %collective-permute-start.16 = (bf16[2,4,48,768]{3,2,1,0:T(8,128)(2,1)}, bf16[2,4,48,768]{3,2,1,0:T(8,128)(2,1)}, u32[]{:S(2)}, u32[]{:S(2)}) collective-permute-start(bf16[2,4,48,768]{3,2,1,0:T(8,128)(2,1)} %slice.159), channel_id=1, source_target_pairs={{0,33},{1,0},{2,35},{3,2},{4,37},{5,4},{6,39},{7,6},{8,41},{9,8},{... | collective-permute-start | bytes 1769480 | tf_op jit(solution)/shard_map/qkv_far/ppermute | solution.py:36
  97.0 7.0 %copy-start.21 = (f32[1536]{0:T(1024)S(1)}, f32[1536]{0:T(1024)}, u32[]{:S(2)}) copy-start(f32[1536]{0:T(1024)} %param.11) | copy-start | bytes 18436
  97.0 11.2 %collective-permute-start.15 = (bf16[2,4,48,768]{3,2,1,0:T(8,128)(2,1)S(1)}, bf16[2,4,48,768]{3,2,1,0:T(8,128)(2,1)S(1)}, u32[]{:S(2)}, u32[]{:S(2)}) collective-permute-start(bf16[2,4,48,768]{3,2,1,0:T(8,128)(2,1)S(1)} %slice.158), channel_id=1, source_target_pairs={{0,1},{1,32},{2,3},{3,34},{4,5},{5,36},{6,7},{7,38},{8,9},{9,40},{... | collective-permute-start | bytes 1769480 | tf_op jit(solution)/shard_map/qkv_far/ppermute | solution.py:36
  103.9 1.7 collective-permute-start.12
  117.8 27.6 %copy-start.12 = (bf16[4,192,256]{2,1,0:T(8,128)(2,1)S(1)}, bf16[4,192,256]{2,1,0:T(8,128)(2,1)}, u32[]{:S(2)}) copy-start(bf16[4,192,256]{2,1,0:T(8,128)(2,1)} %get-tuple-element.12) | copy-start | bytes 1179652
  119.1 14.4 %collective-permute-start.17 = (bf16[2,192,256]{2,1,0:T(8,128)(2,1)S(1)}, bf16[2,192,256]{2,1,0:T(8,128)(2,1)S(1)}, u32[]{:S(2)}, u32[]{:S(2)}) collective-permute-start(bf16[2,192,256]{2,1,0:T(8,128)(2,1)S(1)} %get-tuple-element.22), channel_id=1, source_target_pairs={{0,4},{1,5},{2,20},{3,21},{4,8},{5,9},{6,24},{7,25},{8,12},{9,13},... | collective-permute-start | bytes 589832 | tf_op jit(solution)/shard_map/keys_z/ppermute | solution.py:36
  121.7 16.0 %collective-permute-start.22 = (bf16[2,192,256]{2,1,0:T(8,128)(2,1)S(1)}, bf16[2,192,256]{2,1,0:T(8,128)(2,1)S(1)}, u32[]{:S(2)}, u32[]{:S(2)}) collective-permute-start(bf16[2,192,256]{2,1,0:T(8,128)(2,1)S(1)} %get-tuple-element.19), channel_id=1, source_target_pairs={{0,12},{1,13},{2,28},{3,29},{4,0},{5,1},{6,16},{7,17},{8,4},{9,5},... | collective-permute-start | bytes 589832 | tf_op jit(solution)/shard_map/keys_z/ppermute | solution.py:36
  124.0 20.3 %collective-permute-start.24 = (bf16[2,192,256]{2,1,0:T(8,128)(2,1)S(1)}, bf16[2,192,256]{2,1,0:T(8,128)(2,1)S(1)}, u32[]{:S(2)}, u32[]{:S(2)}) collective-permute-start(bf16[2,192,256]{2,1,0:T(8,128)(2,1)S(1)} %get-tuple-element.20), channel_id=1, source_target_pairs={{0,8},{1,9},{2,24},{3,25},{4,12},{5,13},{6,28},{7,29},{8,0},{9,1},... | collective-permute-start | bytes 589832 | tf_op jit(solution)/shard_map/keys_z/ppermute | solution.py:36
  128.6 15.8 %collective-permute-start.23 = (bf16[2,192,256]{2,1,0:T(8,128)(2,1)S(1)}, bf16[2,192,256]{2,1,0:T(8,128)(2,1)S(1)}, u32[]{:S(2)}, u32[]{:S(2)}) collective-permute-start(bf16[2,192,256]{2,1,0:T(8,128)(2,1)S(1)} %get-tuple-element.21), channel_id=1, source_target_pairs={{0,0},{1,1},{2,16},{3,17},{4,4},{5,5},{6,20},{7,21},{8,8},{9,9},{1... | collective-permute-start | bytes 589832 | tf_op jit(solution)/shard_map/keys_z/ppermute | solution.py:36
  144.5 17.7 %copy-start.10 = (bf16[4,2,192,256]{3,2,1,0:T(8,128)(2,1)}, bf16[4,2,192,256]{3,2,1,0:T(8,128)(2,1)S(1)}, u32[]{:S(2)}) copy-start(bf16[4,2,192,256]{3,2,1,0:T(8,128)(2,1)S(1)} %pad_maximum_fusion.g0) | copy-start | bytes 2359300
  144.5 17.7 %collective-permute-start.26 = (bf16[4,2,192,256]{3,2,1,0:T(8,128)(2,1)S(1)}, bf16[4,2,192,256]{3,2,1,0:T(8,128)(2,1)S(1)}, u32[]{:S(2)}, u32[]{:S(2)}) collective-permute-start(bf16[4,2,192,256]{3,2,1,0:T(8,128)(2,1)S(1)} %pad_maximum_fusion.g0), channel_id=1, source_target_pairs={{0,16},{1,17},{2,18},{3,19},{4,20},{5,21},{6,22},{7,23},{8,24},{9,... | collective-permute-start | bytes 2359304 | tf_op jit(solution)/shard_map/keys_core/ppermute | solution.py:36
  144.6 29.1 %collective-permute-start.25 = (bf16[4,2,192,256]{3,2,1,0:T(8,128)(2,1)S(1)}, bf16[4,2,192,256]{3,2,1,0:T(8,128)(2,1)S(1)}, u32[]{:S(2)}, u32[]{:S(2)}) collective-permute-start(bf16[4,2,192,256]{3,2,1,0:T(8,128)(2,1)S(1)} %pad_maximum_fusion.g0), channel_id=1, source_target_pairs={{0,1},{1,0},{2,3},{3,2},{4,5},{5,4},{6,7},{7,6},{8,9},{9,8},{10,11... | collective-permute-start | bytes 2359304 | tf_op jit(solution)/shard_map/keys_y/ppermute | solution.py:36
  145.4 10.0 %collective-permute-start.18 = (bf16[192,256]{1,0:T(8,128)(2,1)S(1)}, bf16[192,256]{1,0:T(8,128)(2,1)S(1)}, u32[]{:S(2)}, u32[]{:S(2)}) collective-permute-start(bf16[192,256]{1,0:T(8,128)(2,1)S(1)} %get-tuple-element.29), channel_id=1, source_target_pairs={{0,4},{1,5},{2,20},{3,21},{4,8},{5,9},{6,24},{7,25},{8,12},{9,13},... | collective-permute-start | bytes 294920 | tf_op jit(solution)/shard_map/queries_z/ppermute | solution.py:36
  145.5 11.1 %collective-permute-start.21 = (bf16[192,256]{1,0:T(8,128)(2,1)S(1)}, bf16[192,256]{1,0:T(8,128)(2,1)S(1)}, u32[]{:S(2)}, u32[]{:S(2)}) collective-permute-start(bf16[192,256]{1,0:T(8,128)(2,1)S(1)} %get-tuple-element.30), channel_id=1, source_target_pairs={{0,8},{1,9},{2,24},{3,25},{4,12},{5,13},{6,28},{7,29},{8,0},{9,1},... | collective-permute-start | bytes 294920 | tf_op jit(solution)/shard_map/queries_z/ppermute | solution.py:36
  148.1 8.6 %collective-permute-start.20 = (bf16[192,256]{1,0:T(8,128)(2,1)S(1)}, bf16[192,256]{1,0:T(8,128)(2,1)S(1)}, u32[]{:S(2)}, u32[]{:S(2)}) collective-permute-start(bf16[192,256]{1,0:T(8,128)(2,1)S(1)} %get-tuple-element.31), channel_id=1, source_target_pairs={{0,0},{1,1},{2,16},{3,17},{4,4},{5,5},{6,20},{7,21},{8,8},{9,9},{1... | collective-permute-start | bytes 294920 | tf_op jit(solution)/shard_map/queries_z/ppermute | solution.py:36
  155.5 5.9 %collective-permute-start.19 = (bf16[192,256]{1,0:T(8,128)(2,1)S(1)}, bf16[192,256]{1,0:T(8,128)(2,1)S(1)}, u32[]{:S(2)}, u32[]{:S(2)}) collective-permute-start(bf16[192,256]{1,0:T(8,128)(2,1)S(1)} %get-tuple-element.32), channel_id=1, source_target_pairs={{0,12},{1,13},{2,28},{3,29},{4,0},{5,1},{6,16},{7,17},{8,4},{9,5},... | collective-permute-start | bytes 294920 | tf_op jit(solution)/shard_map/queries_z/ppermute | solution.py:36
  171.8 4.6 %copy-start.1 = (bf16[16,48,768]{2,1,0:T(8,128)(2,1)S(1)}, bf16[16,48,768]{2,1,0:T(8,128)(2,1)}, u32[]{:S(2)}) copy-start(bf16[16,48,768]{2,1,0:T(8,128)(2,1)} %get-tuple-element.18.mine) | copy-start | bytes 3538948
  173.8 4.5 %collective-permute-start.27 = (bf16[4,2,192,256]{3,2,1,0:T(8,128)(2,1)S(1)}, bf16[4,2,192,256]{3,2,1,0:T(8,128)(2,1)S(1)}, u32[]{:S(2)}, u32[]{:S(2)}) collective-permute-start(bf16[4,2,192,256]{3,2,1,0:T(8,128)(2,1)S(1)} %broadcast_add_fusion.1), channel_id=1, source_target_pairs={{0,16},{1,17},{2,18},{3,19},{4,20},{5,21},{6,22},{7,23},{8,24},{9,... | collective-permute-start | bytes 2359304 | tf_op jit(solution)/shard_map/keys_y_core/ppermute | solution.py:36
  176.4 24.6 %collective-permute-start.32 = (bf16[16,48,768]{2,1,0:T(8,128)(2,1)S(1)}, bf16[16,48,768]{2,1,0:T(8,128)(2,1)S(1)}, u32[]{:S(2)}, u32[]{:S(2)}) collective-permute-start(bf16[16,48,768]{2,1,0:T(8,128)(2,1)S(1)} %broadcast_add_fusion), channel_id=1, source_target_pairs={{0,16},{1,17},{2,18},{3,19},{4,20},{5,21},{6,22},{7,23},{8,24},{9,... | collective-permute-start | bytes 3538952 | tf_op jit(solution)/shard_map/out_core/ppermute | solution.py:36
  189.7 11.4 %collective-permute-start.31 = (bf16[192,256]{1,0:T(8,128)(2,1)S(1)}, bf16[192,256]{1,0:T(8,128)(2,1)S(1)}, u32[]{:S(2)}, u32[]{:S(2)}) collective-permute-start(bf16[192,256]{1,0:T(8,128)(2,1)S(1)} %get-tuple-element.25), channel_id=1, source_target_pairs={{0,8},{1,9},{2,4},{3,5},{4,20},{5,21},{6,16},{7,17},{8,0},{9,1},{1... | collective-permute-start | bytes 294920 | tf_op jit(solution)/shard_map/heads_back/ppermute | solution.py:36
  190.2 10.8 %collective-permute-start.30 = (bf16[192,256]{1,0:T(8,128)(2,1)S(1)}, bf16[192,256]{1,0:T(8,128)(2,1)S(1)}, u32[]{:S(2)}, u32[]{:S(2)}) collective-permute-start(bf16[192,256]{1,0:T(8,128)(2,1)S(1)} %get-tuple-element.26), channel_id=1, source_target_pairs={{0,0},{1,1},{2,12},{3,13},{4,24},{5,25},{6,28},{7,29},{8,8},{9,9},... | collective-permute-start | bytes 294920 | tf_op jit(solution)/shard_map/heads_back/ppermute | solution.py:36
  190.9 11.7 %collective-permute-start.29 = (bf16[192,256]{1,0:T(8,128)(2,1)S(1)}, bf16[192,256]{1,0:T(8,128)(2,1)S(1)}, u32[]{:S(2)}, u32[]{:S(2)}) collective-permute-start(bf16[192,256]{1,0:T(8,128)(2,1)S(1)} %get-tuple-element.27), channel_id=1, source_target_pairs={{0,12},{1,13},{2,0},{3,1},{4,28},{5,29},{6,24},{7,25},{8,4},{9,5},... | collective-permute-start | bytes 294920 | tf_op jit(solution)/shard_map/heads_back/ppermute | solution.py:36
  198.4 9.1 %collective-permute-start.28 = (bf16[192,256]{1,0:T(8,128)(2,1)S(1)}, bf16[192,256]{1,0:T(8,128)(2,1)S(1)}, u32[]{:S(2)}, u32[]{:S(2)}) collective-permute-start(bf16[192,256]{1,0:T(8,128)(2,1)S(1)} %get-tuple-element.28), channel_id=1, source_target_pairs={{0,4},{1,5},{2,8},{3,9},{4,16},{5,17},{6,20},{7,21},{8,12},{9,13},... | collective-permute-start | bytes 294920 | tf_op jit(solution)/shard_map/heads_back/ppermute | solution.py:36
  201.0 6.4 %copy-start.6 = (bf16[16,48,768]{2,1,0:T(8,128)(2,1)}, bf16[16,48,768]{2,1,0:T(8,128)(2,1)S(1)}, u32[]{:S(2)}) copy-start(bf16[16,48,768]{2,1,0:T(8,128)(2,1)S(1)} %collective-permute-done.32.theirs) | copy-start | bytes 3538948
  201.1 6.4 %copy-start.17 = (bf16[192,256]{1,0:T(8,128)(2,1)}, bf16[192,256]{1,0:T(8,128)(2,1)S(1)}, u32[]{:S(2)}) copy-start(bf16[192,256]{1,0:T(8,128)(2,1)S(1)} %collective-permute-done.31.h3) | copy-start | bytes 294916
  201.1 6.4 %copy-start.18 = (bf16[192,256]{1,0:T(8,128)(2,1)}, bf16[192,256]{1,0:T(8,128)(2,1)S(1)}, u32[]{:S(2)}) copy-start(bf16[192,256]{1,0:T(8,128)(2,1)S(1)} %collective-permute-done.30.h2) | copy-start | bytes 294916
  202.6 4.9 %copy-start.19 = (bf16[192,256]{1,0:T(8,128)(2,1)}, bf16[192,256]{1,0:T(8,128)(2,1)S(1)}, u32[]{:S(2)}) copy-start(bf16[192,256]{1,0:T(8,128)(2,1)S(1)} %collective-permute-done.29.h1) | copy-start | bytes 294916
  (10 other events, 18.1 us)

commit v3 on v2

--- a/solution.py
+++ b/solution.py
@@ -81,8 +81,8 @@
     return out
 
 
-def gather_first(block):
-    return [block] + [send(block, first(step), "weights_first") for step in (1, -1, 2)]
+def gather_first(block, name):
+    return [block] + [send(block, first(step), name) for step in (1, -1, 2)]
 
 
 ROWS, CORE, SENDS, HEAD, STEPS, OTHER, FROM = 0, 16, 17, 25, 26, 30, 46
@@ -149,16 +149,14 @@
 def acts_kernel(own, other, out):
     for which, window in enumerate((own, other)):
         columns = window[...].T
-
-        def one(number, _):
-            row = lax.broadcasted_iota(jnp.int32, (528, 256), 0)
-            col = lax.broadcasted_iota(jnp.int32, (528, 256), 1)
-            pick = jnp.where(row == 2 * col + number, 1.0, 0.0).astype(BF16)
+        for odd in range(2):
+            row = lax.broadcasted_iota(jnp.int32, (528, 384), 0)
+            col = lax.broadcasted_iota(jnp.int32, (528, 384), 1)
+            pick = jnp.where(row == 2 * col + odd, 1.0, 0.0).astype(BF16)
             picked = jnp.dot(columns, pick, preferred_element_type=F32)
-            out[number, :, 256 * which : 256 * which + 256] = picked.astype(BF16)
-            return 0
-
-        lax.fori_loop(0, 6, one, 0)
+            for step in range(3):
+                lanes = slice(256 * which, 256 * which + 256)
+                out[2 * step + odd, :, lanes] = picked[:, step : step + 256].astype(BF16)
 
 
 def conv_kernel(base, table, acts, bias, *refs):
@@ -350,9 +348,10 @@
     taps = lax.dynamic_slice_in_dim(conv_weight.transpose(0, 2, 1), 48 * high, 48, axis=1)
     qkv = lax.dynamic_slice_in_dim(qkv_weight.transpose(0, 2, 1), 768 * high, 768, axis=2)
     last = lax.dynamic_slice_in_dim(out_weight.T, 48 * high, 48, axis=0)
-    block = jnp.concatenate([taps, qkv[1:], qkv[:1], last[None]], axis=0)
-    features = after(dna_features, block)
-    block = send(block, spread_z, "weights_z")
+    rest = jnp.concatenate([qkv[1:], qkv[:1], last[None]], axis=0)
+    features = dna_features
+    taps = send(taps, spread_z, "taps_z")
+    rest = send(after(rest, taps), spread_z, "rest_z")
 
     activated = jax.nn.gelu(features.astype(F32), approximate=True).astype(BF16)
     forward = [(16 * b + i, 16 * b + i + 1) for b in range(16) for i in range(15)]
@@ -370,14 +369,13 @@
         send(padded, other_core, "acts_core"),
     )
 
-    pieces = gather_first(block)
-    stack = stacked([after(pieces[0][:5], acts)] + [p[:5] for p in pieces[1:]])
+    pieces = gather_first(taps, "taps_first")
+    stack = stacked([after(pieces[0], rest)] + pieces[1:])
+    pieces = gather_first(after(rest, *pieces[1:]), "rest_first")
     low, high_stack = [send(stack, second(step), "conv_second") for step in (1, -1)]
-    far = (
-        send(low[:2], second(1), "conv_far"),
-        send(high_stack[2:], second(-1), "conv_far"),
-    )
-    qkv_stack = stacked([after(pieces[0][5:], low, high_stack)] + [p[5:] for p in pieces[1:]])
+    onward = low[:2], high_stack[2:]
+    far = send(onward[0], second(1), "conv_far"), send(onward[1], second(-1), "conv_far")
+    qkv_stack = stacked([after(pieces[0], onward[1], acts)] + pieces[1:])
     qkv_near = [send(qkv_stack, second(step), "qkv_second") for step in (1, -1)]
     qkv_groups = (
         qkv_stack,
@@ -451,7 +449,7 @@
     )
     base = call(base_kernel, [VMEM], shape(256, 1536), [], 1_000_000, tokens)
     other_last = send(after(last, queries), other_core, "out_core")
-    far_near = send(after(far, partial[0]), other_core, "keys_y_core")
+    far_near = send(far, other_core, "keys_y_core")
     heads = call(
         finish_kernel,
         [SMEM, SMEM] + [VMEM] * 6,

time: 213 us -> 225 us (1.056); the launches traced: 212 us -> 221 us
  starting transfers between devices: 53.4 us -> 81.2 us
  waiting for transfers between devices: 63.1 us -> 46.9 us
  Pallas kernels: 60.9 us -> 57.2 us
    ppermute x31 -> x35, starting transfers between devices: 48.7 us -> 75.7 us  [send(): return lax.ppermute(value, AXES, pairs)]
    ppermute x31 -> x35, waiting for transfers between devices: 59 us -> 46.9 us  [send(): return lax.ppermute(value, AXES, pairs)]
    ppermute x1, waiting for transfers between devices: 4.1 us -> 0.01 us  [shards(): behind = lax.ppermute(activated[:2], AXES, backward)]
    pallas_call x8, Pallas kernels: 60.9 us -> 57.2 us  [call(): pl.pallas_call(kernel, out_shape=outs, in_specs=ins, out_specs=jax.tree.m...]
    broadcast_in_dim x3 -> x1, local copies, waits for them, and re-layouts: 2.89 us -> 0.02 us  [shards(): rest = jnp.concatenate([qkv[1:], qkv[:1], last[None]], axis=0)]
    slice x7 -> x9, local copies, waits for them, and re-layouts: 5.23 us -> 6.28 us  [after(): zero = sum((o[(0,) * o.ndim].astype(F32) * 0.0 for o in others), F32(0.0))]
  transfers between devices with their start and end apart: 33 -> 37, of which waited for: 16 -> 16; matrix products, arithmetic and copies ran while one was open for 9% -> 11% of each run, Pallas kernels for 23% -> 20%
where the time goes in v3:
time: 225 us; the launch traced here: 221 us
  starting transfers between devices  81.2 us (36%)
  Pallas kernels  57.2 us (25%)
  waiting for transfers between devices  46.9 us (21%)
  local copies, waits for them, and re-layouts  26.5 us (12%)
  between operations  6.54 us (3%)
  other arithmetic  2.83 us (1%)
    ppermute x35, starting transfers between devices, send(): return lax.ppermute(value, AXES, pairs)  75.7 us
    pallas_call x8, Pallas kernels, call(): pl.pallas_call(kernel, out_shape=outs, in_specs=ins, out_specs=jax.tree.m...  57.2 us
    ppermute x35, waiting for transfers between devices, send(): return lax.ppermute(value, AXES, pairs)  46.9 us
    slice x9, local copies, waits for them, and re-layouts, after(): zero = sum((o[(0,) * o.ndim].astype(F32) * 0.0 for o in others), F32(0.0))  6.28 us
  transfers between devices with their start and end apart: 37, of which 16 were waited for; matrix products, arithmetic and copies ran while one was open for 11% of the time, Pallas kernels for 20%

profile of v3, /device:TPU:6, one launch (start us, length us, event | category | flops | bytes accessed | tf_op | source)
XLA Modules:
  0.0 221.2 jit_solution(15693655765531468194)
XLA Ops:
  1.1 6.5 %collective-permute-start.3 = (bf16[5,48,768]{2,1,0:T(8,128)(2,1)S(1)}, bf16[5,48,768]{2,1,0:T(8,128)(2,1)S(1)}, u32[]{:S(2)}, u32[]{:S(2)}) collective-permute-start(bf16[5,48,768]{2,1,0:T(8,128)(2,1)S(1)} %dynamic-slice_bitcast_fusion), channel_id=1, source_target_pairs={{0,4},{1,5},{2,2},{3,3},{4,6},{5,7},{6,0},{7,1},{8,18},{9,19},{10,... | collective-permute-start | bytes 1105928 | tf_op jit(solution)/shard_map/taps_z/ppermute | solution.py:36
  8.7 7.5 %collective-permute-done.3 = bf16[5,48,768]{2,1,0:T(8,128)(2,1)S(1)} collective-permute-done((bf16[5,48,768]{2,1,0:T(8,128)(2,1)S(1)}, bf16[5,48,768]{2,1,0:T(8,128)(2,1)S(1)}, u32[]{:S(2)}, u32[]{:S(2)}) %collective-permute-start.3) | collective-permute-done | bytes 368672 | tf_op jit(solution)/shard_map/taps_z/ppermute | solution.py:36
  17.5 6.3 %collective-permute-start.7 = (bf16[4,48,768]{2,1,0:T(8,128)(2,1)S(1)}, bf16[4,48,768]{2,1,0:T(8,128)(2,1)S(1)}, u32[]{:S(2)}, u32[]{:S(2)}) collective-permute-start(bf16[4,48,768]{2,1,0:T(8,128)(2,1)S(1)} %maximum_add_fusion), channel_id=1, source_target_pairs={{0,4},{1,5},{2,2},{3,3},{4,6},{5,7},{6,0},{7,1},{8,18},{9,19},{10,... | collective-permute-start | bytes 884744 | tf_op jit(solution)/shard_map/rest_z/ppermute | solution.py:36
  24.6 3.3 %collective-permute-start.6 = (bf16[5,48,768]{2,1,0:T(8,128)(2,1)S(1)}, bf16[5,48,768]{2,1,0:T(8,128)(2,1)S(1)}, u32[]{:S(2)}, u32[]{:S(2)}) collective-permute-start(bf16[5,48,768]{2,1,0:T(8,128)(2,1)S(1)} %collective-permute-done.3), channel_id=1, source_target_pairs={{0,64},{1,65},{2,66},{3,67},{4,68},{5,69},{6,70},{7,71},{8,72},{9,... | collective-permute-start | bytes 1105928 | tf_op jit(solution)/shard_map/taps_first/ppermute | solution.py:36
  27.9 1.3 collective-permute-start.1
  29.6 4.3 %collective-permute-start = (bf16[2,768]{1,0:T(2,128)(2,1)S(1)}, bf16[2,768]{1,0:T(2,128)(2,1)S(1)}, u32[]{:S(2)}, u32[]{:S(2)}) collective-permute-start(bf16[2,768]{1,0:T(2,128)(2,1)S(1)} %get-tuple-element.23), channel_id=1, source_target_pairs={{0,1},{1,2},{2,3},{3,4},{4,5},{5,6},{6,7},{7,8},{8,9},{9,10},{10,1... | collective-permute-start | bytes 9224 | tf_op jit(solution)/shard_map/ppermute | solution.py:359
  35.0 1.3 dynamic_update_slice.24
  39.1 3.5 %collective-permute-start.9 = (bf16[4,5,48,768]{3,2,1,0:T(8,128)(2,1)}, bf16[4,5,48,768]{3,2,1,0:T(8,128)(2,1)}, u32[]{:S(2)}, u32[]{:S(2)}) collective-permute-start(bf16[4,5,48,768]{3,2,1,0:T(8,128)(2,1)} %bitcast_dynamic-update-slice_fusion.refs_3_), channel_id=1, source_target_pairs={{0,33},{1,0},{2,35},{3,2},{4,37},{5,4},{6,39},{7,6},{8,41},{9,8},{... | collective-permute-start | bytes 4423688 | tf_op jit(solution)/shard_map/conv_second/ppermute | solution.py:36
  46.7 2.3 %collective-permute-start.14 = (bf16[4,48,768]{2,1,0:T(8,128)(2,1)S(1)}, bf16[4,48,768]{2,1,0:T(8,128)(2,1)S(1)}, u32[]{:S(2)}, u32[]{:S(2)}) collective-permute-start(bf16[4,48,768]{2,1,0:T(8,128)(2,1)S(1)} %broadcast_add_fusion.2), channel_id=1, source_target_pairs={{0,128},{1,129},{2,130},{3,131},{4,132},{5,133},{6,134},{7,135},{8... | collective-permute-start | bytes 884744 | tf_op jit(solution)/shard_map/rest_first/ppermute | solution.py:36
  49.0 1.1 collective-permute-start.15
  50.2 1.6 collective-permute-start.8
  52.7 6.5 %acts_kernel.1.refs_1_ = bf16[6,768,512]{2,1,0:T(8,128)(2,1)} custom-call(bf16[528,768]{1,0:T(8,128)(2,1)} %copy-done.3, bf16[528,768]{1,0:T(8,128)(2,1)} %copy-done.6), custom_call_target="tpu_custom_call" | custom-call | flops 1000000000 | bytes 8000000 | tf_op jit(solution)/shard_map/acts_kernel/pallas_call | solution.py:327
  59.1 1.2 slice.129
  61.1 1.7 collective-permute-done.15
  63.0 3.0 %collective-permute-done.9.refs_5_ = bf16[4,5,48,768]{3,2,1,0:T(8,128)(2,1)} collective-permute-done((bf16[4,5,48,768]{3,2,1,0:T(8,128)(2,1)}, bf16[4,5,48,768]{3,2,1,0:T(8,128)(2,1)}, u32[]{:S(2)}, u32[]{:S(2)}) %collective-permute-start.9) | collective-permute-done | bytes 1474592 | tf_op jit(solution)/shard_map/conv_second/ppermute | solution.py:36
  66.1 1.3 slice.128
  68.1 1.1 collective-permute-start.17
  69.3 2.9 %collective-permute-start.18 = (bf16[4,4,48,768]{3,2,1,0:T(8,128)(2,1)S(1)}, bf16[4,4,48,768]{3,2,1,0:T(8,128)(2,1)}, u32[]{:S(2)}, u32[]{:S(2)}) collective-permute-start(bf16[4,4,48,768]{3,2,1,0:T(8,128)(2,1)S(1)} %bitcast_dynamic-update-slice_fusion.3.g0), channel_id=1, source_target_pairs={{0,33},{1,0},{2,35},{3,2},{4,37},{5,4},{6,39},{7,6},{8,41},{9,8},{... | collective-permute-start | bytes 3538952 | tf_op jit(solution)/shard_map/qkv_second/ppermute | solution.py:36
  74.2 2.0 slice.123
  76.6 2.0 slice.124
  78.7 2.9 %collective-permute-start.11 = (bf16[2,5,48,768]{3,2,1,0:T(8,128)(2,1)}, bf16[2,5,48,768]{3,2,1,0:T(8,128)(2,1)}, u32[]{:S(2)}, u32[]{:S(2)}) collective-permute-start(bf16[2,5,48,768]{3,2,1,0:T(8,128)(2,1)} %slice.124), channel_id=1, source_target_pairs={{0,33},{1,0},{2,35},{3,2},{4,37},{5,4},{6,39},{7,6},{8,41},{9,8},{... | collective-permute-start | bytes 2211848 | tf_op jit(solution)/shard_map/conv_far/ppermute | solution.py:36
  81.5 1.3 fusion.6.refs_0_.table
  82.8 11.0 %conv_kernel.2.refs_3_.ma = bf16[12,48,512]{2,1,0:T(8,128)(2,1)} custom-call(s32[50]{0:T(128)} %fusion.6.refs_0_.table, bf16[6,768,512]{2,1,0:T(8,128)(2,1)} %acts_kernel.1.refs_1_, f32[16,48,1]{2,1,0:T(8,128)} %reshape.42.refs_2_, bf16[4,5,48,768]{3,2,1,0:T(8,128)(2,1)} %bitcast_dynamic-update-slice_fusion.refs_3_, ...), custom_call_target="tpu_custom_call" | custom-call | flops 4499999744 | bytes 8000000 | tf_op jit(solution)/shard_map/conv_kernel/pallas_call | solution.py:327
  96.9 2.4 %collective-permute-start.20 = (bf16[2,4,48,768]{3,2,1,0:T(8,128)(2,1)S(1)}, bf16[2,4,48,768]{3,2,1,0:T(8,128)(2,1)S(1)}, u32[]{:S(2)}, u32[]{:S(2)}) collective-permute-start(bf16[2,4,48,768]{3,2,1,0:T(8,128)(2,1)S(1)} %slice.131), channel_id=1, source_target_pairs={{0,33},{1,0},{2,35},{3,2},{4,37},{5,4},{6,39},{7,6},{8,41},{9,8},{... | collective-permute-start | bytes 1769480 | tf_op jit(solution)/shard_map/qkv_far/ppermute | solution.py:36
  100.2 6.6 %conv_kernel.3.mb = bf16[4,48,512]{2,1,0:T(8,128)(2,1)} custom-call(s32[50]{0:T(128)} %fusion.6.refs_0_.table, bf16[6,768,512]{2,1,0:T(8,128)(2,1)} %acts_kernel.1.refs_1_, f32[16,48,1]{2,1,0:T(8,128)} %reshape.42.refs_2_, bf16[12,48,512]{2,1,0:T(8,128)(2,1)} %conv_kernel.2.refs_3_.ma, bf16[2,5,48,768]{3,2,1,0:T(8,128)(2,1)} %copy-done.9, ...), custom_call_target="tpu_custom_call" | custom-call | flops 1500000000 | bytes 8000000 | tf_op jit(solution)/shard_map/conv_kernel/pallas_call | solution.py:327
  106.9 1.5 reshape.43.gain
  109.5 8.7 %project_kernel.1 = (bf16[4,2,192,256]{3,2,1,0:T(8,128)(2,1)}, bf16[4,192,256]{2,1,0:T(8,128)(2,1)}, bf16[16,48,768]{2,1,0:T(8,128)(2,1)}, bf16[2,16,48,512]{3,2,1,0:T(8,128)(2,1)}) custom-call(s32[50]{0:T(128)} %fusion.6.refs_0_.table, bf16[12,48,512]{2,1,0:T(8,128)(2,1)} %conv_kernel.2.refs_3_.ma, bf16[4,48,512]{2,1,0:T(8,128)(2,1)} %conv_kernel.3.mb, ...), custom_call_target="tpu_custom_call" | custom-call | flops 1800000000 | bytes 8000000 | tf_op jit(solution)/shard_map/project_kernel/pallas_call | solution.py:327
  118.2 1.3 slice_bitcast_fusion.2
  119.5 1.1 collective-permute-start.21
  120.7 6.1 %collective-permute-start.28 = (bf16[2,192,256]{2,1,0:T(8,128)(2,1)S(1)}, bf16[2,192,256]{2,1,0:T(8,128)(2,1)S(1)}, u32[]{:S(2)}, u32[]{:S(2)}) collective-permute-start(bf16[2,192,256]{2,1,0:T(8,128)(2,1)S(1)} %get-tuple-element.20), channel_id=1, source_target_pairs={{0,8},{1,9},{2,24},{3,25},{4,12},{5,13},{6,28},{7,29},{8,0},{9,1},... | collective-permute-start | bytes 589832 | tf_op jit(solution)/shard_map/keys_z/ppermute | solution.py:36
  127.5 4.1 %collective-permute-start.26 = (bf16[2,192,256]{2,1,0:T(8,128)(2,1)S(1)}, bf16[2,192,256]{2,1,0:T(8,128)(2,1)S(1)}, u32[]{:S(2)}, u32[]{:S(2)}) collective-permute-start(bf16[2,192,256]{2,1,0:T(8,128)(2,1)S(1)} %get-tuple-element.19), channel_id=1, source_target_pairs={{0,12},{1,13},{2,28},{3,29},{4,0},{5,1},{6,16},{7,17},{8,4},{9,5},... | collective-permute-start | bytes 589832 | tf_op jit(solution)/shard_map/keys_z/ppermute | solution.py:36
  132.1 9.6 %collective-permute-done.28 = bf16[2,192,256]{2,1,0:T(8,128)(2,1)S(1)} collective-permute-done((bf16[2,192,256]{2,1,0:T(8,128)(2,1)S(1)}, bf16[2,192,256]{2,1,0:T(8,128)(2,1)S(1)}, u32[]{:S(2)}, u32[]{:S(2)}) %collective-permute-start.28) | collective-permute-done | bytes 196640 | tf_op jit(solution)/shard_map/keys_z/ppermute | solution.py:36
  144.2 2.1 collective-permute-start.22
  146.3 1.5 collective-permute-start.31
  147.8 6.4 %collective-permute-done.22 = bf16[192,256]{1,0:T(8,128)(2,1)S(1)} collective-permute-done((bf16[192,256]{1,0:T(8,128)(2,1)S(1)}, bf16[192,256]{1,0:T(8,128)(2,1)S(1)}, u32[]{:S(2)}, u32[]{:S(2)}) %collective-permute-start.22) | collective-permute-done | bytes 98336 | tf_op jit(solution)/shard_map/queries_z/ppermute | solution.py:36
  155.3 6.1 %collective-permute-done.29.g0 = bf16[4,2,192,256]{3,2,1,0:T(8,128)(2,1)S(1)} collective-permute-done((bf16[4,2,192,256]{3,2,1,0:T(8,128)(2,1)S(1)}, bf16[4,2,192,256]{3,2,1,0:T(8,128)(2,1)S(1)}, u32[]{:S(2)}, u32[]{:S(2)}) %collective-permute-start.29) | collective-permute-done | bytes 786464 | tf_op jit(solution)/shard_map/keys_y/ppermute | solution.py:36
  162.2 5.4 %collective-permute-start.25 = (bf16[192,256]{1,0:T(8,128)(2,1)S(1)}, bf16[192,256]{1,0:T(8,128)(2,1)S(1)}, u32[]{:S(2)}, u32[]{:S(2)}) collective-permute-start(bf16[192,256]{1,0:T(8,128)(2,1)S(1)} %get-tuple-element.30), channel_id=1, source_target_pairs={{0,8},{1,9},{2,24},{3,25},{4,12},{5,13},{6,28},{7,29},{8,0},{9,1},... | collective-permute-start | bytes 294920 | tf_op jit(solution)/shard_map/queries_z/ppermute | solution.py:36
  168.2 2.6 %collective-permute-done.25 = bf16[192,256]{1,0:T(8,128)(2,1)S(1)} collective-permute-done((bf16[192,256]{1,0:T(8,128)(2,1)S(1)}, bf16[192,256]{1,0:T(8,128)(2,1)S(1)}, u32[]{:S(2)}, u32[]{:S(2)}) %collective-permute-start.25) | collective-permute-done | bytes 98336 | tf_op jit(solution)/shard_map/queries_z/ppermute | solution.py:36
  170.8 6.4 %collective-permute-start.23 = (bf16[192,256]{1,0:T(8,128)(2,1)S(1)}, bf16[192,256]{1,0:T(8,128)(2,1)S(1)}, u32[]{:S(2)}, u32[]{:S(2)}) collective-permute-start(bf16[192,256]{1,0:T(8,128)(2,1)S(1)} %get-tuple-element.32), channel_id=1, source_target_pairs={{0,12},{1,13},{2,28},{3,29},{4,0},{5,1},{6,16},{7,17},{8,4},{9,5},... | collective-permute-start | bytes 294920 | tf_op jit(solution)/shard_map/queries_z/ppermute | solution.py:36
  177.2 2.5 %collective-permute-done.23 = bf16[192,256]{1,0:T(8,128)(2,1)S(1)} collective-permute-done((bf16[192,256]{1,0:T(8,128)(2,1)S(1)}, bf16[192,256]{1,0:T(8,128)(2,1)S(1)}, u32[]{:S(2)}, u32[]{:S(2)}) %collective-permute-start.23) | collective-permute-done | bytes 98336 | tf_op jit(solution)/shard_map/queries_z/ppermute | solution.py:36
  180.6 8.7 %attend_kernel.1 = (f32[4,256,128]{2,1,0:T(8,128)}, f32[4,256,128]{2,1,0:T(8,128)}, f32[4,256,192]{2,1,0:T(8,128)}) custom-call(s32[50]{0:T(128)} %fusion.6.refs_0_.table, f32[4]{0:T(128)} %factor.3, bf16[4,192,256]{2,1,0:T(8,128)(2,1)} %pad_maximum_fusion.1.queries, bf16[4,2,192,256]{3,2,1,0:T(8,128)(2,1)} %copy-done.8, ...), custom_call_target="tpu_custom_call" | custom-call | flops 1600000000 | bytes 8000000 | tf_op jit(solution)/shard_map/attend_kernel/pallas_call | solution.py:327
  189.2 9.5 %finish_kernel.1 = bf16[4,192,256]{2,1,0:T(8,128)(2,1)} custom-call(s32[50]{0:T(128)} %fusion.6.refs_0_.table, f32[4]{0:T(128)} %factor.3, bf16[4,192,256]{2,1,0:T(8,128)(2,1)} %pad_maximum_fusion.1.queries, bf16[4,2,192,256]{3,2,1,0:T(8,128)(2,1)} %copy-done.19, bf16[4,2,192,256]{3,2,1,0:T(8,128)(2,1)} %collective-permute-done.30.g1, ...), custom_call_target="tpu_custom_call" | custom-call | flops 1600000000 | bytes 8000000 | tf_op jit(solution)/shard_map/finish_kernel/pallas_call | solution.py:327
  199.8 4.1 %collective-permute-start.32 = (bf16[192,256]{1,0:T(8,128)(2,1)S(1)}, bf16[192,256]{1,0:T(8,128)(2,1)S(1)}, u32[]{:S(2)}, u32[]{:S(2)}) collective-permute-start(bf16[192,256]{1,0:T(8,128)(2,1)S(1)} %get-tuple-element.28), channel_id=1, source_target_pairs={{0,4},{1,5},{2,8},{3,9},{4,16},{5,17},{6,20},{7,21},{8,12},{9,13},... | collective-permute-start | bytes 294920 | tf_op jit(solution)/shard_map/heads_back/ppermute | solution.py:36
  203.9 3.1 %collective-permute-start.33 = (bf16[192,256]{1,0:T(8,128)(2,1)S(1)}, bf16[192,256]{1,0:T(8,128)(2,1)S(1)}, u32[]{:S(2)}, u32[]{:S(2)}) collective-permute-start(bf16[192,256]{1,0:T(8,128)(2,1)S(1)} %get-tuple-element.27), channel_id=1, source_target_pairs={{0,12},{1,13},{2,0},{3,1},{4,28},{5,29},{6,24},{7,25},{8,4},{9,5},... | collective-permute-start | bytes 294920 | tf_op jit(solution)/shard_map/heads_back/ppermute | solution.py:36
  207.6 2.5 %collective-permute-start.35 = (bf16[192,256]{1,0:T(8,128)(2,1)S(1)}, bf16[192,256]{1,0:T(8,128)(2,1)S(1)}, u32[]{:S(2)}, u32[]{:S(2)}) collective-permute-start(bf16[192,256]{1,0:T(8,128)(2,1)S(1)} %get-tuple-element.25), channel_id=1, source_target_pairs={{0,8},{1,9},{2,4},{3,5},{4,20},{5,21},{6,16},{7,17},{8,0},{9,1},{1... | collective-permute-start | bytes 294920 | tf_op jit(solution)/shard_map/heads_back/ppermute | solution.py:36
  210.1 2.6 %base_kernel.1.base = bf16[256,1536]{1,0:T(8,128)(2,1)} custom-call(bf16[2,16,48,512]{3,2,1,0:T(8,128)(2,1)} %get-tuple-element.17.tokens), custom_call_target="tpu_custom_call" | custom-call | flops 1000000 | bytes 8000000 | tf_op jit(solution)/shard_map/base_kernel/pallas_call | solution.py:327
  212.7 4.1 %collective-permute-done.35.h3 = bf16[192,256]{1,0:T(8,128)(2,1)S(1)} collective-permute-done((bf16[192,256]{1,0:T(8,128)(2,1)S(1)}, bf16[192,256]{1,0:T(8,128)(2,1)S(1)}, u32[]{:S(2)}, u32[]{:S(2)}) %collective-permute-start.35) | collective-permute-done | bytes 98336 | tf_op jit(solution)/shard_map/heads_back/ppermute | solution.py:36
  217.5 3.8 %out_kernel.1 = bf16[256,1536]{1,0:T(8,128)(2,1)} custom-call(s32[50]{0:T(128)} %fusion.6.refs_0_.table, bf16[192,256]{1,0:T(8,128)(2,1)} %copy-done.12, bf16[192,256]{1,0:T(8,128)(2,1)} %copy-done.13, bf16[192,256]{1,0:T(8,128)(2,1)} %copy-done.14, bf16[192,256]{1,0:T(8,128)(2,1)} %copy-done.15, bf16[256,1536]{1,0:T(8,128)(2,1)} %base_kernel.1.base, ...), custom_call_target="tpu_custom_call" | custom-call | flops 600000000 | bytes 8000000 | tf_op jit(solution)/shard_map/out_kernel/pallas_call | solution.py:327
  (118 shorter events, 26.0 us)
Async XLA Ops:
  0.0 8.7 %copy-start.16 = (bf16[768,96]{0,1:T(8,128)(2,1)S(1)}, bf16[768,96]{0,1:T(8,128)(2,1)}, u32[]{:S(2)}) copy-start(bf16[768,96]{0,1:T(8,128)(2,1)} %param.14) | copy-start | bytes 442372
  0.0 24.0 %copy-start.7 = (bf16[512,768]{1,0:T(8,128)(2,1)S(1)}, bf16[512,768]{1,0:T(8,128)(2,1)}, u32[]{:S(2)}) copy-start(bf16[512,768]{1,0:T(8,128)(2,1)} %param.8) | copy-start | bytes 2359300
  1.1 15.1 %collective-permute-start.3 = (bf16[5,48,768]{2,1,0:T(8,128)(2,1)S(1)}, bf16[5,48,768]{2,1,0:T(8,128)(2,1)S(1)}, u32[]{:S(2)}, u32[]{:S(2)}) collective-permute-start(bf16[5,48,768]{2,1,0:T(8,128)(2,1)S(1)} %dynamic-slice_bitcast_fusion), channel_id=1, source_target_pairs={{0,4},{1,5},{2,2},{3,3},{4,6},{5,7},{6,0},{7,1},{8,18},{9,19},{10,... | collective-permute-start | bytes 1105928 | tf_op jit(solution)/shard_map/taps_z/ppermute | solution.py:36
  17.5 12.1 %collective-permute-start.7 = (bf16[4,48,768]{2,1,0:T(8,128)(2,1)S(1)}, bf16[4,48,768]{2,1,0:T(8,128)(2,1)S(1)}, u32[]{:S(2)}, u32[]{:S(2)}) collective-permute-start(bf16[4,48,768]{2,1,0:T(8,128)(2,1)S(1)} %maximum_add_fusion), channel_id=1, source_target_pairs={{0,4},{1,5},{2,2},{3,3},{4,6},{5,7},{6,0},{7,1},{8,18},{9,19},{10,... | collective-permute-start | bytes 884744 | tf_op jit(solution)/shard_map/rest_z/ppermute | solution.py:36
  23.8 11.2 %collective-permute-start.4 = (bf16[5,48,768]{2,1,0:T(8,128)(2,1)S(1)}, bf16[5,48,768]{2,1,0:T(8,128)(2,1)S(1)}, u32[]{:S(2)}, u32[]{:S(2)}) collective-permute-start(bf16[5,48,768]{2,1,0:T(8,128)(2,1)S(1)} %collective-permute-done.3), channel_id=1, source_target_pairs={{0,128},{1,129},{2,130},{3,131},{4,132},{5,133},{6,134},{7,135},{8... | collective-permute-start | bytes 1105928 | tf_op jit(solution)/shard_map/taps_first/ppermute | solution.py:36
  23.9 12.8 %collective-permute-start.5 = (bf16[5,48,768]{2,1,0:T(8,128)(2,1)S(1)}, bf16[5,48,768]{2,1,0:T(8,128)(2,1)S(1)}, u32[]{:S(2)}, u32[]{:S(2)}) collective-permute-start(bf16[5,48,768]{2,1,0:T(8,128)(2,1)S(1)} %collective-permute-done.3), channel_id=1, source_target_pairs={{0,192},{1,193},{2,194},{3,195},{4,196},{5,197},{6,198},{7,199},{8... | collective-permute-start | bytes 1105928 | tf_op jit(solution)/shard_map/taps_first/ppermute | solution.py:36
  24.6 12.9 %collective-permute-start.6 = (bf16[5,48,768]{2,1,0:T(8,128)(2,1)S(1)}, bf16[5,48,768]{2,1,0:T(8,128)(2,1)S(1)}, u32[]{:S(2)}, u32[]{:S(2)}) collective-permute-start(bf16[5,48,768]{2,1,0:T(8,128)(2,1)S(1)} %collective-permute-done.3), channel_id=1, source_target_pairs={{0,64},{1,65},{2,66},{3,67},{4,68},{5,69},{6,70},{7,71},{8,72},{9,... | collective-permute-start | bytes 1105928 | tf_op jit(solution)/shard_map/taps_first/ppermute | solution.py:36
  27.9 14.7 %collective-permute-start.1 = (bf16[2,768]{1,0:T(2,128)(2,1)S(1)}, bf16[2,768]{1,0:T(2,128)(2,1)S(1)}, u32[]{:S(2)}, u32[]{:S(2)}) collective-permute-start(bf16[2,768]{1,0:T(2,128)(2,1)S(1)} %get-tuple-element.24), channel_id=1, source_target_pairs={{1,0},{2,1},{3,2},{4,3},{5,4},{6,5},{7,6},{8,7},{9,8},{10,9},{11,1... | collective-permute-start | bytes 9224 | tf_op jit(solution)/shard_map/ppermute | solution.py:360
  29.6 13.0 %collective-permute-start = (bf16[2,768]{1,0:T(2,128)(2,1)S(1)}, bf16[2,768]{1,0:T(2,128)(2,1)S(1)}, u32[]{:S(2)}, u32[]{:S(2)}) collective-permute-start(bf16[2,768]{1,0:T(2,128)(2,1)S(1)} %get-tuple-element.23), channel_id=1, source_target_pairs={{0,1},{1,2},{2,3},{3,4},{4,5},{5,6},{6,7},{7,8},{8,9},{9,10},{10,1... | collective-permute-start | bytes 9224 | tf_op jit(solution)/shard_map/ppermute | solution.py:359
  39.1 27.0 %collective-permute-start.9 = (bf16[4,5,48,768]{3,2,1,0:T(8,128)(2,1)}, bf16[4,5,48,768]{3,2,1,0:T(8,128)(2,1)}, u32[]{:S(2)}, u32[]{:S(2)}) collective-permute-start(bf16[4,5,48,768]{3,2,1,0:T(8,128)(2,1)} %bitcast_dynamic-update-slice_fusion.refs_3_), channel_id=1, source_target_pairs={{0,33},{1,0},{2,35},{3,2},{4,37},{5,4},{6,39},{7,6},{8,41},{9,8},{... | collective-permute-start | bytes 4423688 | tf_op jit(solution)/shard_map/conv_second/ppermute | solution.py:36
  42.9 9.5 %copy-start.3 = (bf16[528,768]{1,0:T(8,128)(2,1)}, bf16[528,768]{1,0:T(8,128)(2,1)S(1)}, u32[]{:S(2)}) copy-start(bf16[528,768]{1,0:T(8,128)(2,1)S(1)} %maximum_maximum_fusion.own) | copy-start | bytes 2433028
  42.9 8.9 %collective-permute-start.2 = (bf16[528,768]{1,0:T(8,128)(2,1)S(1)}, bf16[528,768]{1,0:T(8,128)(2,1)S(1)}, u32[]{:S(2)}, u32[]{:S(2)}) collective-permute-start(bf16[528,768]{1,0:T(8,128)(2,1)S(1)} %maximum_maximum_fusion.own), channel_id=1, source_target_pairs={{0,16},{1,17},{2,18},{3,19},{4,20},{5,21},{6,22},{7,23},{8,24},{9,... | collective-permute-start | bytes 2433032 | tf_op jit(solution)/shard_map/acts_core/ppermute | solution.py:36
  46.7 14.3 %collective-permute-start.14 = (bf16[4,48,768]{2,1,0:T(8,128)(2,1)S(1)}, bf16[4,48,768]{2,1,0:T(8,128)(2,1)S(1)}, u32[]{:S(2)}, u32[]{:S(2)}) collective-permute-start(bf16[4,48,768]{2,1,0:T(8,128)(2,1)S(1)} %broadcast_add_fusion.2), channel_id=1, source_target_pairs={{0,128},{1,129},{2,130},{3,131},{4,132},{5,133},{6,134},{7,135},{8... | collective-permute-start | bytes 884744 | tf_op jit(solution)/shard_map/rest_first/ppermute | solution.py:36
  49.0 13.8 %collective-permute-start.15 = (bf16[4,48,768]{2,1,0:T(8,128)(2,1)S(1)}, bf16[4,48,768]{2,1,0:T(8,128)(2,1)S(1)}, u32[]{:S(2)}, u32[]{:S(2)}) collective-permute-start(bf16[4,48,768]{2,1,0:T(8,128)(2,1)S(1)} %broadcast_add_fusion.2), channel_id=1, source_target_pairs={{0,192},{1,193},{2,194},{3,195},{4,196},{5,197},{6,198},{7,199},{8... | collective-permute-start | bytes 884744 | tf_op jit(solution)/shard_map/rest_first/ppermute | solution.py:36
  50.2 24.0 %collective-permute-start.8 = (bf16[4,5,48,768]{3,2,1,0:T(8,128)(2,1)}, bf16[4,5,48,768]{3,2,1,0:T(8,128)(2,1)}, u32[]{:S(2)}, u32[]{:S(2)}) collective-permute-start(bf16[4,5,48,768]{3,2,1,0:T(8,128)(2,1)} %bitcast_dynamic-update-slice_fusion.refs_3_), channel_id=1, source_target_pairs={{0,1},{1,32},{2,3},{3,34},{4,5},{5,36},{6,7},{7,38},{8,9},{9,40},{... | collective-permute-start | bytes 4423688 | tf_op jit(solution)/shard_map/conv_second/ppermute | solution.py:36
  51.8 11.3 %collective-permute-start.16 = (bf16[4,48,768]{2,1,0:T(8,128)(2,1)S(1)}, bf16[4,48,768]{2,1,0:T(8,128)(2,1)S(1)}, u32[]{:S(2)}, u32[]{:S(2)}) collective-permute-start(bf16[4,48,768]{2,1,0:T(8,128)(2,1)S(1)} %broadcast_add_fusion.2), channel_id=1, source_target_pairs={{0,64},{1,65},{2,66},{3,67},{4,68},{5,69},{6,70},{7,71},{8,72},{9,... | collective-permute-start | bytes 884744 | tf_op jit(solution)/shard_map/rest_first/ppermute | solution.py:36
  61.0 11.2 %copy-start.18 = (f32[1536]{0:T(1024)S(1)}, f32[1536]{0:T(1024)}, u32[]{:S(2)}) copy-start(f32[1536]{0:T(1024)} %param.10) | copy-start | bytes 18436
  68.1 10.5 %copy-start.2 = (bf16[4,4,48,768]{3,2,1,0:T(8,128)(2,1)}, bf16[4,4,48,768]{3,2,1,0:T(8,128)(2,1)S(1)}, u32[]{:S(2)}) copy-start(bf16[4,4,48,768]{3,2,1,0:T(8,128)(2,1)S(1)} %bitcast_dynamic-update-slice_fusion.3.g0) | copy-start | bytes 3538948
  68.1 25.8 %collective-permute-start.17 = (bf16[4,4,48,768]{3,2,1,0:T(8,128)(2,1)S(1)}, bf16[4,4,48,768]{3,2,1,0:T(8,128)(2,1)S(1)}, u32[]{:S(2)}, u32[]{:S(2)}) collective-permute-start(bf16[4,4,48,768]{3,2,1,0:T(8,128)(2,1)S(1)} %bitcast_dynamic-update-slice_fusion.3.g0), channel_id=1, source_target_pairs={{0,1},{1,32},{2,3},{3,34},{4,5},{5,36},{6,7},{7,38},{8,9},{9,40},{... | collective-permute-start | bytes 3538952 | tf_op jit(solution)/shard_map/qkv_second/ppermute | solution.py:36
  69.3 26.5 %collective-permute-start.18 = (bf16[4,4,48,768]{3,2,1,0:T(8,128)(2,1)S(1)}, bf16[4,4,48,768]{3,2,1,0:T(8,128)(2,1)}, u32[]{:S(2)}, u32[]{:S(2)}) collective-permute-start(bf16[4,4,48,768]{3,2,1,0:T(8,128)(2,1)S(1)} %bitcast_dynamic-update-slice_fusion.3.g0), channel_id=1, source_target_pairs={{0,33},{1,0},{2,35},{3,2},{4,37},{5,4},{6,39},{7,6},{8,41},{9,8},{... | collective-permute-start | bytes 3538952 | tf_op jit(solution)/shard_map/qkv_second/ppermute | solution.py:36
  76.2 23.1 %collective-permute-start.10 = (bf16[2,5,48,768]{3,2,1,0:T(8,128)(2,1)}, bf16[2,5,48,768]{3,2,1,0:T(8,128)(2,1)S(1)}, u32[]{:S(2)}, u32[]{:S(2)}) collective-permute-start(bf16[2,5,48,768]{3,2,1,0:T(8,128)(2,1)} %slice.123), channel_id=1, source_target_pairs={{0,1},{1,32},{2,3},{3,34},{4,5},{5,36},{6,7},{7,38},{8,9},{9,40},{... | collective-permute-start | bytes 2211848 | tf_op jit(solution)/shard_map/conv_far/ppermute | solution.py:36
  78.7 20.7 %collective-permute-start.11 = (bf16[2,5,48,768]{3,2,1,0:T(8,128)(2,1)}, bf16[2,5,48,768]{3,2,1,0:T(8,128)(2,1)}, u32[]{:S(2)}, u32[]{:S(2)}) collective-permute-start(bf16[2,5,48,768]{3,2,1,0:T(8,128)(2,1)} %slice.124), channel_id=1, source_target_pairs={{0,33},{1,0},{2,35},{3,2},{4,37},{5,4},{6,39},{7,6},{8,41},{9,8},{... | collective-permute-start | bytes 2211848 | tf_op jit(solution)/shard_map/conv_far/ppermute | solution.py:36
  93.8 14.6 %collective-permute-start.12 = (bf16[12,48,512]{2,1,0:T(8,128)(2,1)}, bf16[12,48,512]{2,1,0:T(8,128)(2,1)}, u32[]{:S(2)}, u32[]{:S(2)}) collective-permute-start(bf16[12,48,512]{2,1,0:T(8,128)(2,1)} %conv_kernel.2.refs_3_.ma), channel_id=1, source_target_pairs={{0,16},{1,17},{2,18},{3,19},{4,20},{5,21},{6,22},{7,23},{8,24},{9,... | collective-permute-start | bytes 1769480 | tf_op jit(solution)/shard_map/pooled_core/ppermute | solution.py:36
  93.9 12.9 %copy-start.4 = (bf16[4,4,48,768]{3,2,1,0:T(8,128)(2,1)}, bf16[4,4,48,768]{3,2,1,0:T(8,128)(2,1)S(1)}, u32[]{:S(2)}) copy-start(bf16[4,4,48,768]{3,2,1,0:T(8,128)(2,1)S(1)} %collective-permute-done.17.g1) | copy-start | bytes 3538948
  94.9 13.8 %collective-permute-start.19 = (bf16[2,4,48,768]{3,2,1,0:T(8,128)(2,1)}, bf16[2,4,48,768]{3,2,1,0:T(8,128)(2,1)}, u32[]{:S(2)}, u32[]{:S(2)}) collective-permute-start(bf16[2,4,48,768]{3,2,1,0:T(8,128)(2,1)} %slice.130), channel_id=1, source_target_pairs={{0,1},{1,32},{2,3},{3,34},{4,5},{5,36},{6,7},{7,38},{8,9},{9,40},{... | collective-permute-start | bytes 1769480 | tf_op jit(solution)/shard_map/qkv_far/ppermute | solution.py:36
  96.9 10.0 %copy-start.17 = (f32[1536]{0:T(1024)S(1)}, f32[1536]{0:T(1024)}, u32[]{:S(2)}) copy-start(f32[1536]{0:T(1024)} %param.11) | copy-start | bytes 18436
  96.9 11.8 %collective-permute-start.20 = (bf16[2,4,48,768]{3,2,1,0:T(8,128)(2,1)S(1)}, bf16[2,4,48,768]{3,2,1,0:T(8,128)(2,1)S(1)}, u32[]{:S(2)}, u32[]{:S(2)}) collective-permute-start(bf16[2,4,48,768]{3,2,1,0:T(8,128)(2,1)S(1)} %slice.131), channel_id=1, source_target_pairs={{0,33},{1,0},{2,35},{3,2},{4,37},{5,4},{6,39},{7,6},{8,41},{9,8},{... | collective-permute-start | bytes 1769480 | tf_op jit(solution)/shard_map/qkv_far/ppermute | solution.py:36
  106.8 1.9 collective-permute-start.13
  118.2 25.9 %copy-start.11 = (bf16[4,192,256]{2,1,0:T(8,128)(2,1)S(1)}, bf16[4,192,256]{2,1,0:T(8,128)(2,1)}, u32[]{:S(2)}) copy-start(bf16[4,192,256]{2,1,0:T(8,128)(2,1)} %get-tuple-element.12) | copy-start | bytes 1179652
  119.5 12.6 %collective-permute-start.21 = (bf16[2,192,256]{2,1,0:T(8,128)(2,1)S(1)}, bf16[2,192,256]{2,1,0:T(8,128)(2,1)S(1)}, u32[]{:S(2)}, u32[]{:S(2)}) collective-permute-start(bf16[2,192,256]{2,1,0:T(8,128)(2,1)S(1)} %get-tuple-element.22), channel_id=1, source_target_pairs={{0,4},{1,5},{2,20},{3,21},{4,8},{5,9},{6,24},{7,25},{8,12},{9,13},... | collective-permute-start | bytes 589832 | tf_op jit(solution)/shard_map/keys_z/ppermute | solution.py:36
  120.7 21.1 %collective-permute-start.28 = (bf16[2,192,256]{2,1,0:T(8,128)(2,1)S(1)}, bf16[2,192,256]{2,1,0:T(8,128)(2,1)S(1)}, u32[]{:S(2)}, u32[]{:S(2)}) collective-permute-start(bf16[2,192,256]{2,1,0:T(8,128)(2,1)S(1)} %get-tuple-element.20), channel_id=1, source_target_pairs={{0,8},{1,9},{2,24},{3,25},{4,12},{5,13},{6,28},{7,29},{8,0},{9,1},... | collective-permute-start | bytes 589832 | tf_op jit(solution)/shard_map/keys_z/ppermute | solution.py:36
  126.8 14.9 %collective-permute-start.27 = (bf16[2,192,256]{2,1,0:T(8,128)(2,1)S(1)}, bf16[2,192,256]{2,1,0:T(8,128)(2,1)S(1)}, u32[]{:S(2)}, u32[]{:S(2)}) collective-permute-start(bf16[2,192,256]{2,1,0:T(8,128)(2,1)S(1)} %get-tuple-element.21), channel_id=1, source_target_pairs={{0,0},{1,1},{2,16},{3,17},{4,4},{5,5},{6,20},{7,21},{8,8},{9,9},{1... | collective-permute-start | bytes 589832 | tf_op jit(solution)/shard_map/keys_z/ppermute | solution.py:36
  127.5 15.0 %collective-permute-start.26 = (bf16[2,192,256]{2,1,0:T(8,128)(2,1)S(1)}, bf16[2,192,256]{2,1,0:T(8,128)(2,1)S(1)}, u32[]{:S(2)}, u32[]{:S(2)}) collective-permute-start(bf16[2,192,256]{2,1,0:T(8,128)(2,1)S(1)} %get-tuple-element.19), channel_id=1, source_target_pairs={{0,12},{1,13},{2,28},{3,29},{4,0},{5,1},{6,16},{7,17},{8,4},{9,5},... | collective-permute-start | bytes 589832 | tf_op jit(solution)/shard_map/keys_z/ppermute | solution.py:36
  142.5 19.0 %copy-start.1 = (bf16[16,48,768]{2,1,0:T(8,128)(2,1)S(1)}, bf16[16,48,768]{2,1,0:T(8,128)(2,1)}, u32[]{:S(2)}) copy-start(bf16[16,48,768]{2,1,0:T(8,128)(2,1)} %get-tuple-element.18.mine) | copy-start | bytes 3538948
  142.6 19.0 %copy-start.8 = (bf16[4,2,192,256]{3,2,1,0:T(8,128)(2,1)}, bf16[4,2,192,256]{3,2,1,0:T(8,128)(2,1)S(1)}, u32[]{:S(2)}) copy-start(bf16[4,2,192,256]{3,2,1,0:T(8,128)(2,1)S(1)} %pad_maximum_fusion.g0) | copy-start | bytes 2359300
  142.6 18.9 %collective-permute-start.29 = (bf16[4,2,192,256]{3,2,1,0:T(8,128)(2,1)S(1)}, bf16[4,2,192,256]{3,2,1,0:T(8,128)(2,1)S(1)}, u32[]{:S(2)}, u32[]{:S(2)}) collective-permute-start(bf16[4,2,192,256]{3,2,1,0:T(8,128)(2,1)S(1)} %pad_maximum_fusion.g0), channel_id=1, source_target_pairs={{0,1},{1,0},{2,3},{3,2},{4,5},{5,4},{6,7},{7,6},{8,9},{9,8},{10,11... | collective-permute-start | bytes 2359304 | tf_op jit(solution)/shard_map/keys_y/ppermute | solution.py:36
  144.2 10.0 %collective-permute-start.22 = (bf16[192,256]{1,0:T(8,128)(2,1)S(1)}, bf16[192,256]{1,0:T(8,128)(2,1)S(1)}, u32[]{:S(2)}, u32[]{:S(2)}) collective-permute-start(bf16[192,256]{1,0:T(8,128)(2,1)S(1)} %get-tuple-element.29), channel_id=1, source_target_pairs={{0,4},{1,5},{2,20},{3,21},{4,8},{5,9},{6,24},{7,25},{8,12},{9,13},... | collective-permute-start | bytes 294920 | tf_op jit(solution)/shard_map/queries_z/ppermute | solution.py:36
  146.3 34.3 %collective-permute-start.31 = (bf16[4,2,192,256]{3,2,1,0:T(8,128)(2,1)S(1)}, bf16[4,2,192,256]{3,2,1,0:T(8,128)(2,1)}, u32[]{:S(2)}, u32[]{:S(2)}) collective-permute-start(bf16[4,2,192,256]{3,2,1,0:T(8,128)(2,1)S(1)} %pad_maximum_fusion.g0), channel_id=1, source_target_pairs={{0,16},{1,17},{2,18},{3,19},{4,20},{5,21},{6,22},{7,23},{8,24},{9,... | collective-permute-start | bytes 2359304 | tf_op jit(solution)/shard_map/keys_core/ppermute | solution.py:36
  161.5 19.1 %copy-start.19 = (bf16[4,2,192,256]{3,2,1,0:T(8,128)(2,1)}, bf16[4,2,192,256]{3,2,1,0:T(8,128)(2,1)S(1)}, u32[]{:S(2)}) copy-start(bf16[4,2,192,256]{3,2,1,0:T(8,128)(2,1)S(1)} %collective-permute-done.29.g0) | copy-start | bytes 2359300
  161.5 27.7 %collective-permute-start.30 = (bf16[4,2,192,256]{3,2,1,0:T(8,128)(2,1)S(1)}, bf16[4,2,192,256]{3,2,1,0:T(8,128)(2,1)}, u32[]{:S(2)}, u32[]{:S(2)}) collective-permute-start(bf16[4,2,192,256]{3,2,1,0:T(8,128)(2,1)S(1)} %collective-permute-done.29.g0), channel_id=1, source_target_pairs={{0,16},{1,17},{2,18},{3,19},{4,20},{5,21},{6,22},{7,23},{8,24},{9,... | collective-permute-start | bytes 2359304 | tf_op jit(solution)/shard_map/keys_y_core/ppermute | solution.py:36
  161.6 51.1 %collective-permute-start.36 = (bf16[16,48,768]{2,1,0:T(8,128)(2,1)S(1)}, bf16[16,48,768]{2,1,0:T(8,128)(2,1)S(1)}, u32[]{:S(2)}, u32[]{:S(2)}) collective-permute-start(bf16[16,48,768]{2,1,0:T(8,128)(2,1)S(1)} %broadcast_add_fusion), channel_id=1, source_target_pairs={{0,16},{1,17},{2,18},{3,19},{4,20},{5,21},{6,22},{7,23},{8,24},{9,... | collective-permute-start | bytes 3538952 | tf_op jit(solution)/shard_map/out_core/ppermute | solution.py:36
  162.2 8.6 %collective-permute-start.25 = (bf16[192,256]{1,0:T(8,128)(2,1)S(1)}, bf16[192,256]{1,0:T(8,128)(2,1)S(1)}, u32[]{:S(2)}, u32[]{:S(2)}) collective-permute-start(bf16[192,256]{1,0:T(8,128)(2,1)S(1)} %get-tuple-element.30), channel_id=1, source_target_pairs={{0,8},{1,9},{2,24},{3,25},{4,12},{5,13},{6,28},{7,29},{8,0},{9,1},... | collective-permute-start | bytes 294920 | tf_op jit(solution)/shard_map/queries_z/ppermute | solution.py:36
  167.6 9.7 %collective-permute-start.24 = (bf16[192,256]{1,0:T(8,128)(2,1)S(1)}, bf16[192,256]{1,0:T(8,128)(2,1)S(1)}, u32[]{:S(2)}, u32[]{:S(2)}) collective-permute-start(bf16[192,256]{1,0:T(8,128)(2,1)S(1)} %get-tuple-element.31), channel_id=1, source_target_pairs={{0,0},{1,1},{2,16},{3,17},{4,4},{5,5},{6,20},{7,21},{8,8},{9,9},{1... | collective-permute-start | bytes 294920 | tf_op jit(solution)/shard_map/queries_z/ppermute | solution.py:36
  170.8 8.9 %collective-permute-start.23 = (bf16[192,256]{1,0:T(8,128)(2,1)S(1)}, bf16[192,256]{1,0:T(8,128)(2,1)S(1)}, u32[]{:S(2)}, u32[]{:S(2)}) collective-permute-start(bf16[192,256]{1,0:T(8,128)(2,1)S(1)} %get-tuple-element.32), channel_id=1, source_target_pairs={{0,12},{1,13},{2,28},{3,29},{4,0},{5,1},{6,16},{7,17},{8,4},{9,5},... | collective-permute-start | bytes 294920 | tf_op jit(solution)/shard_map/queries_z/ppermute | solution.py:36
  199.8 12.9 %collective-permute-start.32 = (bf16[192,256]{1,0:T(8,128)(2,1)S(1)}, bf16[192,256]{1,0:T(8,128)(2,1)S(1)}, u32[]{:S(2)}, u32[]{:S(2)}) collective-permute-start(bf16[192,256]{1,0:T(8,128)(2,1)S(1)} %get-tuple-element.28), channel_id=1, source_target_pairs={{0,4},{1,5},{2,8},{3,9},{4,16},{5,17},{6,20},{7,21},{8,12},{9,13},... | collective-permute-start | bytes 294920 | tf_op jit(solution)/shard_map/heads_back/ppermute | solution.py:36
  203.9 8.8 %collective-permute-start.33 = (bf16[192,256]{1,0:T(8,128)(2,1)S(1)}, bf16[192,256]{1,0:T(8,128)(2,1)S(1)}, u32[]{:S(2)}, u32[]{:S(2)}) collective-permute-start(bf16[192,256]{1,0:T(8,128)(2,1)S(1)} %get-tuple-element.27), channel_id=1, source_target_pairs={{0,12},{1,13},{2,0},{3,1},{4,28},{5,29},{6,24},{7,25},{8,4},{9,5},... | collective-permute-start | bytes 294920 | tf_op jit(solution)/shard_map/heads_back/ppermute | solution.py:36
  207.0 5.8 %collective-permute-start.34 = (bf16[192,256]{1,0:T(8,128)(2,1)S(1)}, bf16[192,256]{1,0:T(8,128)(2,1)S(1)}, u32[]{:S(2)}, u32[]{:S(2)}) collective-permute-start(bf16[192,256]{1,0:T(8,128)(2,1)S(1)} %get-tuple-element.26), channel_id=1, source_target_pairs={{0,0},{1,1},{2,12},{3,13},{4,24},{5,25},{6,28},{7,29},{8,8},{9,9},... | collective-permute-start | bytes 294920 | tf_op jit(solution)/shard_map/heads_back/ppermute | solution.py:36
  207.6 9.2 %collective-permute-start.35 = (bf16[192,256]{1,0:T(8,128)(2,1)S(1)}, bf16[192,256]{1,0:T(8,128)(2,1)S(1)}, u32[]{:S(2)}, u32[]{:S(2)}) collective-permute-start(bf16[192,256]{1,0:T(8,128)(2,1)S(1)} %get-tuple-element.25), channel_id=1, source_target_pairs={{0,8},{1,9},{2,4},{3,5},{4,20},{5,21},{6,16},{7,17},{8,0},{9,1},{1... | collective-permute-start | bytes 294920 | tf_op jit(solution)/shard_map/heads_back/ppermute | solution.py:36
  (9 other events, 20.8 us)

commit v4 on v2

--- a/solution.py
+++ b/solution.py
@@ -377,7 +377,7 @@
         send(low[:2], second(1), "conv_far"),
         send(high_stack[2:], second(-1), "conv_far"),
     )
-    qkv_stack = stacked([after(pieces[0][5:], low, high_stack)] + [p[5:] for p in pieces[1:]])
+    qkv_stack = stacked([after(pieces[0][5:], high_stack)] + [p[5:] for p in pieces[1:]])
     qkv_near = [send(qkv_stack, second(step), "qkv_second") for step in (1, -1)]
     qkv_groups = (
         qkv_stack,
@@ -431,7 +431,8 @@
     far = send(keys, other_low, "keys_y")
     near = send(keys, other_core, "keys_core")
     query = after(query, keys)
-    queries = jnp.stack([send(query[m], to_head(m), "queries_z") for m in range(4)])
+    query = [send(query[m], to_head(m), "queries_z") for m in range(4)]
+    queries = jnp.stack(query)
 
     partial = call(
         attend_kernel,
@@ -451,7 +452,7 @@
     )
     base = call(base_kernel, [VMEM], shape(256, 1536), [], 1_000_000, tokens)
     other_last = send(after(last, queries), other_core, "out_core")
-    far_near = send(after(far, partial[0]), other_core, "keys_y_core")
+    far_near = send(after(far, *query), other_core, "keys_y_core")
     heads = call(
         finish_kernel,
         [SMEM, SMEM] + [VMEM] * 6,

time: 213 us -> 208 us (0.977)
  waiting for transfers between devices: 63.1 us -> 40.5 us
  starting transfers between devices: 53.4 us -> 66.8 us
    ppermute x31, waiting for transfers between devices: 59 us -> 39.2 us  [send(): return lax.ppermute(value, AXES, pairs)]
    ppermute x31, starting transfers between devices: 48.7 us -> 60.9 us  [send(): return lax.ppermute(value, AXES, pairs)]
    ppermute x1, waiting for transfers between devices: 4.1 us -> 0.01 us  [shards(): behind = lax.ppermute(activated[:2], AXES, backward)]
    dynamic_update_slice x6, local copies, waits for them, and re-layouts: 2.22 us -> 4.92 us  [stacked(): lax.dynamic_update_slice(out, blocks[at][None], (at,) + (0,) * blocks[at]...]
    unnamed x50 -> x46, local copies, waits for them, and re-layouts: 4.27 us -> 4.06 us
    slice x7 -> x9, local copies, waits for them, and re-layouts: 5.23 us -> 5.42 us  [after(): zero = sum((o[(0,) * o.ndim].astype(F32) * 0.0 for o in others), F32(0.0))]
  transfers between devices with their start and end apart: 33 -> 33, of which waited for: 16 -> 9; matrix products, arithmetic and copies ran while one was open for 9% -> 11% of each run, Pallas kernels for 23% -> 23%
where the time goes in v4:
time: 208 us; the launch traced here: 207 us
  starting transfers between devices  66.8 us (32%)
  Pallas kernels  60.9 us (29%)
  waiting for transfers between devices  40.5 us (19%)
  local copies, waits for them, and re-layouts  29 us (14%)
  between operations  6.37 us (3%)
  other arithmetic  3.97 us (2%)
    ppermute x31, starting transfers between devices, send(): return lax.ppermute(value, AXES, pairs)  60.9 us
    pallas_call x8, Pallas kernels, call(): pl.pallas_call(kernel, out_shape=outs, in_specs=ins, out_specs=jax.tree.m...  60.9 us
    ppermute x31, waiting for transfers between devices, send(): return lax.ppermute(value, AXES, pairs)  39.2 us
    slice x9, local copies, waits for them, and re-layouts, after(): zero = sum((o[(0,) * o.ndim].astype(F32) * 0.0 for o in others), F32(0.0))  5.42 us
    dynamic_update_slice x6, local copies, waits for them, and re-layouts, stacked(): lax.dynamic_update_slice(out, blocks[at][None], (at,) + (0,) * blocks[at]...  4.92 us
    ppermute x1, starting transfers between devices, shards(): before = lax.ppermute(activated[-2:], AXES, forward)  4.55 us
  transfers between devices with their start and end apart: 33, of which 9 were waited for; matrix products, arithmetic and copies ran while one was open for 11% of the time, Pallas kernels for 23%

profile of v4, /device:TPU:6, one launch (start us, length us, event | category | flops | bytes accessed | tf_op | source)
XLA Modules:
  0.0 207.4 jit_solution(11121370362145508900)
XLA Ops:
  0.0 1.1 dynamic-slice_bitcast_fusion.1
  1.4 6.5 %collective-permute-start.3 = (bf16[9,48,768]{2,1,0:T(8,128)(2,1)S(1)}, bf16[9,48,768]{2,1,0:T(8,128)(2,1)S(1)}, u32[]{:S(2)}, u32[]{:S(2)}) collective-permute-start(bf16[9,48,768]{2,1,0:T(8,128)(2,1)S(1)} %pad_maximum_fusion.1), channel_id=1, source_target_pairs={{0,4},{1,5},{2,2},{3,3},{4,6},{5,7},{6,0},{7,1},{8,18},{9,19},{10,... | collective-permute-start | bytes 1990664 | tf_op jit(solution)/shard_map/weights_z/ppermute | solution.py:36
  9.7 1.3 collective-permute-start.1
  11.0 4.5 %collective-permute-start = (bf16[2,768]{1,0:T(2,128)(2,1)S(1)}, bf16[2,768]{1,0:T(2,128)(2,1)S(1)}, u32[]{:S(2)}, u32[]{:S(2)}) collective-permute-start(bf16[2,768]{1,0:T(2,128)(2,1)S(1)} %get-tuple-element.23), channel_id=1, source_target_pairs={{0,1},{1,2},{2,3},{3,4},{4,5},{5,6},{6,7},{7,8},{8,9},{9,10},{10,1... | collective-permute-start | bytes 9224 | tf_op jit(solution)/shard_map/ppermute | solution.py:360
  15.7 1.2 collective-permute-done
  17.2 1.2 collective-permute-start.2
  18.4 4.5 %collective-permute-done.3 = bf16[9,48,768]{2,1,0:T(8,128)(2,1)S(1)} collective-permute-done((bf16[9,48,768]{2,1,0:T(8,128)(2,1)S(1)}, bf16[9,48,768]{2,1,0:T(8,128)(2,1)S(1)}, u32[]{:S(2)}, u32[]{:S(2)}) %collective-permute-start.3) | collective-permute-done | bytes 663584 | tf_op jit(solution)/shard_map/weights_z/ppermute | solution.py:36
  22.8 2.9 %collective-permute-start.5 = (bf16[9,48,768]{2,1,0:T(8,128)(2,1)S(1)}, bf16[9,48,768]{2,1,0:T(8,128)(2,1)S(1)}, u32[]{:S(2)}, u32[]{:S(2)}) collective-permute-start(bf16[9,48,768]{2,1,0:T(8,128)(2,1)S(1)} %collective-permute-done.3), channel_id=1, source_target_pairs={{0,192},{1,193},{2,194},{3,195},{4,196},{5,197},{6,198},{7,199},{8... | collective-permute-start | bytes 1990664 | tf_op jit(solution)/shard_map/weights_first/ppermute | solution.py:36
  27.0 10.1 %acts_kernel.1.refs_1_ = bf16[6,768,512]{2,1,0:T(8,128)(2,1)} custom-call(bf16[528,768]{1,0:T(8,128)(2,1)} %copy-done.3, bf16[528,768]{1,0:T(8,128)(2,1)} %copy-done.6), custom_call_target="tpu_custom_call" | custom-call | flops 1000000000 | bytes 8000000 | tf_op jit(solution)/shard_map/acts_kernel/pallas_call | solution.py:329
  37.1 1.2 slice.157
  39.0 1.0 slice_bitcast_fusion.2
  40.0 1.3 dynamic_update_slice.24
  42.6 1.8 fusion.8
  45.2 6.1 %collective-permute-start.8 = (bf16[4,5,48,768]{3,2,1,0:T(8,128)(2,1)}, bf16[4,5,48,768]{3,2,1,0:T(8,128)(2,1)S(1)}, u32[]{:S(2)}, u32[]{:S(2)}) collective-permute-start(bf16[4,5,48,768]{3,2,1,0:T(8,128)(2,1)} %fusion.7.refs_3_), channel_id=1, source_target_pairs={{0,33},{1,0},{2,35},{3,2},{4,37},{5,4},{6,39},{7,6},{8,41},{9,8},{... | collective-permute-start | bytes 4423688 | tf_op jit(solution)/shard_map/conv_second/ppermute | solution.py:36
  53.5 15.1 %collective-permute-done.8.refs_5_ = bf16[4,5,48,768]{3,2,1,0:T(8,128)(2,1)S(1)} collective-permute-done((bf16[4,5,48,768]{3,2,1,0:T(8,128)(2,1)}, bf16[4,5,48,768]{3,2,1,0:T(8,128)(2,1)S(1)}, u32[]{:S(2)}, u32[]{:S(2)}) %collective-permute-start.8) | collective-permute-done | bytes 1474592 | tf_op jit(solution)/shard_map/conv_second/ppermute | solution.py:36
  70.4 3.2 %collective-permute-start.14 = (bf16[4,4,48,768]{3,2,1,0:T(8,128)(2,1)S(1)}, bf16[4,4,48,768]{3,2,1,0:T(8,128)(2,1)}, u32[]{:S(2)}, u32[]{:S(2)}) collective-permute-start(bf16[4,4,48,768]{3,2,1,0:T(8,128)(2,1)S(1)} %fusion.11.g0), channel_id=1, source_target_pairs={{0,33},{1,0},{2,35},{3,2},{4,37},{5,4},{6,39},{7,6},{8,41},{9,8},{... | collective-permute-start | bytes 3538952 | tf_op jit(solution)/shard_map/qkv_second/ppermute | solution.py:36
  73.7 1.0 reshape.44.refs_2_
  74.7 2.1 %slice.158 = bf16[2,5,48,768]{3,2,1,0:T(8,128)(2,1)} slice(bf16[4,5,48,768]{3,2,1,0:T(8,128)(2,1)} %collective-permute-done.7.refs_4_), slice={[0:2], [0:5], [0:48], [0:768]} | slice | bytes 1474560 | tf_op jit(solution)/shard_map/slice | solution.py:377
  77.8 3.2 %collective-permute-start.10 = (bf16[2,5,48,768]{3,2,1,0:T(8,128)(2,1)}, bf16[2,5,48,768]{3,2,1,0:T(8,128)(2,1)}, u32[]{:S(2)}, u32[]{:S(2)}) collective-permute-start(bf16[2,5,48,768]{3,2,1,0:T(8,128)(2,1)} %slice.159), channel_id=1, source_target_pairs={{0,33},{1,0},{2,35},{3,2},{4,37},{5,4},{6,39},{7,6},{8,41},{9,8},{... | collective-permute-start | bytes 2211848 | tf_op jit(solution)/shard_map/conv_far/ppermute | solution.py:36
  81.0 1.2 fusion.14.refs_0_.table
  82.2 11.0 %conv_kernel.2.refs_3_.ma = bf16[12,48,512]{2,1,0:T(8,128)(2,1)} custom-call(s32[50]{0:T(128)} %fusion.14.refs_0_.table, bf16[6,768,512]{2,1,0:T(8,128)(2,1)} %acts_kernel.1.refs_1_, f32[16,48,1]{2,1,0:T(8,128)} %reshape.44.refs_2_, bf16[4,5,48,768]{3,2,1,0:T(8,128)(2,1)} %fusion.7.refs_3_, bf16[4,5,48,768]{3,2,1,0:T(8,128)(2,1)} %collective-permute-done.7.refs_4_, ...), custom_call_target="tpu_custom_call" | custom-call | flops 4499999744 | bytes 8000000 | tf_op jit(solution)/shard_map/conv_kernel/pallas_call | solution.py:329
  94.4 1.1 slice.166
  95.5 3.3 %collective-permute-start.16 = (bf16[2,4,48,768]{3,2,1,0:T(8,128)(2,1)S(1)}, bf16[2,4,48,768]{3,2,1,0:T(8,128)(2,1)S(1)}, u32[]{:S(2)}, u32[]{:S(2)}) collective-permute-start(bf16[2,4,48,768]{3,2,1,0:T(8,128)(2,1)S(1)} %slice.166), channel_id=1, source_target_pairs={{0,33},{1,0},{2,35},{3,2},{4,37},{5,4},{6,39},{7,6},{8,41},{9,8},{... | collective-permute-start | bytes 1769480 | tf_op jit(solution)/shard_map/qkv_far/ppermute | solution.py:36
  98.8 6.6 %conv_kernel.3.mb = bf16[4,48,512]{2,1,0:T(8,128)(2,1)} custom-call(s32[50]{0:T(128)} %fusion.14.refs_0_.table, bf16[6,768,512]{2,1,0:T(8,128)(2,1)} %acts_kernel.1.refs_1_, f32[16,48,1]{2,1,0:T(8,128)} %reshape.44.refs_2_, bf16[12,48,512]{2,1,0:T(8,128)(2,1)} %conv_kernel.2.refs_3_.ma, bf16[2,5,48,768]{3,2,1,0:T(8,128)(2,1)} %collective-permute-done.9.refs_4_, ...), custom_call_target="tpu_custom_call" | custom-call | flops 1500000000 | bytes 8000000 | tf_op jit(solution)/shard_map/conv_kernel/pallas_call | solution.py:329
  105.5 1.5 reshape.45.gain
  108.6 8.8 %project_kernel.1 = (bf16[4,2,192,256]{3,2,1,0:T(8,128)(2,1)}, bf16[4,192,256]{2,1,0:T(8,128)(2,1)}, bf16[16,48,768]{2,1,0:T(8,128)(2,1)}, bf16[2,16,48,512]{3,2,1,0:T(8,128)(2,1)}) custom-call(s32[50]{0:T(128)} %fusion.14.refs_0_.table, bf16[12,48,512]{2,1,0:T(8,128)(2,1)} %conv_kernel.2.refs_3_.ma, bf16[4,48,512]{2,1,0:T(8,128)(2,1)} %conv_kernel.3.mb, ...), custom_call_target="tpu_custom_call" | custom-call | flops 1800000000 | bytes 8000000 | tf_op jit(solution)/shard_map/project_kernel/pallas_call | solution.py:329
  117.4 1.3 slice_bitcast_fusion.8
  118.7 2.5 %collective-permute-start.17 = (bf16[2,192,256]{2,1,0:T(8,128)(2,1)S(1)}, bf16[2,192,256]{2,1,0:T(8,128)(2,1)S(1)}, u32[]{:S(2)}, u32[]{:S(2)}) collective-permute-start(bf16[2,192,256]{2,1,0:T(8,128)(2,1)S(1)} %get-tuple-element.22), channel_id=1, source_target_pairs={{0,4},{1,5},{2,20},{3,21},{4,8},{5,9},{6,24},{7,25},{8,12},{9,13},... | collective-permute-start | bytes 589832 | tf_op jit(solution)/shard_map/keys_z/ppermute | solution.py:36
  121.2 3.5 %collective-permute-start.24 = (bf16[2,192,256]{2,1,0:T(8,128)(2,1)S(1)}, bf16[2,192,256]{2,1,0:T(8,128)(2,1)S(1)}, u32[]{:S(2)}, u32[]{:S(2)}) collective-permute-start(bf16[2,192,256]{2,1,0:T(8,128)(2,1)S(1)} %get-tuple-element.20), channel_id=1, source_target_pairs={{0,8},{1,9},{2,24},{3,25},{4,12},{5,13},{6,28},{7,29},{8,0},{9,1},... | collective-permute-start | bytes 589832 | tf_op jit(solution)/shard_map/keys_z/ppermute | solution.py:36
  125.3 4.0 %collective-permute-start.22 = (bf16[2,192,256]{2,1,0:T(8,128)(2,1)S(1)}, bf16[2,192,256]{2,1,0:T(8,128)(2,1)S(1)}, u32[]{:S(2)}, u32[]{:S(2)}) collective-permute-start(bf16[2,192,256]{2,1,0:T(8,128)(2,1)S(1)} %get-tuple-element.19), channel_id=1, source_target_pairs={{0,12},{1,13},{2,28},{3,29},{4,0},{5,1},{6,16},{7,17},{8,4},{9,5},... | collective-permute-start | bytes 589832 | tf_op jit(solution)/shard_map/keys_z/ppermute | solution.py:36
  129.4 8.5 %collective-permute-done.24 = bf16[2,192,256]{2,1,0:T(8,128)(2,1)S(1)} collective-permute-done((bf16[2,192,256]{2,1,0:T(8,128)(2,1)S(1)}, bf16[2,192,256]{2,1,0:T(8,128)(2,1)S(1)}, u32[]{:S(2)}, u32[]{:S(2)}) %collective-permute-start.24) | collective-permute-done | bytes 196640 | tf_op jit(solution)/shard_map/keys_z/ppermute | solution.py:36
  137.9 3.1 %collective-permute-done.22 = bf16[2,192,256]{2,1,0:T(8,128)(2,1)S(1)} collective-permute-done((bf16[2,192,256]{2,1,0:T(8,128)(2,1)S(1)}, bf16[2,192,256]{2,1,0:T(8,128)(2,1)S(1)}, u32[]{:S(2)}, u32[]{:S(2)}) %collective-permute-start.22) | collective-permute-done | bytes 196640 | tf_op jit(solution)/shard_map/keys_z/ppermute | solution.py:36
  142.5 2.2 %collective-permute-start.18 = (bf16[192,256]{1,0:T(8,128)(2,1)S(1)}, bf16[192,256]{1,0:T(8,128)(2,1)S(1)}, u32[]{:S(2)}, u32[]{:S(2)}) collective-permute-start(bf16[192,256]{1,0:T(8,128)(2,1)S(1)} %get-tuple-element.29), channel_id=1, source_target_pairs={{0,4},{1,5},{2,20},{3,21},{4,8},{5,9},{6,24},{7,25},{8,12},{9,13},... | collective-permute-start | bytes 294920 | tf_op jit(solution)/shard_map/queries_z/ppermute | solution.py:36
  144.8 2.9 %collective-permute-start.19 = (bf16[192,256]{1,0:T(8,128)(2,1)S(1)}, bf16[192,256]{1,0:T(8,128)(2,1)S(1)}, u32[]{:S(2)}, u32[]{:S(2)}) collective-permute-start(bf16[192,256]{1,0:T(8,128)(2,1)S(1)} %get-tuple-element.32), channel_id=1, source_target_pairs={{0,12},{1,13},{2,28},{3,29},{4,0},{5,1},{6,16},{7,17},{8,4},{9,5},... | collective-permute-start | bytes 294920 | tf_op jit(solution)/shard_map/queries_z/ppermute | solution.py:36
  148.4 3.6 %collective-permute-start.21 = (bf16[192,256]{1,0:T(8,128)(2,1)S(1)}, bf16[192,256]{1,0:T(8,128)(2,1)S(1)}, u32[]{:S(2)}, u32[]{:S(2)}) collective-permute-start(bf16[192,256]{1,0:T(8,128)(2,1)S(1)} %get-tuple-element.30), channel_id=1, source_target_pairs={{0,8},{1,9},{2,24},{3,25},{4,12},{5,13},{6,28},{7,29},{8,0},{9,1},... | collective-permute-start | bytes 294920 | tf_op jit(solution)/shard_map/queries_z/ppermute | solution.py:36
  151.9 1.2 collective-permute-done.18
  153.1 2.6 %collective-permute-start.27 = (bf16[4,2,192,256]{3,2,1,0:T(8,128)(2,1)S(1)}, bf16[4,2,192,256]{3,2,1,0:T(8,128)(2,1)S(1)}, u32[]{:S(2)}, u32[]{:S(2)}) collective-permute-start(bf16[4,2,192,256]{3,2,1,0:T(8,128)(2,1)S(1)} %pad_maximum_fusion.g0), channel_id=1, source_target_pairs={{0,16},{1,17},{2,18},{3,19},{4,20},{5,21},{6,22},{7,23},{8,24},{9,... | collective-permute-start | bytes 2359304 | tf_op jit(solution)/shard_map/keys_core/ppermute | solution.py:36
  161.5 1.1 broadcast_add_fusion.1
  162.6 1.0 collective-permute-start.26
  165.5 8.7 %attend_kernel.1 = (f32[4,256,128]{2,1,0:T(8,128)}, f32[4,256,128]{2,1,0:T(8,128)}, f32[4,256,192]{2,1,0:T(8,128)}) custom-call(s32[50]{0:T(128)} %fusion.14.refs_0_.table, f32[4]{0:T(128)} %factor.3, bf16[4,192,256]{2,1,0:T(8,128)(2,1)} %pad_maximum_fusion.2.queries, bf16[4,2,192,256]{3,2,1,0:T(8,128)(2,1)} %copy-done.9, bf16[4,2,192,256]{3,2,1,0:T(8,128)(2,1)} %copy-done.22), custom_call_target="tpu_custom_call" | custom-call | flops 1600000000 | bytes 8000000 | tf_op jit(solution)/shard_map/attend_kernel/pallas_call | solution.py:329
  174.2 9.4 %finish_kernel.1 = bf16[4,192,256]{2,1,0:T(8,128)(2,1)} custom-call(s32[50]{0:T(128)} %fusion.14.refs_0_.table, f32[4]{0:T(128)} %factor.3, bf16[4,192,256]{2,1,0:T(8,128)(2,1)} %pad_maximum_fusion.2.queries, bf16[4,2,192,256]{3,2,1,0:T(8,128)(2,1)} %copy-done.8, bf16[4,2,192,256]{3,2,1,0:T(8,128)(2,1)} %collective-permute-done.26.g1, ...), custom_call_target="tpu_custom_call" | custom-call | flops 1600000000 | bytes 8000000 | tf_op jit(solution)/shard_map/finish_kernel/pallas_call | solution.py:329
  183.6 1.1 slice_bitcast_fusion.10
  184.7 1.1 collective-permute-start.28
  185.7 5.4 %collective-permute-start.29 = (bf16[192,256]{1,0:T(8,128)(2,1)S(1)}, bf16[192,256]{1,0:T(8,128)(2,1)S(1)}, u32[]{:S(2)}, u32[]{:S(2)}) collective-permute-start(bf16[192,256]{1,0:T(8,128)(2,1)S(1)} %get-tuple-element.27), channel_id=1, source_target_pairs={{0,12},{1,13},{2,0},{3,1},{4,28},{5,29},{6,24},{7,25},{8,4},{9,5},... | collective-permute-start | bytes 294920 | tf_op jit(solution)/shard_map/heads_back/ppermute | solution.py:36
  191.9 2.3 %collective-permute-start.31 = (bf16[192,256]{1,0:T(8,128)(2,1)S(1)}, bf16[192,256]{1,0:T(8,128)(2,1)S(1)}, u32[]{:S(2)}, u32[]{:S(2)}) collective-permute-start(bf16[192,256]{1,0:T(8,128)(2,1)S(1)} %get-tuple-element.25), channel_id=1, source_target_pairs={{0,8},{1,9},{2,4},{3,5},{4,20},{5,21},{6,16},{7,17},{8,0},{9,1},{1... | collective-permute-start | bytes 294920 | tf_op jit(solution)/shard_map/heads_back/ppermute | solution.py:36
  194.2 2.5 %base_kernel.1.base = bf16[256,1536]{1,0:T(8,128)(2,1)} custom-call(bf16[2,16,48,512]{3,2,1,0:T(8,128)(2,1)} %get-tuple-element.17.tokens), custom_call_target="tpu_custom_call" | custom-call | flops 1000000 | bytes 8000000 | tf_op jit(solution)/shard_map/base_kernel/pallas_call | solution.py:329
  196.8 6.2 %collective-permute-done.31.h3 = bf16[192,256]{1,0:T(8,128)(2,1)S(1)} collective-permute-done((bf16[192,256]{1,0:T(8,128)(2,1)S(1)}, bf16[192,256]{1,0:T(8,128)(2,1)S(1)}, u32[]{:S(2)}, u32[]{:S(2)}) %collective-permute-start.31) | collective-permute-done | bytes 98336 | tf_op jit(solution)/shard_map/heads_back/ppermute | solution.py:36
  203.7 3.8 %out_kernel.1 = bf16[256,1536]{1,0:T(8,128)(2,1)} custom-call(s32[50]{0:T(128)} %fusion.14.refs_0_.table, bf16[192,256]{1,0:T(8,128)(2,1)} %copy-done.15, bf16[192,256]{1,0:T(8,128)(2,1)} %copy-done.16, bf16[192,256]{1,0:T(8,128)(2,1)} %copy-done.17, bf16[192,256]{1,0:T(8,128)(2,1)} %copy-done.18, bf16[256,1536]{1,0:T(8,128)(2,1)} %base_kernel.1.base, ...), custom_call_target="tpu_custom_call" | custom-call | flops 600000000 | bytes 8000000 | tf_op jit(solution)/shard_map/out_kernel/pallas_call | solution.py:329
  (118 shorter events, 20.2 us)
Async XLA Ops:
  0.0 9.1 %copy-start.7 = (bf16[512,768]{1,0:T(8,128)(2,1)S(1)}, bf16[512,768]{1,0:T(8,128)(2,1)}, u32[]{:S(2)}) copy-start(bf16[512,768]{1,0:T(8,128)(2,1)} %param.8) | copy-start | bytes 2359300
  1.4 21.4 %collective-permute-start.3 = (bf16[9,48,768]{2,1,0:T(8,128)(2,1)S(1)}, bf16[9,48,768]{2,1,0:T(8,128)(2,1)S(1)}, u32[]{:S(2)}, u32[]{:S(2)}) collective-permute-start(bf16[9,48,768]{2,1,0:T(8,128)(2,1)S(1)} %pad_maximum_fusion.1), channel_id=1, source_target_pairs={{0,4},{1,5},{2,2},{3,3},{4,6},{5,7},{6,0},{7,1},{8,18},{9,19},{10,... | collective-permute-start | bytes 1990664 | tf_op jit(solution)/shard_map/weights_z/ppermute | solution.py:36
  9.7 5.9 %collective-permute-start.1 = (bf16[2,768]{1,0:T(2,128)(2,1)S(1)}, bf16[2,768]{1,0:T(2,128)(2,1)S(1)}, u32[]{:S(2)}, u32[]{:S(2)}) collective-permute-start(bf16[2,768]{1,0:T(2,128)(2,1)S(1)} %get-tuple-element.24), channel_id=1, source_target_pairs={{1,0},{2,1},{3,2},{4,3},{5,4},{6,5},{7,6},{8,7},{9,8},{10,9},{11,1... | collective-permute-start | bytes 9224 | tf_op jit(solution)/shard_map/ppermute | solution.py:361
  11.0 5.9 %collective-permute-start = (bf16[2,768]{1,0:T(2,128)(2,1)S(1)}, bf16[2,768]{1,0:T(2,128)(2,1)S(1)}, u32[]{:S(2)}, u32[]{:S(2)}) collective-permute-start(bf16[2,768]{1,0:T(2,128)(2,1)S(1)} %get-tuple-element.23), channel_id=1, source_target_pairs={{0,1},{1,2},{2,3},{3,4},{4,5},{5,6},{6,7},{7,8},{8,9},{9,10},{10,1... | collective-permute-start | bytes 9224 | tf_op jit(solution)/shard_map/ppermute | solution.py:360
  17.2 8.9 %copy-start.3 = (bf16[528,768]{1,0:T(8,128)(2,1)}, bf16[528,768]{1,0:T(8,128)(2,1)S(1)}, u32[]{:S(2)}) copy-start(bf16[528,768]{1,0:T(8,128)(2,1)S(1)} %maximum_maximum_fusion.own) | copy-start | bytes 2433028
  17.2 8.9 %collective-permute-start.2 = (bf16[528,768]{1,0:T(8,128)(2,1)S(1)}, bf16[528,768]{1,0:T(8,128)(2,1)S(1)}, u32[]{:S(2)}, u32[]{:S(2)}) collective-permute-start(bf16[528,768]{1,0:T(8,128)(2,1)S(1)} %maximum_maximum_fusion.own), channel_id=1, source_target_pairs={{0,16},{1,17},{2,18},{3,19},{4,20},{5,21},{6,22},{7,23},{8,24},{9,... | collective-permute-start | bytes 2433032 | tf_op jit(solution)/shard_map/acts_core/ppermute | solution.py:36
  22.8 16.1 %collective-permute-start.4 = (bf16[9,48,768]{2,1,0:T(8,128)(2,1)S(1)}, bf16[9,48,768]{2,1,0:T(8,128)(2,1)}, u32[]{:S(2)}, u32[]{:S(2)}) collective-permute-start(bf16[9,48,768]{2,1,0:T(8,128)(2,1)S(1)} %collective-permute-done.3), channel_id=1, source_target_pairs={{0,128},{1,129},{2,130},{3,131},{4,132},{5,133},{6,134},{7,135},{8... | collective-permute-start | bytes 1990664 | tf_op jit(solution)/shard_map/weights_first/ppermute | solution.py:36
  22.8 19.0 %collective-permute-start.5 = (bf16[9,48,768]{2,1,0:T(8,128)(2,1)S(1)}, bf16[9,48,768]{2,1,0:T(8,128)(2,1)S(1)}, u32[]{:S(2)}, u32[]{:S(2)}) collective-permute-start(bf16[9,48,768]{2,1,0:T(8,128)(2,1)S(1)} %collective-permute-done.3), channel_id=1, source_target_pairs={{0,192},{1,193},{2,194},{3,195},{4,196},{5,197},{6,198},{7,199},{8... | collective-permute-start | bytes 1990664 | tf_op jit(solution)/shard_map/weights_first/ppermute | solution.py:36
  25.7 16.9 %collective-permute-start.6 = (bf16[9,48,768]{2,1,0:T(8,128)(2,1)S(1)}, bf16[9,48,768]{2,1,0:T(8,128)(2,1)}, u32[]{:S(2)}, u32[]{:S(2)}) collective-permute-start(bf16[9,48,768]{2,1,0:T(8,128)(2,1)S(1)} %collective-permute-done.3), channel_id=1, source_target_pairs={{0,64},{1,65},{2,66},{3,67},{4,68},{5,69},{6,70},{7,71},{8,72},{9,... | collective-permute-start | bytes 1990664 | tf_op jit(solution)/shard_map/weights_first/ppermute | solution.py:36
  45.2 23.3 %collective-permute-start.8 = (bf16[4,5,48,768]{3,2,1,0:T(8,128)(2,1)}, bf16[4,5,48,768]{3,2,1,0:T(8,128)(2,1)S(1)}, u32[]{:S(2)}, u32[]{:S(2)}) collective-permute-start(bf16[4,5,48,768]{3,2,1,0:T(8,128)(2,1)} %fusion.7.refs_3_), channel_id=1, source_target_pairs={{0,33},{1,0},{2,35},{3,2},{4,37},{5,4},{6,39},{7,6},{8,41},{9,8},{... | collective-permute-start | bytes 4423688 | tf_op jit(solution)/shard_map/conv_second/ppermute | solution.py:36
  51.4 23.3 %collective-permute-start.7 = (bf16[4,5,48,768]{3,2,1,0:T(8,128)(2,1)}, bf16[4,5,48,768]{3,2,1,0:T(8,128)(2,1)}, u32[]{:S(2)}, u32[]{:S(2)}) collective-permute-start(bf16[4,5,48,768]{3,2,1,0:T(8,128)(2,1)} %fusion.7.refs_3_), channel_id=1, source_target_pairs={{0,1},{1,32},{2,3},{3,34},{4,5},{5,36},{6,7},{7,38},{8,9},{9,40},{... | collective-permute-start | bytes 4423688 | tf_op jit(solution)/shard_map/conv_second/ppermute | solution.py:36
  52.3 21.2 %copy-start.21 = (f32[1536]{0:T(1024)S(1)}, f32[1536]{0:T(1024)}, u32[]{:S(2)}) copy-start(f32[1536]{0:T(1024)} %param.10) | copy-start | bytes 18436
  69.8 8.0 %copy-start.2 = (bf16[4,4,48,768]{3,2,1,0:T(8,128)(2,1)}, bf16[4,4,48,768]{3,2,1,0:T(8,128)(2,1)S(1)}, u32[]{:S(2)}) copy-start(bf16[4,4,48,768]{3,2,1,0:T(8,128)(2,1)S(1)} %fusion.11.g0) | copy-start | bytes 3538948
  69.8 23.5 %collective-permute-start.13 = (bf16[4,4,48,768]{3,2,1,0:T(8,128)(2,1)S(1)}, bf16[4,4,48,768]{3,2,1,0:T(8,128)(2,1)S(1)}, u32[]{:S(2)}, u32[]{:S(2)}) collective-permute-start(bf16[4,4,48,768]{3,2,1,0:T(8,128)(2,1)S(1)} %fusion.11.g0), channel_id=1, source_target_pairs={{0,1},{1,32},{2,3},{3,34},{4,5},{5,36},{6,7},{7,38},{8,9},{9,40},{... | collective-permute-start | bytes 3538952 | tf_op jit(solution)/shard_map/qkv_second/ppermute | solution.py:36
  70.4 24.0 %collective-permute-start.14 = (bf16[4,4,48,768]{3,2,1,0:T(8,128)(2,1)S(1)}, bf16[4,4,48,768]{3,2,1,0:T(8,128)(2,1)}, u32[]{:S(2)}, u32[]{:S(2)}) collective-permute-start(bf16[4,4,48,768]{3,2,1,0:T(8,128)(2,1)S(1)} %fusion.11.g0), channel_id=1, source_target_pairs={{0,33},{1,0},{2,35},{3,2},{4,37},{5,4},{6,39},{7,6},{8,41},{9,8},{... | collective-permute-start | bytes 3538952 | tf_op jit(solution)/shard_map/qkv_second/ppermute | solution.py:36
  74.7 2.1 %copy-start.13 = (bf16[4,5,48,768]{3,2,1,0:T(8,128)(2,1)S(1)}, bf16[4,5,48,768]{3,2,1,0:T(8,128)(2,1)}, u32[]{:S(2)}) copy-start(bf16[4,5,48,768]{3,2,1,0:T(8,128)(2,1)} %copy-done.12) | copy-start | bytes 4423684
  76.8 22.0 %collective-permute-start.9 = (bf16[2,5,48,768]{3,2,1,0:T(8,128)(2,1)}, bf16[2,5,48,768]{3,2,1,0:T(8,128)(2,1)}, u32[]{:S(2)}, u32[]{:S(2)}) collective-permute-start(bf16[2,5,48,768]{3,2,1,0:T(8,128)(2,1)} %slice.158), channel_id=1, source_target_pairs={{0,1},{1,32},{2,3},{3,34},{4,5},{5,36},{6,7},{7,38},{8,9},{9,40},{... | collective-permute-start | bytes 2211848 | tf_op jit(solution)/shard_map/conv_far/ppermute | solution.py:36
  77.8 21.0 %collective-permute-start.10 = (bf16[2,5,48,768]{3,2,1,0:T(8,128)(2,1)}, bf16[2,5,48,768]{3,2,1,0:T(8,128)(2,1)}, u32[]{:S(2)}, u32[]{:S(2)}) collective-permute-start(bf16[2,5,48,768]{3,2,1,0:T(8,128)(2,1)} %slice.159), channel_id=1, source_target_pairs={{0,33},{1,0},{2,35},{3,2},{4,37},{5,4},{6,39},{7,6},{8,41},{9,8},{... | collective-permute-start | bytes 2211848 | tf_op jit(solution)/shard_map/conv_far/ppermute | solution.py:36
  93.3 13.7 %collective-permute-start.11 = (bf16[12,48,512]{2,1,0:T(8,128)(2,1)}, bf16[12,48,512]{2,1,0:T(8,128)(2,1)}, u32[]{:S(2)}, u32[]{:S(2)}) collective-permute-start(bf16[12,48,512]{2,1,0:T(8,128)(2,1)} %conv_kernel.2.refs_3_.ma), channel_id=1, source_target_pairs={{0,16},{1,17},{2,18},{3,19},{4,20},{5,21},{6,22},{7,23},{8,24},{9,... | collective-permute-start | bytes 1769480 | tf_op jit(solution)/shard_map/pooled_core/ppermute | solution.py:36
  93.4 12.0 %copy-start.4 = (bf16[4,4,48,768]{3,2,1,0:T(8,128)(2,1)}, bf16[4,4,48,768]{3,2,1,0:T(8,128)(2,1)S(1)}, u32[]{:S(2)}) copy-start(bf16[4,4,48,768]{3,2,1,0:T(8,128)(2,1)S(1)} %collective-permute-done.13.g1) | copy-start | bytes 3538948
  94.4 12.8 %collective-permute-start.15 = (bf16[2,4,48,768]{3,2,1,0:T(8,128)(2,1)}, bf16[2,4,48,768]{3,2,1,0:T(8,128)(2,1)}, u32[]{:S(2)}, u32[]{:S(2)}) collective-permute-start(bf16[2,4,48,768]{3,2,1,0:T(8,128)(2,1)} %slice.165), channel_id=1, source_target_pairs={{0,1},{1,32},{2,3},{3,34},{4,5},{5,36},{6,7},{7,38},{8,9},{9,40},{... | collective-permute-start | bytes 1769480 | tf_op jit(solution)/shard_map/qkv_far/ppermute | solution.py:36
  95.5 10.0 %copy-start.20 = (f32[1536]{0:T(1024)S(1)}, f32[1536]{0:T(1024)}, u32[]{:S(2)}) copy-start(f32[1536]{0:T(1024)} %param.11) | copy-start | bytes 18436
  95.5 11.6 %collective-permute-start.16 = (bf16[2,4,48,768]{3,2,1,0:T(8,128)(2,1)S(1)}, bf16[2,4,48,768]{3,2,1,0:T(8,128)(2,1)S(1)}, u32[]{:S(2)}, u32[]{:S(2)}) collective-permute-start(bf16[2,4,48,768]{3,2,1,0:T(8,128)(2,1)S(1)} %slice.166), channel_id=1, source_target_pairs={{0,33},{1,0},{2,35},{3,2},{4,37},{5,4},{6,39},{7,6},{8,41},{9,8},{... | collective-permute-start | bytes 1769480 | tf_op jit(solution)/shard_map/qkv_far/ppermute | solution.py:36
  105.4 1.7 collective-permute-start.12
  117.4 25.1 %copy-start.11 = (bf16[4,192,256]{2,1,0:T(8,128)(2,1)S(1)}, bf16[4,192,256]{2,1,0:T(8,128)(2,1)}, u32[]{:S(2)}) copy-start(bf16[4,192,256]{2,1,0:T(8,128)(2,1)} %get-tuple-element.12) | copy-start | bytes 1179652
  118.7 10.7 %collective-permute-start.17 = (bf16[2,192,256]{2,1,0:T(8,128)(2,1)S(1)}, bf16[2,192,256]{2,1,0:T(8,128)(2,1)S(1)}, u32[]{:S(2)}, u32[]{:S(2)}) collective-permute-start(bf16[2,192,256]{2,1,0:T(8,128)(2,1)S(1)} %get-tuple-element.22), channel_id=1, source_target_pairs={{0,4},{1,5},{2,20},{3,21},{4,8},{5,9},{6,24},{7,25},{8,12},{9,13},... | collective-permute-start | bytes 589832 | tf_op jit(solution)/shard_map/keys_z/ppermute | solution.py:36
  121.2 16.7 %collective-permute-start.24 = (bf16[2,192,256]{2,1,0:T(8,128)(2,1)S(1)}, bf16[2,192,256]{2,1,0:T(8,128)(2,1)S(1)}, u32[]{:S(2)}, u32[]{:S(2)}) collective-permute-start(bf16[2,192,256]{2,1,0:T(8,128)(2,1)S(1)} %get-tuple-element.20), channel_id=1, source_target_pairs={{0,8},{1,9},{2,24},{3,25},{4,12},{5,13},{6,28},{7,29},{8,0},{9,1},... | collective-permute-start | bytes 589832 | tf_op jit(solution)/shard_map/keys_z/ppermute | solution.py:36
  124.7 13.2 %collective-permute-start.23 = (bf16[2,192,256]{2,1,0:T(8,128)(2,1)S(1)}, bf16[2,192,256]{2,1,0:T(8,128)(2,1)S(1)}, u32[]{:S(2)}, u32[]{:S(2)}) collective-permute-start(bf16[2,192,256]{2,1,0:T(8,128)(2,1)S(1)} %get-tuple-element.21), channel_id=1, source_target_pairs={{0,0},{1,1},{2,16},{3,17},{4,4},{5,5},{6,20},{7,21},{8,8},{9,9},{1... | collective-permute-start | bytes 589832 | tf_op jit(solution)/shard_map/keys_z/ppermute | solution.py:36
  125.3 15.6 %collective-permute-start.22 = (bf16[2,192,256]{2,1,0:T(8,128)(2,1)S(1)}, bf16[2,192,256]{2,1,0:T(8,128)(2,1)S(1)}, u32[]{:S(2)}, u32[]{:S(2)}) collective-permute-start(bf16[2,192,256]{2,1,0:T(8,128)(2,1)S(1)} %get-tuple-element.19), channel_id=1, source_target_pairs={{0,12},{1,13},{2,28},{3,29},{4,0},{5,1},{6,16},{7,17},{8,4},{9,5},... | collective-permute-start | bytes 589832 | tf_op jit(solution)/shard_map/keys_z/ppermute | solution.py:36
  141.1 21.5 %copy-start.9 = (bf16[4,2,192,256]{3,2,1,0:T(8,128)(2,1)}, bf16[4,2,192,256]{3,2,1,0:T(8,128)(2,1)S(1)}, u32[]{:S(2)}) copy-start(bf16[4,2,192,256]{3,2,1,0:T(8,128)(2,1)S(1)} %pad_maximum_fusion.g0) | copy-start | bytes 2359300
  141.1 20.4 %collective-permute-start.25 = (bf16[4,2,192,256]{3,2,1,0:T(8,128)(2,1)S(1)}, bf16[4,2,192,256]{3,2,1,0:T(8,128)(2,1)S(1)}, u32[]{:S(2)}, u32[]{:S(2)}) collective-permute-start(bf16[4,2,192,256]{3,2,1,0:T(8,128)(2,1)S(1)} %pad_maximum_fusion.g0), channel_id=1, source_target_pairs={{0,1},{1,0},{2,3},{3,2},{4,5},{5,4},{6,7},{7,6},{8,9},{9,8},{10,11... | collective-permute-start | bytes 2359304 | tf_op jit(solution)/shard_map/keys_y/ppermute | solution.py:36
  142.5 21.1 %copy-start.1 = (bf16[16,48,768]{2,1,0:T(8,128)(2,1)S(1)}, bf16[16,48,768]{2,1,0:T(8,128)(2,1)}, u32[]{:S(2)}) copy-start(bf16[16,48,768]{2,1,0:T(8,128)(2,1)} %get-tuple-element.18.mine) | copy-start | bytes 3538948
  142.5 10.5 %collective-permute-start.18 = (bf16[192,256]{1,0:T(8,128)(2,1)S(1)}, bf16[192,256]{1,0:T(8,128)(2,1)S(1)}, u32[]{:S(2)}, u32[]{:S(2)}) collective-permute-start(bf16[192,256]{1,0:T(8,128)(2,1)S(1)} %get-tuple-element.29), channel_id=1, source_target_pairs={{0,4},{1,5},{2,20},{3,21},{4,8},{5,9},{6,24},{7,25},{8,12},{9,13},... | collective-permute-start | bytes 294920 | tf_op jit(solution)/shard_map/queries_z/ppermute | solution.py:36
  144.8 12.6 %collective-permute-start.19 = (bf16[192,256]{1,0:T(8,128)(2,1)S(1)}, bf16[192,256]{1,0:T(8,128)(2,1)S(1)}, u32[]{:S(2)}, u32[]{:S(2)}) collective-permute-start(bf16[192,256]{1,0:T(8,128)(2,1)S(1)} %get-tuple-element.32), channel_id=1, source_target_pairs={{0,12},{1,13},{2,28},{3,29},{4,0},{5,1},{6,16},{7,17},{8,4},{9,5},... | collective-permute-start | bytes 294920 | tf_op jit(solution)/shard_map/queries_z/ppermute | solution.py:36
  147.7 11.4 %collective-permute-start.20 = (bf16[192,256]{1,0:T(8,128)(2,1)S(1)}, bf16[192,256]{1,0:T(8,128)(2,1)S(1)}, u32[]{:S(2)}, u32[]{:S(2)}) collective-permute-start(bf16[192,256]{1,0:T(8,128)(2,1)S(1)} %get-tuple-element.31), channel_id=1, source_target_pairs={{0,0},{1,1},{2,16},{3,17},{4,4},{5,5},{6,20},{7,21},{8,8},{9,9},{1... | collective-permute-start | bytes 294920 | tf_op jit(solution)/shard_map/queries_z/ppermute | solution.py:36
  148.4 11.9 %collective-permute-start.21 = (bf16[192,256]{1,0:T(8,128)(2,1)S(1)}, bf16[192,256]{1,0:T(8,128)(2,1)S(1)}, u32[]{:S(2)}, u32[]{:S(2)}) collective-permute-start(bf16[192,256]{1,0:T(8,128)(2,1)S(1)} %get-tuple-element.30), channel_id=1, source_target_pairs={{0,8},{1,9},{2,24},{3,25},{4,12},{5,13},{6,28},{7,29},{8,0},{9,1},... | collective-permute-start | bytes 294920 | tf_op jit(solution)/shard_map/queries_z/ppermute | solution.py:36
  153.1 11.5 %collective-permute-start.27 = (bf16[4,2,192,256]{3,2,1,0:T(8,128)(2,1)S(1)}, bf16[4,2,192,256]{3,2,1,0:T(8,128)(2,1)S(1)}, u32[]{:S(2)}, u32[]{:S(2)}) collective-permute-start(bf16[4,2,192,256]{3,2,1,0:T(8,128)(2,1)S(1)} %pad_maximum_fusion.g0), channel_id=1, source_target_pairs={{0,16},{1,17},{2,18},{3,19},{4,20},{5,21},{6,22},{7,23},{8,24},{9,... | collective-permute-start | bytes 2359304 | tf_op jit(solution)/shard_map/keys_core/ppermute | solution.py:36
  161.5 2.2 %copy-start.8 = (bf16[4,2,192,256]{3,2,1,0:T(8,128)(2,1)}, bf16[4,2,192,256]{3,2,1,0:T(8,128)(2,1)S(1)}, u32[]{:S(2)}) copy-start(bf16[4,2,192,256]{3,2,1,0:T(8,128)(2,1)S(1)} %collective-permute-done.25.g0) | copy-start | bytes 2359300
  162.6 11.6 %collective-permute-start.26 = (bf16[4,2,192,256]{3,2,1,0:T(8,128)(2,1)}, bf16[4,2,192,256]{3,2,1,0:T(8,128)(2,1)}, u32[]{:S(2)}, u32[]{:S(2)}) collective-permute-start(bf16[4,2,192,256]{3,2,1,0:T(8,128)(2,1)} %broadcast_add_fusion.1), channel_id=1, source_target_pairs={{0,16},{1,17},{2,18},{3,19},{4,20},{5,21},{6,22},{7,23},{8,24},{9,... | collective-permute-start | bytes 2359304 | tf_op jit(solution)/shard_map/keys_y_core/ppermute | solution.py:36
  163.7 33.1 %collective-permute-start.32 = (bf16[16,48,768]{2,1,0:T(8,128)(2,1)S(1)}, bf16[16,48,768]{2,1,0:T(8,128)(2,1)S(1)}, u32[]{:S(2)}, u32[]{:S(2)}) collective-permute-start(bf16[16,48,768]{2,1,0:T(8,128)(2,1)S(1)} %broadcast_add_fusion), channel_id=1, source_target_pairs={{0,16},{1,17},{2,18},{3,19},{4,20},{5,21},{6,22},{7,23},{8,24},{9,... | collective-permute-start | bytes 3538952 | tf_op jit(solution)/shard_map/out_core/ppermute | solution.py:36
  184.7 12.1 %collective-permute-start.28 = (bf16[192,256]{1,0:T(8,128)(2,1)S(1)}, bf16[192,256]{1,0:T(8,128)(2,1)S(1)}, u32[]{:S(2)}, u32[]{:S(2)}) collective-permute-start(bf16[192,256]{1,0:T(8,128)(2,1)S(1)} %get-tuple-element.28), channel_id=1, source_target_pairs={{0,4},{1,5},{2,8},{3,9},{4,16},{5,17},{6,20},{7,21},{8,12},{9,13},... | collective-permute-start | bytes 294920 | tf_op jit(solution)/shard_map/heads_back/ppermute | solution.py:36
  185.7 11.0 %collective-permute-start.29 = (bf16[192,256]{1,0:T(8,128)(2,1)S(1)}, bf16[192,256]{1,0:T(8,128)(2,1)S(1)}, u32[]{:S(2)}, u32[]{:S(2)}) collective-permute-start(bf16[192,256]{1,0:T(8,128)(2,1)S(1)} %get-tuple-element.27), channel_id=1, source_target_pairs={{0,12},{1,13},{2,0},{3,1},{4,28},{5,29},{6,24},{7,25},{8,4},{9,5},... | collective-permute-start | bytes 294920 | tf_op jit(solution)/shard_map/heads_back/ppermute | solution.py:36
  191.2 5.6 %collective-permute-start.30 = (bf16[192,256]{1,0:T(8,128)(2,1)S(1)}, bf16[192,256]{1,0:T(8,128)(2,1)S(1)}, u32[]{:S(2)}, u32[]{:S(2)}) collective-permute-start(bf16[192,256]{1,0:T(8,128)(2,1)S(1)} %get-tuple-element.26), channel_id=1, source_target_pairs={{0,0},{1,1},{2,12},{3,13},{4,24},{5,25},{6,28},{7,29},{8,8},{9,9},... | collective-permute-start | bytes 294920 | tf_op jit(solution)/shard_map/heads_back/ppermute | solution.py:36
  191.9 11.1 %collective-permute-start.31 = (bf16[192,256]{1,0:T(8,128)(2,1)S(1)}, bf16[192,256]{1,0:T(8,128)(2,1)S(1)}, u32[]{:S(2)}, u32[]{:S(2)}) collective-permute-start(bf16[192,256]{1,0:T(8,128)(2,1)S(1)} %get-tuple-element.25), channel_id=1, source_target_pairs={{0,8},{1,9},{2,4},{3,5},{4,20},{5,21},{6,16},{7,17},{8,0},{9,1},{1... | collective-permute-start | bytes 294920 | tf_op jit(solution)/shard_map/heads_back/ppermute | solution.py:36
  196.7 6.3 %copy-start.5 = (bf16[16,48,768]{2,1,0:T(8,128)(2,1)}, bf16[16,48,768]{2,1,0:T(8,128)(2,1)S(1)}, u32[]{:S(2)}) copy-start(bf16[16,48,768]{2,1,0:T(8,128)(2,1)S(1)} %collective-permute-done.32.theirs) | copy-start | bytes 3538948
  196.8 6.3 %copy-start.15 = (bf16[192,256]{1,0:T(8,128)(2,1)}, bf16[192,256]{1,0:T(8,128)(2,1)S(1)}, u32[]{:S(2)}) copy-start(bf16[192,256]{1,0:T(8,128)(2,1)S(1)} %collective-permute-done.28.h0) | copy-start | bytes 294916
  196.8 6.2 %copy-start.16 = (bf16[192,256]{1,0:T(8,128)(2,1)}, bf16[192,256]{1,0:T(8,128)(2,1)S(1)}, u32[]{:S(2)}) copy-start(bf16[192,256]{1,0:T(8,128)(2,1)S(1)} %collective-permute-done.29.h1) | copy-start | bytes 294916
  196.8 6.2 %copy-start.17 = (bf16[192,256]{1,0:T(8,128)(2,1)}, bf16[192,256]{1,0:T(8,128)(2,1)S(1)}, u32[]{:S(2)}) copy-start(bf16[192,256]{1,0:T(8,128)(2,1)S(1)} %collective-permute-done.30.h2) | copy-start | bytes 294916
  (8 other events, 7.6 us)

commit v5 on v4

--- a/solution.py
+++ b/solution.py
@@ -149,16 +149,14 @@
 def acts_kernel(own, other, out):
     for which, window in enumerate((own, other)):
         columns = window[...].T
-
-        def one(number, _):
-            row = lax.broadcasted_iota(jnp.int32, (528, 256), 0)
-            col = lax.broadcasted_iota(jnp.int32, (528, 256), 1)
-            pick = jnp.where(row == 2 * col + number, 1.0, 0.0).astype(BF16)
+        for odd in range(2):
+            row = lax.broadcasted_iota(jnp.int32, (528, 384), 0)
+            col = lax.broadcasted_iota(jnp.int32, (528, 384), 1)
+            pick = jnp.where(row == 2 * col + odd, 1.0, 0.0).astype(BF16)
             picked = jnp.dot(columns, pick, preferred_element_type=F32)
-            out[number, :, 256 * which : 256 * which + 256] = picked.astype(BF16)
-            return 0
-
-        lax.fori_loop(0, 6, one, 0)
+            for step in range(3):
+                lanes = slice(256 * which, 256 * which + 256)
+                out[2 * step + odd, :, lanes] = picked[:, step : step + 256].astype(BF16)
 
 
 def conv_kernel(base, table, acts, bias, *refs):

time: 208 us -> 208 us (level)
  Pallas kernels: 60.9 us -> 57.2 us
  waiting for transfers between devices: 40.5 us -> 42.8 us
    pallas_call x8, Pallas kernels: 60.9 us -> 57.2 us  [call(): pl.pallas_call(kernel, out_shape=outs, in_specs=ins, out_specs=jax.tree.m...]
    ppermute x31, waiting for transfers between devices: 39.2 us -> 41.6 us  [send(): return lax.ppermute(value, AXES, pairs)]
  transfers between devices with their start and end apart: 33 -> 33, of which waited for: 9 -> 9; matrix products, arithmetic and copies ran while one was open for 11% -> 12% of each run, Pallas kernels for 23% -> 22%
where the time goes in v5:
time: 208 us; the launch traced here: 205 us
  starting transfers between devices  66.1 us (32%)
  Pallas kernels  57.2 us (28%)
  waiting for transfers between devices  42.8 us (21%)
  local copies, waits for them, and re-layouts  29 us (14%)
  between operations  6.37 us (3%)
  other arithmetic  3.97 us (2%)
    ppermute x31, starting transfers between devices, send(): return lax.ppermute(value, AXES, pairs)  60.3 us
    pallas_call x8, Pallas kernels, call(): pl.pallas_call(kernel, out_shape=outs, in_specs=ins, out_specs=jax.tree.m...  57.2 us
    ppermute x31, waiting for transfers between devices, send(): return lax.ppermute(value, AXES, pairs)  41.6 us
    slice x9, local copies, waits for them, and re-layouts, after(): zero = sum((o[(0,) * o.ndim].astype(F32) * 0.0 for o in others), F32(0.0))  5.42 us
    dynamic_update_slice x6, local copies, waits for them, and re-layouts, stacked(): lax.dynamic_update_slice(out, blocks[at][None], (at,) + (0,) * blocks[at]...  4.92 us
    ppermute x1, starting transfers between devices, shards(): before = lax.ppermute(activated[-2:], AXES, forward)  4.55 us
  transfers between devices with their start and end apart: 33, of which 9 were waited for; matrix products, arithmetic and copies ran while one was open for 12% of the time, Pallas kernels for 22%

profile of v5, /device:TPU:6, one launch (start us, length us, event | category | flops | bytes accessed | tf_op | source)
XLA Modules:
  0.0 205.4 jit_solution(2520591654645550251)
XLA Ops:
  0.0 1.1 dynamic-slice_bitcast_fusion.1
  1.4 6.5 %collective-permute-start.3 = (bf16[9,48,768]{2,1,0:T(8,128)(2,1)S(1)}, bf16[9,48,768]{2,1,0:T(8,128)(2,1)S(1)}, u32[]{:S(2)}, u32[]{:S(2)}) collective-permute-start(bf16[9,48,768]{2,1,0:T(8,128)(2,1)S(1)} %pad_maximum_fusion.1), channel_id=1, source_target_pairs={{0,4},{1,5},{2,2},{3,3},{4,6},{5,7},{6,0},{7,1},{8,18},{9,19},{10,... | collective-permute-start | bytes 1990664 | tf_op jit(solution)/shard_map/weights_z/ppermute | solution.py:36
  9.7 1.3 collective-permute-start.1
  11.0 4.5 %collective-permute-start = (bf16[2,768]{1,0:T(2,128)(2,1)S(1)}, bf16[2,768]{1,0:T(2,128)(2,1)S(1)}, u32[]{:S(2)}, u32[]{:S(2)}) collective-permute-start(bf16[2,768]{1,0:T(2,128)(2,1)S(1)} %get-tuple-element.23), channel_id=1, source_target_pairs={{0,1},{1,2},{2,3},{3,4},{4,5},{5,6},{6,7},{7,8},{8,9},{9,10},{10,1... | collective-permute-start | bytes 9224 | tf_op jit(solution)/shard_map/ppermute | solution.py:358
  15.7 1.2 collective-permute-done
  17.2 1.2 collective-permute-start.2
  18.4 4.5 %collective-permute-done.3 = bf16[9,48,768]{2,1,0:T(8,128)(2,1)S(1)} collective-permute-done((bf16[9,48,768]{2,1,0:T(8,128)(2,1)S(1)}, bf16[9,48,768]{2,1,0:T(8,128)(2,1)S(1)}, u32[]{:S(2)}, u32[]{:S(2)}) %collective-permute-start.3) | collective-permute-done | bytes 663584 | tf_op jit(solution)/shard_map/weights_z/ppermute | solution.py:36
  22.8 2.9 %collective-permute-start.5 = (bf16[9,48,768]{2,1,0:T(8,128)(2,1)S(1)}, bf16[9,48,768]{2,1,0:T(8,128)(2,1)S(1)}, u32[]{:S(2)}, u32[]{:S(2)}) collective-permute-start(bf16[9,48,768]{2,1,0:T(8,128)(2,1)S(1)} %collective-permute-done.3), channel_id=1, source_target_pairs={{0,192},{1,193},{2,194},{3,195},{4,196},{5,197},{6,198},{7,199},{8... | collective-permute-start | bytes 1990664 | tf_op jit(solution)/shard_map/weights_first/ppermute | solution.py:36
  27.0 6.5 %acts_kernel.1.refs_1_ = bf16[6,768,512]{2,1,0:T(8,128)(2,1)} custom-call(bf16[528,768]{1,0:T(8,128)(2,1)} %copy-done.3, bf16[528,768]{1,0:T(8,128)(2,1)} %copy-done.6), custom_call_target="tpu_custom_call" | custom-call | flops 1000000000 | bytes 8000000 | tf_op jit(solution)/shard_map/acts_kernel/pallas_call | solution.py:327
  33.5 1.2 slice.157
  36.3 1.3 dynamic_update_slice.24
  37.6 4.2 %collective-permute-done.5 = bf16[9,48,768]{2,1,0:T(8,128)(2,1)S(1)} collective-permute-done((bf16[9,48,768]{2,1,0:T(8,128)(2,1)S(1)}, bf16[9,48,768]{2,1,0:T(8,128)(2,1)S(1)}, u32[]{:S(2)}, u32[]{:S(2)}) %collective-permute-start.5) | collective-permute-done | bytes 663584 | tf_op jit(solution)/shard_map/weights_first/ppermute | solution.py:36
  42.6 1.8 fusion.8
  45.2 3.9 %collective-permute-start.8 = (bf16[4,5,48,768]{3,2,1,0:T(8,128)(2,1)}, bf16[4,5,48,768]{3,2,1,0:T(8,128)(2,1)S(1)}, u32[]{:S(2)}, u32[]{:S(2)}) collective-permute-start(bf16[4,5,48,768]{3,2,1,0:T(8,128)(2,1)} %fusion.7.refs_3_), channel_id=1, source_target_pairs={{0,33},{1,0},{2,35},{3,2},{4,37},{5,4},{6,39},{7,6},{8,41},{9,8},{... | collective-permute-start | bytes 4423688 | tf_op jit(solution)/shard_map/conv_second/ppermute | solution.py:36
  51.3 15.1 %collective-permute-done.8.refs_5_ = bf16[4,5,48,768]{3,2,1,0:T(8,128)(2,1)S(1)} collective-permute-done((bf16[4,5,48,768]{3,2,1,0:T(8,128)(2,1)}, bf16[4,5,48,768]{3,2,1,0:T(8,128)(2,1)S(1)}, u32[]{:S(2)}, u32[]{:S(2)}) %collective-permute-start.8) | collective-permute-done | bytes 1474592 | tf_op jit(solution)/shard_map/conv_second/ppermute | solution.py:36
  67.6 1.0 collective-permute-start.13
  68.7 2.7 %collective-permute-start.14 = (bf16[4,4,48,768]{3,2,1,0:T(8,128)(2,1)S(1)}, bf16[4,4,48,768]{3,2,1,0:T(8,128)(2,1)}, u32[]{:S(2)}, u32[]{:S(2)}) collective-permute-start(bf16[4,4,48,768]{3,2,1,0:T(8,128)(2,1)S(1)} %fusion.11.g0), channel_id=1, source_target_pairs={{0,33},{1,0},{2,35},{3,2},{4,37},{5,4},{6,39},{7,6},{8,41},{9,8},{... | collective-permute-start | bytes 3538952 | tf_op jit(solution)/shard_map/qkv_second/ppermute | solution.py:36
  71.5 1.0 reshape.44.refs_2_
  72.5 2.1 %slice.158 = bf16[2,5,48,768]{3,2,1,0:T(8,128)(2,1)} slice(bf16[4,5,48,768]{3,2,1,0:T(8,128)(2,1)} %collective-permute-done.7.refs_4_), slice={[0:2], [0:5], [0:48], [0:768]} | slice | bytes 1474560 | tf_op jit(solution)/shard_map/slice | solution.py:375
  75.6 3.2 %collective-permute-start.10 = (bf16[2,5,48,768]{3,2,1,0:T(8,128)(2,1)}, bf16[2,5,48,768]{3,2,1,0:T(8,128)(2,1)}, u32[]{:S(2)}, u32[]{:S(2)}) collective-permute-start(bf16[2,5,48,768]{3,2,1,0:T(8,128)(2,1)} %slice.159), channel_id=1, source_target_pairs={{0,33},{1,0},{2,35},{3,2},{4,37},{5,4},{6,39},{7,6},{8,41},{9,8},{... | collective-permute-start | bytes 2211848 | tf_op jit(solution)/shard_map/conv_far/ppermute | solution.py:36
  78.8 1.2 fusion.14.refs_0_.table
  80.1 11.0 %conv_kernel.2.refs_3_.ma = bf16[12,48,512]{2,1,0:T(8,128)(2,1)} custom-call(s32[50]{0:T(128)} %fusion.14.refs_0_.table, bf16[6,768,512]{2,1,0:T(8,128)(2,1)} %acts_kernel.1.refs_1_, f32[16,48,1]{2,1,0:T(8,128)} %reshape.44.refs_2_, bf16[4,5,48,768]{3,2,1,0:T(8,128)(2,1)} %fusion.7.refs_3_, bf16[4,5,48,768]{3,2,1,0:T(8,128)(2,1)} %collective-permute-done.7.refs_4_, ...), custom_call_target="tpu_custom_call" | custom-call | flops 4499999744 | bytes 8000000 | tf_op jit(solution)/shard_map/conv_kernel/pallas_call | solution.py:327
  92.2 1.1 slice.166
  93.3 3.3 %collective-permute-start.16 = (bf16[2,4,48,768]{3,2,1,0:T(8,128)(2,1)S(1)}, bf16[2,4,48,768]{3,2,1,0:T(8,128)(2,1)S(1)}, u32[]{:S(2)}, u32[]{:S(2)}) collective-permute-start(bf16[2,4,48,768]{3,2,1,0:T(8,128)(2,1)S(1)} %slice.166), channel_id=1, source_target_pairs={{0,33},{1,0},{2,35},{3,2},{4,37},{5,4},{6,39},{7,6},{8,41},{9,8},{... | collective-permute-start | bytes 1769480 | tf_op jit(solution)/shard_map/qkv_far/ppermute | solution.py:36
  96.6 6.6 %conv_kernel.3.mb = bf16[4,48,512]{2,1,0:T(8,128)(2,1)} custom-call(s32[50]{0:T(128)} %fusion.14.refs_0_.table, bf16[6,768,512]{2,1,0:T(8,128)(2,1)} %acts_kernel.1.refs_1_, f32[16,48,1]{2,1,0:T(8,128)} %reshape.44.refs_2_, bf16[12,48,512]{2,1,0:T(8,128)(2,1)} %conv_kernel.2.refs_3_.ma, bf16[2,5,48,768]{3,2,1,0:T(8,128)(2,1)} %collective-permute-done.9.refs_4_, ...), custom_call_target="tpu_custom_call" | custom-call | flops 1500000000 | bytes 8000000 | tf_op jit(solution)/shard_map/conv_kernel/pallas_call | solution.py:327
  103.3 1.5 reshape.45.gain
  106.4 8.8 %project_kernel.1 = (bf16[4,2,192,256]{3,2,1,0:T(8,128)(2,1)}, bf16[4,192,256]{2,1,0:T(8,128)(2,1)}, bf16[16,48,768]{2,1,0:T(8,128)(2,1)}, bf16[2,16,48,512]{3,2,1,0:T(8,128)(2,1)}) custom-call(s32[50]{0:T(128)} %fusion.14.refs_0_.table, bf16[12,48,512]{2,1,0:T(8,128)(2,1)} %conv_kernel.2.refs_3_.ma, bf16[4,48,512]{2,1,0:T(8,128)(2,1)} %conv_kernel.3.mb, ...), custom_call_target="tpu_custom_call" | custom-call | flops 1800000000 | bytes 8000000 | tf_op jit(solution)/shard_map/project_kernel/pallas_call | solution.py:327
  115.2 1.3 slice_bitcast_fusion.8
  116.5 3.4 %collective-permute-start.17 = (bf16[2,192,256]{2,1,0:T(8,128)(2,1)S(1)}, bf16[2,192,256]{2,1,0:T(8,128)(2,1)S(1)}, u32[]{:S(2)}, u32[]{:S(2)}) collective-permute-start(bf16[2,192,256]{2,1,0:T(8,128)(2,1)S(1)} %get-tuple-element.22), channel_id=1, source_target_pairs={{0,4},{1,5},{2,20},{3,21},{4,8},{5,9},{6,24},{7,25},{8,12},{9,13},... | collective-permute-start | bytes 589832 | tf_op jit(solution)/shard_map/keys_z/ppermute | solution.py:36
  120.0 4.7 %collective-permute-start.24 = (bf16[2,192,256]{2,1,0:T(8,128)(2,1)S(1)}, bf16[2,192,256]{2,1,0:T(8,128)(2,1)S(1)}, u32[]{:S(2)}, u32[]{:S(2)}) collective-permute-start(bf16[2,192,256]{2,1,0:T(8,128)(2,1)S(1)} %get-tuple-element.20), channel_id=1, source_target_pairs={{0,8},{1,9},{2,24},{3,25},{4,12},{5,13},{6,28},{7,29},{8,0},{9,1},... | collective-permute-start | bytes 589832 | tf_op jit(solution)/shard_map/keys_z/ppermute | solution.py:36
  125.3 2.6 %collective-permute-start.22 = (bf16[2,192,256]{2,1,0:T(8,128)(2,1)S(1)}, bf16[2,192,256]{2,1,0:T(8,128)(2,1)S(1)}, u32[]{:S(2)}, u32[]{:S(2)}) collective-permute-start(bf16[2,192,256]{2,1,0:T(8,128)(2,1)S(1)} %get-tuple-element.19), channel_id=1, source_target_pairs={{0,12},{1,13},{2,28},{3,29},{4,0},{5,1},{6,16},{7,17},{8,4},{9,5},... | collective-permute-start | bytes 589832 | tf_op jit(solution)/shard_map/keys_z/ppermute | solution.py:36
  128.0 4.7 %collective-permute-done.17 = bf16[2,192,256]{2,1,0:T(8,128)(2,1)S(1)} collective-permute-done((bf16[2,192,256]{2,1,0:T(8,128)(2,1)S(1)}, bf16[2,192,256]{2,1,0:T(8,128)(2,1)S(1)}, u32[]{:S(2)}, u32[]{:S(2)}) %collective-permute-start.17) | collective-permute-done | bytes 196640 | tf_op jit(solution)/shard_map/keys_z/ppermute | solution.py:36
  132.7 3.7 %collective-permute-done.24 = bf16[2,192,256]{2,1,0:T(8,128)(2,1)S(1)} collective-permute-done((bf16[2,192,256]{2,1,0:T(8,128)(2,1)S(1)}, bf16[2,192,256]{2,1,0:T(8,128)(2,1)S(1)}, u32[]{:S(2)}, u32[]{:S(2)}) %collective-permute-start.24) | collective-permute-done | bytes 196640 | tf_op jit(solution)/shard_map/keys_z/ppermute | solution.py:36
  136.5 3.2 %collective-permute-done.22 = bf16[2,192,256]{2,1,0:T(8,128)(2,1)S(1)} collective-permute-done((bf16[2,192,256]{2,1,0:T(8,128)(2,1)S(1)}, bf16[2,192,256]{2,1,0:T(8,128)(2,1)S(1)}, u32[]{:S(2)}, u32[]{:S(2)}) %collective-permute-start.22) | collective-permute-done | bytes 196640 | tf_op jit(solution)/shard_map/keys_z/ppermute | solution.py:36
  141.3 3.3 %collective-permute-start.18 = (bf16[192,256]{1,0:T(8,128)(2,1)S(1)}, bf16[192,256]{1,0:T(8,128)(2,1)S(1)}, u32[]{:S(2)}, u32[]{:S(2)}) collective-permute-start(bf16[192,256]{1,0:T(8,128)(2,1)S(1)} %get-tuple-element.29), channel_id=1, source_target_pairs={{0,4},{1,5},{2,20},{3,21},{4,8},{5,9},{6,24},{7,25},{8,12},{9,13},... | collective-permute-start | bytes 294920 | tf_op jit(solution)/shard_map/queries_z/ppermute | solution.py:36
  144.6 1.3 collective-permute-start.19
  146.6 5.5 %collective-permute-start.21 = (bf16[192,256]{1,0:T(8,128)(2,1)S(1)}, bf16[192,256]{1,0:T(8,128)(2,1)S(1)}, u32[]{:S(2)}, u32[]{:S(2)}) collective-permute-start(bf16[192,256]{1,0:T(8,128)(2,1)S(1)} %get-tuple-element.30), channel_id=1, source_target_pairs={{0,8},{1,9},{2,24},{3,25},{4,12},{5,13},{6,28},{7,29},{8,0},{9,1},... | collective-permute-start | bytes 294920 | tf_op jit(solution)/shard_map/queries_z/ppermute | solution.py:36
  152.0 2.4 %collective-permute-start.27 = (bf16[4,2,192,256]{3,2,1,0:T(8,128)(2,1)S(1)}, bf16[4,2,192,256]{3,2,1,0:T(8,128)(2,1)S(1)}, u32[]{:S(2)}, u32[]{:S(2)}) collective-permute-start(bf16[4,2,192,256]{3,2,1,0:T(8,128)(2,1)S(1)} %pad_maximum_fusion.g0), channel_id=1, source_target_pairs={{0,16},{1,17},{2,18},{3,19},{4,20},{5,21},{6,22},{7,23},{8,24},{9,... | collective-permute-start | bytes 2359304 | tf_op jit(solution)/shard_map/keys_core/ppermute | solution.py:36
  160.2 1.1 broadcast_add_fusion.1
  164.0 8.7 %attend_kernel.1 = (f32[4,256,128]{2,1,0:T(8,128)}, f32[4,256,128]{2,1,0:T(8,128)}, f32[4,256,192]{2,1,0:T(8,128)}) custom-call(s32[50]{0:T(128)} %fusion.14.refs_0_.table, f32[4]{0:T(128)} %factor.3, bf16[4,192,256]{2,1,0:T(8,128)(2,1)} %pad_maximum_fusion.2.queries, bf16[4,2,192,256]{3,2,1,0:T(8,128)(2,1)} %copy-done.9, bf16[4,2,192,256]{3,2,1,0:T(8,128)(2,1)} %copy-done.22), custom_call_target="tpu_custom_call" | custom-call | flops 1600000000 | bytes 8000000 | tf_op jit(solution)/shard_map/attend_kernel/pallas_call | solution.py:327
  172.7 9.4 %finish_kernel.1 = bf16[4,192,256]{2,1,0:T(8,128)(2,1)} custom-call(s32[50]{0:T(128)} %fusion.14.refs_0_.table, f32[4]{0:T(128)} %factor.3, bf16[4,192,256]{2,1,0:T(8,128)(2,1)} %pad_maximum_fusion.2.queries, bf16[4,2,192,256]{3,2,1,0:T(8,128)(2,1)} %copy-done.8, bf16[4,2,192,256]{3,2,1,0:T(8,128)(2,1)} %collective-permute-done.26.g1, ...), custom_call_target="tpu_custom_call" | custom-call | flops 1600000000 | bytes 8000000 | tf_op jit(solution)/shard_map/finish_kernel/pallas_call | solution.py:327
  182.1 1.1 slice_bitcast_fusion.10
  183.2 2.5 %collective-permute-start.28 = (bf16[192,256]{1,0:T(8,128)(2,1)S(1)}, bf16[192,256]{1,0:T(8,128)(2,1)S(1)}, u32[]{:S(2)}, u32[]{:S(2)}) collective-permute-start(bf16[192,256]{1,0:T(8,128)(2,1)S(1)} %get-tuple-element.28), channel_id=1, source_target_pairs={{0,4},{1,5},{2,8},{3,9},{4,16},{5,17},{6,20},{7,21},{8,12},{9,13},... | collective-permute-start | bytes 294920 | tf_op jit(solution)/shard_map/heads_back/ppermute | solution.py:36
  185.6 3.5 %collective-permute-start.29 = (bf16[192,256]{1,0:T(8,128)(2,1)S(1)}, bf16[192,256]{1,0:T(8,128)(2,1)S(1)}, u32[]{:S(2)}, u32[]{:S(2)}) collective-permute-start(bf16[192,256]{1,0:T(8,128)(2,1)S(1)} %get-tuple-element.27), channel_id=1, source_target_pairs={{0,12},{1,13},{2,0},{3,1},{4,28},{5,29},{6,24},{7,25},{8,4},{9,5},... | collective-permute-start | bytes 294920 | tf_op jit(solution)/shard_map/heads_back/ppermute | solution.py:36
  189.9 2.6 %collective-permute-start.31 = (bf16[192,256]{1,0:T(8,128)(2,1)S(1)}, bf16[192,256]{1,0:T(8,128)(2,1)S(1)}, u32[]{:S(2)}, u32[]{:S(2)}) collective-permute-start(bf16[192,256]{1,0:T(8,128)(2,1)S(1)} %get-tuple-element.25), channel_id=1, source_target_pairs={{0,8},{1,9},{2,4},{3,5},{4,20},{5,21},{6,16},{7,17},{8,0},{9,1},{1... | collective-permute-start | bytes 294920 | tf_op jit(solution)/shard_map/heads_back/ppermute | solution.py:36
  192.5 2.5 %base_kernel.1.base = bf16[256,1536]{1,0:T(8,128)(2,1)} custom-call(bf16[2,16,48,512]{3,2,1,0:T(8,128)(2,1)} %get-tuple-element.17.tokens), custom_call_target="tpu_custom_call" | custom-call | flops 1000000 | bytes 8000000 | tf_op jit(solution)/shard_map/base_kernel/pallas_call | solution.py:327
  195.1 5.9 %collective-permute-done.31.h3 = bf16[192,256]{1,0:T(8,128)(2,1)S(1)} collective-permute-done((bf16[192,256]{1,0:T(8,128)(2,1)S(1)}, bf16[192,256]{1,0:T(8,128)(2,1)S(1)}, u32[]{:S(2)}, u32[]{:S(2)}) %collective-permute-start.31) | collective-permute-done | bytes 98336 | tf_op jit(solution)/shard_map/heads_back/ppermute | solution.py:36
  201.7 3.8 %out_kernel.1 = bf16[256,1536]{1,0:T(8,128)(2,1)} custom-call(s32[50]{0:T(128)} %fusion.14.refs_0_.table, bf16[192,256]{1,0:T(8,128)(2,1)} %copy-done.15, bf16[192,256]{1,0:T(8,128)(2,1)} %copy-done.16, bf16[192,256]{1,0:T(8,128)(2,1)} %copy-done.17, bf16[192,256]{1,0:T(8,128)(2,1)} %copy-done.18, bf16[256,1536]{1,0:T(8,128)(2,1)} %base_kernel.1.base, ...), custom_call_target="tpu_custom_call" | custom-call | flops 600000000 | bytes 8000000 | tf_op jit(solution)/shard_map/out_kernel/pallas_call | solution.py:327
  (118 shorter events, 21.0 us)
Async XLA Ops:
  0.0 9.1 %copy-start.7 = (bf16[512,768]{1,0:T(8,128)(2,1)S(1)}, bf16[512,768]{1,0:T(8,128)(2,1)}, u32[]{:S(2)}) copy-start(bf16[512,768]{1,0:T(8,128)(2,1)} %param.8) | copy-start | bytes 2359300
  1.4 21.4 %collective-permute-start.3 = (bf16[9,48,768]{2,1,0:T(8,128)(2,1)S(1)}, bf16[9,48,768]{2,1,0:T(8,128)(2,1)S(1)}, u32[]{:S(2)}, u32[]{:S(2)}) collective-permute-start(bf16[9,48,768]{2,1,0:T(8,128)(2,1)S(1)} %pad_maximum_fusion.1), channel_id=1, source_target_pairs={{0,4},{1,5},{2,2},{3,3},{4,6},{5,7},{6,0},{7,1},{8,18},{9,19},{10,... | collective-permute-start | bytes 1990664 | tf_op jit(solution)/shard_map/weights_z/ppermute | solution.py:36
  9.7 5.9 %collective-permute-start.1 = (bf16[2,768]{1,0:T(2,128)(2,1)S(1)}, bf16[2,768]{1,0:T(2,128)(2,1)S(1)}, u32[]{:S(2)}, u32[]{:S(2)}) collective-permute-start(bf16[2,768]{1,0:T(2,128)(2,1)S(1)} %get-tuple-element.24), channel_id=1, source_target_pairs={{1,0},{2,1},{3,2},{4,3},{5,4},{6,5},{7,6},{8,7},{9,8},{10,9},{11,1... | collective-permute-start | bytes 9224 | tf_op jit(solution)/shard_map/ppermute | solution.py:359
  11.0 5.9 %collective-permute-start = (bf16[2,768]{1,0:T(2,128)(2,1)S(1)}, bf16[2,768]{1,0:T(2,128)(2,1)S(1)}, u32[]{:S(2)}, u32[]{:S(2)}) collective-permute-start(bf16[2,768]{1,0:T(2,128)(2,1)S(1)} %get-tuple-element.23), channel_id=1, source_target_pairs={{0,1},{1,2},{2,3},{3,4},{4,5},{5,6},{6,7},{7,8},{8,9},{9,10},{10,1... | collective-permute-start | bytes 9224 | tf_op jit(solution)/shard_map/ppermute | solution.py:358
  17.2 8.9 %copy-start.3 = (bf16[528,768]{1,0:T(8,128)(2,1)}, bf16[528,768]{1,0:T(8,128)(2,1)S(1)}, u32[]{:S(2)}) copy-start(bf16[528,768]{1,0:T(8,128)(2,1)S(1)} %maximum_maximum_fusion.own) | copy-start | bytes 2433028
  17.2 8.9 %collective-permute-start.2 = (bf16[528,768]{1,0:T(8,128)(2,1)S(1)}, bf16[528,768]{1,0:T(8,128)(2,1)S(1)}, u32[]{:S(2)}, u32[]{:S(2)}) collective-permute-start(bf16[528,768]{1,0:T(8,128)(2,1)S(1)} %maximum_maximum_fusion.own), channel_id=1, source_target_pairs={{0,16},{1,17},{2,18},{3,19},{4,20},{5,21},{6,22},{7,23},{8,24},{9,... | collective-permute-start | bytes 2433032 | tf_op jit(solution)/shard_map/acts_core/ppermute | solution.py:36
  22.8 12.5 %collective-permute-start.4 = (bf16[9,48,768]{2,1,0:T(8,128)(2,1)S(1)}, bf16[9,48,768]{2,1,0:T(8,128)(2,1)}, u32[]{:S(2)}, u32[]{:S(2)}) collective-permute-start(bf16[9,48,768]{2,1,0:T(8,128)(2,1)S(1)} %collective-permute-done.3), channel_id=1, source_target_pairs={{0,128},{1,129},{2,130},{3,131},{4,132},{5,133},{6,134},{7,135},{8... | collective-permute-start | bytes 1990664 | tf_op jit(solution)/shard_map/weights_first/ppermute | solution.py:36
  22.8 19.0 %collective-permute-start.5 = (bf16[9,48,768]{2,1,0:T(8,128)(2,1)S(1)}, bf16[9,48,768]{2,1,0:T(8,128)(2,1)S(1)}, u32[]{:S(2)}, u32[]{:S(2)}) collective-permute-start(bf16[9,48,768]{2,1,0:T(8,128)(2,1)S(1)} %collective-permute-done.3), channel_id=1, source_target_pairs={{0,192},{1,193},{2,194},{3,195},{4,196},{5,197},{6,198},{7,199},{8... | collective-permute-start | bytes 1990664 | tf_op jit(solution)/shard_map/weights_first/ppermute | solution.py:36
  25.7 16.9 %collective-permute-start.6 = (bf16[9,48,768]{2,1,0:T(8,128)(2,1)S(1)}, bf16[9,48,768]{2,1,0:T(8,128)(2,1)}, u32[]{:S(2)}, u32[]{:S(2)}) collective-permute-start(bf16[9,48,768]{2,1,0:T(8,128)(2,1)S(1)} %collective-permute-done.3), channel_id=1, source_target_pairs={{0,64},{1,65},{2,66},{3,67},{4,68},{5,69},{6,70},{7,71},{8,72},{9,... | collective-permute-start | bytes 1990664 | tf_op jit(solution)/shard_map/weights_first/ppermute | solution.py:36
  45.2 21.1 %collective-permute-start.8 = (bf16[4,5,48,768]{3,2,1,0:T(8,128)(2,1)}, bf16[4,5,48,768]{3,2,1,0:T(8,128)(2,1)S(1)}, u32[]{:S(2)}, u32[]{:S(2)}) collective-permute-start(bf16[4,5,48,768]{3,2,1,0:T(8,128)(2,1)} %fusion.7.refs_3_), channel_id=1, source_target_pairs={{0,33},{1,0},{2,35},{3,2},{4,37},{5,4},{6,39},{7,6},{8,41},{9,8},{... | collective-permute-start | bytes 4423688 | tf_op jit(solution)/shard_map/conv_second/ppermute | solution.py:36
  49.2 23.3 %collective-permute-start.7 = (bf16[4,5,48,768]{3,2,1,0:T(8,128)(2,1)}, bf16[4,5,48,768]{3,2,1,0:T(8,128)(2,1)}, u32[]{:S(2)}, u32[]{:S(2)}) collective-permute-start(bf16[4,5,48,768]{3,2,1,0:T(8,128)(2,1)} %fusion.7.refs_3_), channel_id=1, source_target_pairs={{0,1},{1,32},{2,3},{3,34},{4,5},{5,36},{6,7},{7,38},{8,9},{9,40},{... | collective-permute-start | bytes 4423688 | tf_op jit(solution)/shard_map/conv_second/ppermute | solution.py:36
  50.2 21.2 %copy-start.21 = (f32[1536]{0:T(1024)S(1)}, f32[1536]{0:T(1024)}, u32[]{:S(2)}) copy-start(f32[1536]{0:T(1024)} %param.10) | copy-start | bytes 18436
  67.6 8.0 %copy-start.2 = (bf16[4,4,48,768]{3,2,1,0:T(8,128)(2,1)}, bf16[4,4,48,768]{3,2,1,0:T(8,128)(2,1)S(1)}, u32[]{:S(2)}) copy-start(bf16[4,4,48,768]{3,2,1,0:T(8,128)(2,1)S(1)} %fusion.11.g0) | copy-start | bytes 3538948
  67.6 23.5 %collective-permute-start.13 = (bf16[4,4,48,768]{3,2,1,0:T(8,128)(2,1)S(1)}, bf16[4,4,48,768]{3,2,1,0:T(8,128)(2,1)S(1)}, u32[]{:S(2)}, u32[]{:S(2)}) collective-permute-start(bf16[4,4,48,768]{3,2,1,0:T(8,128)(2,1)S(1)} %fusion.11.g0), channel_id=1, source_target_pairs={{0,1},{1,32},{2,3},{3,34},{4,5},{5,36},{6,7},{7,38},{8,9},{9,40},{... | collective-permute-start | bytes 3538952 | tf_op jit(solution)/shard_map/qkv_second/ppermute | solution.py:36
  68.7 23.5 %collective-permute-start.14 = (bf16[4,4,48,768]{3,2,1,0:T(8,128)(2,1)S(1)}, bf16[4,4,48,768]{3,2,1,0:T(8,128)(2,1)}, u32[]{:S(2)}, u32[]{:S(2)}) collective-permute-start(bf16[4,4,48,768]{3,2,1,0:T(8,128)(2,1)S(1)} %fusion.11.g0), channel_id=1, source_target_pairs={{0,33},{1,0},{2,35},{3,2},{4,37},{5,4},{6,39},{7,6},{8,41},{9,8},{... | collective-permute-start | bytes 3538952 | tf_op jit(solution)/shard_map/qkv_second/ppermute | solution.py:36
  72.5 2.1 %copy-start.13 = (bf16[4,5,48,768]{3,2,1,0:T(8,128)(2,1)S(1)}, bf16[4,5,48,768]{3,2,1,0:T(8,128)(2,1)}, u32[]{:S(2)}) copy-start(bf16[4,5,48,768]{3,2,1,0:T(8,128)(2,1)} %copy-done.12) | copy-start | bytes 4423684
  74.7 22.0 %collective-permute-start.9 = (bf16[2,5,48,768]{3,2,1,0:T(8,128)(2,1)}, bf16[2,5,48,768]{3,2,1,0:T(8,128)(2,1)}, u32[]{:S(2)}, u32[]{:S(2)}) collective-permute-start(bf16[2,5,48,768]{3,2,1,0:T(8,128)(2,1)} %slice.158), channel_id=1, source_target_pairs={{0,1},{1,32},{2,3},{3,34},{4,5},{5,36},{6,7},{7,38},{8,9},{9,40},{... | collective-permute-start | bytes 2211848 | tf_op jit(solution)/shard_map/conv_far/ppermute | solution.py:36
  75.6 21.0 %collective-permute-start.10 = (bf16[2,5,48,768]{3,2,1,0:T(8,128)(2,1)}, bf16[2,5,48,768]{3,2,1,0:T(8,128)(2,1)}, u32[]{:S(2)}, u32[]{:S(2)}) collective-permute-start(bf16[2,5,48,768]{3,2,1,0:T(8,128)(2,1)} %slice.159), channel_id=1, source_target_pairs={{0,33},{1,0},{2,35},{3,2},{4,37},{5,4},{6,39},{7,6},{8,41},{9,8},{... | collective-permute-start | bytes 2211848 | tf_op jit(solution)/shard_map/conv_far/ppermute | solution.py:36
  91.1 13.7 %collective-permute-start.11 = (bf16[12,48,512]{2,1,0:T(8,128)(2,1)}, bf16[12,48,512]{2,1,0:T(8,128)(2,1)}, u32[]{:S(2)}, u32[]{:S(2)}) collective-permute-start(bf16[12,48,512]{2,1,0:T(8,128)(2,1)} %conv_kernel.2.refs_3_.ma), channel_id=1, source_target_pairs={{0,16},{1,17},{2,18},{3,19},{4,20},{5,21},{6,22},{7,23},{8,24},{9,... | collective-permute-start | bytes 1769480 | tf_op jit(solution)/shard_map/pooled_core/ppermute | solution.py:36
  91.2 12.0 %copy-start.4 = (bf16[4,4,48,768]{3,2,1,0:T(8,128)(2,1)}, bf16[4,4,48,768]{3,2,1,0:T(8,128)(2,1)S(1)}, u32[]{:S(2)}) copy-start(bf16[4,4,48,768]{3,2,1,0:T(8,128)(2,1)S(1)} %collective-permute-done.13.g1) | copy-start | bytes 3538948
  92.2 12.8 %collective-permute-start.15 = (bf16[2,4,48,768]{3,2,1,0:T(8,128)(2,1)}, bf16[2,4,48,768]{3,2,1,0:T(8,128)(2,1)}, u32[]{:S(2)}, u32[]{:S(2)}) collective-permute-start(bf16[2,4,48,768]{3,2,1,0:T(8,128)(2,1)} %slice.165), channel_id=1, source_target_pairs={{0,1},{1,32},{2,3},{3,34},{4,5},{5,36},{6,7},{7,38},{8,9},{9,40},{... | collective-permute-start | bytes 1769480 | tf_op jit(solution)/shard_map/qkv_far/ppermute | solution.py:36
  93.3 10.0 %copy-start.20 = (f32[1536]{0:T(1024)S(1)}, f32[1536]{0:T(1024)}, u32[]{:S(2)}) copy-start(f32[1536]{0:T(1024)} %param.11) | copy-start | bytes 18436
  93.3 11.6 %collective-permute-start.16 = (bf16[2,4,48,768]{3,2,1,0:T(8,128)(2,1)S(1)}, bf16[2,4,48,768]{3,2,1,0:T(8,128)(2,1)S(1)}, u32[]{:S(2)}, u32[]{:S(2)}) collective-permute-start(bf16[2,4,48,768]{3,2,1,0:T(8,128)(2,1)S(1)} %slice.166), channel_id=1, source_target_pairs={{0,33},{1,0},{2,35},{3,2},{4,37},{5,4},{6,39},{7,6},{8,41},{9,8},{... | collective-permute-start | bytes 1769480 | tf_op jit(solution)/shard_map/qkv_far/ppermute | solution.py:36
  103.2 1.7 collective-permute-start.12
  115.2 26.0 %copy-start.11 = (bf16[4,192,256]{2,1,0:T(8,128)(2,1)S(1)}, bf16[4,192,256]{2,1,0:T(8,128)(2,1)}, u32[]{:S(2)}) copy-start(bf16[4,192,256]{2,1,0:T(8,128)(2,1)} %get-tuple-element.12) | copy-start | bytes 1179652
  116.5 16.2 %collective-permute-start.17 = (bf16[2,192,256]{2,1,0:T(8,128)(2,1)S(1)}, bf16[2,192,256]{2,1,0:T(8,128)(2,1)S(1)}, u32[]{:S(2)}, u32[]{:S(2)}) collective-permute-start(bf16[2,192,256]{2,1,0:T(8,128)(2,1)S(1)} %get-tuple-element.22), channel_id=1, source_target_pairs={{0,4},{1,5},{2,20},{3,21},{4,8},{5,9},{6,24},{7,25},{8,12},{9,13},... | collective-permute-start | bytes 589832 | tf_op jit(solution)/shard_map/keys_z/ppermute | solution.py:36
  120.0 16.5 %collective-permute-start.24 = (bf16[2,192,256]{2,1,0:T(8,128)(2,1)S(1)}, bf16[2,192,256]{2,1,0:T(8,128)(2,1)S(1)}, u32[]{:S(2)}, u32[]{:S(2)}) collective-permute-start(bf16[2,192,256]{2,1,0:T(8,128)(2,1)S(1)} %get-tuple-element.20), channel_id=1, source_target_pairs={{0,8},{1,9},{2,24},{3,25},{4,12},{5,13},{6,28},{7,29},{8,0},{9,1},... | collective-permute-start | bytes 589832 | tf_op jit(solution)/shard_map/keys_z/ppermute | solution.py:36
  124.7 11.8 %collective-permute-start.23 = (bf16[2,192,256]{2,1,0:T(8,128)(2,1)S(1)}, bf16[2,192,256]{2,1,0:T(8,128)(2,1)S(1)}, u32[]{:S(2)}, u32[]{:S(2)}) collective-permute-start(bf16[2,192,256]{2,1,0:T(8,128)(2,1)S(1)} %get-tuple-element.21), channel_id=1, source_target_pairs={{0,0},{1,1},{2,16},{3,17},{4,4},{5,5},{6,20},{7,21},{8,8},{9,9},{1... | collective-permute-start | bytes 589832 | tf_op jit(solution)/shard_map/keys_z/ppermute | solution.py:36
  125.3 14.4 %collective-permute-start.22 = (bf16[2,192,256]{2,1,0:T(8,128)(2,1)S(1)}, bf16[2,192,256]{2,1,0:T(8,128)(2,1)S(1)}, u32[]{:S(2)}, u32[]{:S(2)}) collective-permute-start(bf16[2,192,256]{2,1,0:T(8,128)(2,1)S(1)} %get-tuple-element.19), channel_id=1, source_target_pairs={{0,12},{1,13},{2,28},{3,29},{4,0},{5,1},{6,16},{7,17},{8,4},{9,5},... | collective-permute-start | bytes 589832 | tf_op jit(solution)/shard_map/keys_z/ppermute | solution.py:36
  139.8 21.5 %copy-start.9 = (bf16[4,2,192,256]{3,2,1,0:T(8,128)(2,1)}, bf16[4,2,192,256]{3,2,1,0:T(8,128)(2,1)S(1)}, u32[]{:S(2)}) copy-start(bf16[4,2,192,256]{3,2,1,0:T(8,128)(2,1)S(1)} %pad_maximum_fusion.g0) | copy-start | bytes 2359300
  139.8 20.4 %collective-permute-start.25 = (bf16[4,2,192,256]{3,2,1,0:T(8,128)(2,1)S(1)}, bf16[4,2,192,256]{3,2,1,0:T(8,128)(2,1)S(1)}, u32[]{:S(2)}, u32[]{:S(2)}) collective-permute-start(bf16[4,2,192,256]{3,2,1,0:T(8,128)(2,1)S(1)} %pad_maximum_fusion.g0), channel_id=1, source_target_pairs={{0,1},{1,0},{2,3},{3,2},{4,5},{5,4},{6,7},{7,6},{8,9},{9,8},{10,11... | collective-permute-start | bytes 2359304 | tf_op jit(solution)/shard_map/keys_y/ppermute | solution.py:36
  141.2 20.9 %copy-start.1 = (bf16[16,48,768]{2,1,0:T(8,128)(2,1)S(1)}, bf16[16,48,768]{2,1,0:T(8,128)(2,1)}, u32[]{:S(2)}) copy-start(bf16[16,48,768]{2,1,0:T(8,128)(2,1)} %get-tuple-element.18.mine) | copy-start | bytes 3538948
  141.3 10.7 %collective-permute-start.18 = (bf16[192,256]{1,0:T(8,128)(2,1)S(1)}, bf16[192,256]{1,0:T(8,128)(2,1)S(1)}, u32[]{:S(2)}, u32[]{:S(2)}) collective-permute-start(bf16[192,256]{1,0:T(8,128)(2,1)S(1)} %get-tuple-element.29), channel_id=1, source_target_pairs={{0,4},{1,5},{2,20},{3,21},{4,8},{5,9},{6,24},{7,25},{8,12},{9,13},... | collective-permute-start | bytes 294920 | tf_op jit(solution)/shard_map/queries_z/ppermute | solution.py:36
  144.6 11.5 %collective-permute-start.19 = (bf16[192,256]{1,0:T(8,128)(2,1)S(1)}, bf16[192,256]{1,0:T(8,128)(2,1)S(1)}, u32[]{:S(2)}, u32[]{:S(2)}) collective-permute-start(bf16[192,256]{1,0:T(8,128)(2,1)S(1)} %get-tuple-element.32), channel_id=1, source_target_pairs={{0,12},{1,13},{2,28},{3,29},{4,0},{5,1},{6,16},{7,17},{8,4},{9,5},... | collective-permute-start | bytes 294920 | tf_op jit(solution)/shard_map/queries_z/ppermute | solution.py:36
  145.9 11.9 %collective-permute-start.20 = (bf16[192,256]{1,0:T(8,128)(2,1)S(1)}, bf16[192,256]{1,0:T(8,128)(2,1)S(1)}, u32[]{:S(2)}, u32[]{:S(2)}) collective-permute-start(bf16[192,256]{1,0:T(8,128)(2,1)S(1)} %get-tuple-element.31), channel_id=1, source_target_pairs={{0,0},{1,1},{2,16},{3,17},{4,4},{5,5},{6,20},{7,21},{8,8},{9,9},{1... | collective-permute-start | bytes 294920 | tf_op jit(solution)/shard_map/queries_z/ppermute | solution.py:36
  146.6 12.4 %collective-permute-start.21 = (bf16[192,256]{1,0:T(8,128)(2,1)S(1)}, bf16[192,256]{1,0:T(8,128)(2,1)S(1)}, u32[]{:S(2)}, u32[]{:S(2)}) collective-permute-start(bf16[192,256]{1,0:T(8,128)(2,1)S(1)} %get-tuple-element.30), channel_id=1, source_target_pairs={{0,8},{1,9},{2,24},{3,25},{4,12},{5,13},{6,28},{7,29},{8,0},{9,1},... | collective-permute-start | bytes 294920 | tf_op jit(solution)/shard_map/queries_z/ppermute | solution.py:36
  152.0 11.1 %collective-permute-start.27 = (bf16[4,2,192,256]{3,2,1,0:T(8,128)(2,1)S(1)}, bf16[4,2,192,256]{3,2,1,0:T(8,128)(2,1)S(1)}, u32[]{:S(2)}, u32[]{:S(2)}) collective-permute-start(bf16[4,2,192,256]{3,2,1,0:T(8,128)(2,1)S(1)} %pad_maximum_fusion.g0), channel_id=1, source_target_pairs={{0,16},{1,17},{2,18},{3,19},{4,20},{5,21},{6,22},{7,23},{8,24},{9,... | collective-permute-start | bytes 2359304 | tf_op jit(solution)/shard_map/keys_core/ppermute | solution.py:36
  160.2 2.0 copy-start.8
  161.3 11.4 %collective-permute-start.26 = (bf16[4,2,192,256]{3,2,1,0:T(8,128)(2,1)}, bf16[4,2,192,256]{3,2,1,0:T(8,128)(2,1)}, u32[]{:S(2)}, u32[]{:S(2)}) collective-permute-start(bf16[4,2,192,256]{3,2,1,0:T(8,128)(2,1)} %broadcast_add_fusion.1), channel_id=1, source_target_pairs={{0,16},{1,17},{2,18},{3,19},{4,20},{5,21},{6,22},{7,23},{8,24},{9,... | collective-permute-start | bytes 2359304 | tf_op jit(solution)/shard_map/keys_y_core/ppermute | solution.py:36
  162.2 32.9 %collective-permute-start.32 = (bf16[16,48,768]{2,1,0:T(8,128)(2,1)S(1)}, bf16[16,48,768]{2,1,0:T(8,128)(2,1)S(1)}, u32[]{:S(2)}, u32[]{:S(2)}) collective-permute-start(bf16[16,48,768]{2,1,0:T(8,128)(2,1)S(1)} %broadcast_add_fusion), channel_id=1, source_target_pairs={{0,16},{1,17},{2,18},{3,19},{4,20},{5,21},{6,22},{7,23},{8,24},{9,... | collective-permute-start | bytes 3538952 | tf_op jit(solution)/shard_map/out_core/ppermute | solution.py:36
  183.2 11.9 %collective-permute-start.28 = (bf16[192,256]{1,0:T(8,128)(2,1)S(1)}, bf16[192,256]{1,0:T(8,128)(2,1)S(1)}, u32[]{:S(2)}, u32[]{:S(2)}) collective-permute-start(bf16[192,256]{1,0:T(8,128)(2,1)S(1)} %get-tuple-element.28), channel_id=1, source_target_pairs={{0,4},{1,5},{2,8},{3,9},{4,16},{5,17},{6,20},{7,21},{8,12},{9,13},... | collective-permute-start | bytes 294920 | tf_op jit(solution)/shard_map/heads_back/ppermute | solution.py:36
  185.6 9.4 %collective-permute-start.29 = (bf16[192,256]{1,0:T(8,128)(2,1)S(1)}, bf16[192,256]{1,0:T(8,128)(2,1)S(1)}, u32[]{:S(2)}, u32[]{:S(2)}) collective-permute-start(bf16[192,256]{1,0:T(8,128)(2,1)S(1)} %get-tuple-element.27), channel_id=1, source_target_pairs={{0,12},{1,13},{2,0},{3,1},{4,28},{5,29},{6,24},{7,25},{8,4},{9,5},... | collective-permute-start | bytes 294920 | tf_op jit(solution)/shard_map/heads_back/ppermute | solution.py:36
  189.2 5.9 %collective-permute-start.30 = (bf16[192,256]{1,0:T(8,128)(2,1)S(1)}, bf16[192,256]{1,0:T(8,128)(2,1)S(1)}, u32[]{:S(2)}, u32[]{:S(2)}) collective-permute-start(bf16[192,256]{1,0:T(8,128)(2,1)S(1)} %get-tuple-element.26), channel_id=1, source_target_pairs={{0,0},{1,1},{2,12},{3,13},{4,24},{5,25},{6,28},{7,29},{8,8},{9,9},... | collective-permute-start | bytes 294920 | tf_op jit(solution)/shard_map/heads_back/ppermute | solution.py:36
  189.9 11.2 %collective-permute-start.31 = (bf16[192,256]{1,0:T(8,128)(2,1)S(1)}, bf16[192,256]{1,0:T(8,128)(2,1)S(1)}, u32[]{:S(2)}, u32[]{:S(2)}) collective-permute-start(bf16[192,256]{1,0:T(8,128)(2,1)S(1)} %get-tuple-element.25), channel_id=1, source_target_pairs={{0,8},{1,9},{2,4},{3,5},{4,20},{5,21},{6,16},{7,17},{8,0},{9,1},{1... | collective-permute-start | bytes 294920 | tf_op jit(solution)/shard_map/heads_back/ppermute | solution.py:36
  195.1 6.0 %copy-start.5 = (bf16[16,48,768]{2,1,0:T(8,128)(2,1)}, bf16[16,48,768]{2,1,0:T(8,128)(2,1)S(1)}, u32[]{:S(2)}) copy-start(bf16[16,48,768]{2,1,0:T(8,128)(2,1)S(1)} %collective-permute-done.32.theirs) | copy-start | bytes 3538948
  195.1 6.0 %copy-start.15 = (bf16[192,256]{1,0:T(8,128)(2,1)}, bf16[192,256]{1,0:T(8,128)(2,1)S(1)}, u32[]{:S(2)}) copy-start(bf16[192,256]{1,0:T(8,128)(2,1)S(1)} %collective-permute-done.28.h0) | copy-start | bytes 294916
  195.1 6.0 %copy-start.16 = (bf16[192,256]{1,0:T(8,128)(2,1)}, bf16[192,256]{1,0:T(8,128)(2,1)S(1)}, u32[]{:S(2)}) copy-start(bf16[192,256]{1,0:T(8,128)(2,1)S(1)} %collective-permute-done.29.h1) | copy-start | bytes 294916
  195.1 5.9 %copy-start.17 = (bf16[192,256]{1,0:T(8,128)(2,1)}, bf16[192,256]{1,0:T(8,128)(2,1)S(1)}, u32[]{:S(2)}) copy-start(bf16[192,256]{1,0:T(8,128)(2,1)S(1)} %collective-permute-done.30.h2) | copy-start | bytes 294916
  (8 other events, 7.6 us)

commit v6 on v5

--- a/solution.py
+++ b/solution.py
@@ -140,6 +140,10 @@
 
 
 TABLE = np.array([integers(i) for i in range(256)], np.int32)
+
+
+def column(row):
+    return jnp.broadcast_to(row, (8, row.shape[1])).T[:, :1]
 
 
 def nt(a, b):
@@ -223,7 +227,7 @@
         spread = sum(jnp.sum(v * v, axis=0, keepdims=True) for v in values) / 1536.0
         rate = lax.rsqrt(spread + 1e-05)
         for half in range(2):
-            normed[part, half] = (values[half] * rate * gain[half]).astype(BF16)
+            normed[part, half] = (values[half] * rate * column(gain[half])).astype(BF16)
         return 0
 
     lax.fori_loop(0, 2, norm, 0)
@@ -421,7 +425,7 @@
         table,
         *mine,
         *theirs,
-        norm_gain.reshape(2, 768, 1),
+        norm_gain.reshape(2, 1, 768),
         *qkv_groups,
     )
 

time: 208 us -> 209 us (level)
    unnamed x46 -> x52, local copies, waits for them, and re-layouts: 4.06 us -> 5.02 us
where the time goes in v6:
time: 209 us; the launch traced here: 206 us
  starting transfers between devices  66 us (32%)
  Pallas kernels  57 us (27%)
  waiting for transfers between devices  43.6 us (21%)
  local copies, waits for them, and re-layouts  28.6 us (14%)
  between operations  6.52 us (3%)
  other arithmetic  4.17 us (2%)
    ppermute x31, starting transfers between devices, send(): return lax.ppermute(value, AXES, pairs)  60.1 us
    pallas_call x8, Pallas kernels, call(): pl.pallas_call(kernel, out_shape=outs, in_specs=ins, out_specs=jax.tree.m...  57 us
    ppermute x31, waiting for transfers between devices, send(): return lax.ppermute(value, AXES, pairs)  42.4 us
    slice x9, local copies, waits for them, and re-layouts, after(): zero = sum((o[(0,) * o.ndim].astype(F32) * 0.0 for o in others), F32(0.0))  5.51 us
    unnamed x52, local copies, waits for them, and re-layouts  5.02 us
    ppermute x1, starting transfers between devices, shards(): before = lax.ppermute(activated[-2:], AXES, forward)  4.55 us
  transfers between devices with their start and end apart: 33, of which 9 were waited for; matrix products, arithmetic and copies ran while one was open for 12% of the time, Pallas kernels for 22%

profile of v6, /device:TPU:6, one launch (start us, length us, event | category | flops | bytes accessed | tf_op | source)
XLA Modules:
  0.0 205.8 jit_solution(5492709444486380550)
XLA Ops:
  0.0 1.1 dynamic-slice_bitcast_fusion.1
  1.4 6.5 %collective-permute-start.3 = (bf16[9,48,768]{2,1,0:T(8,128)(2,1)S(1)}, bf16[9,48,768]{2,1,0:T(8,128)(2,1)S(1)}, u32[]{:S(2)}, u32[]{:S(2)}) collective-permute-start(bf16[9,48,768]{2,1,0:T(8,128)(2,1)S(1)} %pad_maximum_fusion.1), channel_id=1, source_target_pairs={{0,4},{1,5},{2,2},{3,3},{4,6},{5,7},{6,0},{7,1},{8,18},{9,19},{10,... | collective-permute-start | bytes 1990664 | tf_op jit(solution)/shard_map/weights_z/ppermute | solution.py:36
  9.7 1.3 collective-permute-start.1
  11.0 4.5 %collective-permute-start = (bf16[2,768]{1,0:T(2,128)(2,1)S(1)}, bf16[2,768]{1,0:T(2,128)(2,1)S(1)}, u32[]{:S(2)}, u32[]{:S(2)}) collective-permute-start(bf16[2,768]{1,0:T(2,128)(2,1)S(1)} %get-tuple-element.23), channel_id=1, source_target_pairs={{0,1},{1,2},{2,3},{3,4},{4,5},{5,6},{6,7},{7,8},{8,9},{9,10},{10,1... | collective-permute-start | bytes 9224 | tf_op jit(solution)/shard_map/ppermute | solution.py:362
  15.7 1.2 collective-permute-done
  17.2 1.2 collective-permute-start.2
  18.4 4.5 %collective-permute-done.3 = bf16[9,48,768]{2,1,0:T(8,128)(2,1)S(1)} collective-permute-done((bf16[9,48,768]{2,1,0:T(8,128)(2,1)S(1)}, bf16[9,48,768]{2,1,0:T(8,128)(2,1)S(1)}, u32[]{:S(2)}, u32[]{:S(2)}) %collective-permute-start.3) | collective-permute-done | bytes 663584 | tf_op jit(solution)/shard_map/weights_z/ppermute | solution.py:36
  22.8 2.9 %collective-permute-start.5 = (bf16[9,48,768]{2,1,0:T(8,128)(2,1)S(1)}, bf16[9,48,768]{2,1,0:T(8,128)(2,1)S(1)}, u32[]{:S(2)}, u32[]{:S(2)}) collective-permute-start(bf16[9,48,768]{2,1,0:T(8,128)(2,1)S(1)} %collective-permute-done.3), channel_id=1, source_target_pairs={{0,192},{1,193},{2,194},{3,195},{4,196},{5,197},{6,198},{7,199},{8... | collective-permute-start | bytes 1990664 | tf_op jit(solution)/shard_map/weights_first/ppermute | solution.py:36
  27.0 6.5 %acts_kernel.1.refs_1_ = bf16[6,768,512]{2,1,0:T(8,128)(2,1)} custom-call(bf16[528,768]{1,0:T(8,128)(2,1)} %copy-done.2, bf16[528,768]{1,0:T(8,128)(2,1)} %copy-done.6), custom_call_target="tpu_custom_call" | custom-call | flops 1000000000 | bytes 8000000 | tf_op jit(solution)/shard_map/acts_kernel/pallas_call | solution.py:331
  33.5 1.2 slice.157
  36.5 5.4 %collective-permute-done.5 = bf16[9,48,768]{2,1,0:T(8,128)(2,1)S(1)} collective-permute-done((bf16[9,48,768]{2,1,0:T(8,128)(2,1)S(1)}, bf16[9,48,768]{2,1,0:T(8,128)(2,1)S(1)}, u32[]{:S(2)}, u32[]{:S(2)}) %collective-permute-start.5) | collective-permute-done | bytes 663584 | tf_op jit(solution)/shard_map/weights_first/ppermute | solution.py:36
  41.9 1.2 fusion.8
  43.2 4.0 %collective-permute-start.8 = (bf16[4,5,48,768]{3,2,1,0:T(8,128)(2,1)S(1)}, bf16[4,5,48,768]{3,2,1,0:T(8,128)(2,1)S(1)}, u32[]{:S(2)}, u32[]{:S(2)}) collective-permute-start(bf16[4,5,48,768]{3,2,1,0:T(8,128)(2,1)S(1)} %fusion.7.refs_3_), channel_id=1, source_target_pairs={{0,33},{1,0},{2,35},{3,2},{4,37},{5,4},{6,39},{7,6},{8,41},{9,8},{... | collective-permute-start | bytes 4423688 | tf_op jit(solution)/shard_map/conv_second/ppermute | solution.py:36
  50.3 13.8 %collective-permute-done.8.refs_5_ = bf16[4,5,48,768]{3,2,1,0:T(8,128)(2,1)S(1)} collective-permute-done((bf16[4,5,48,768]{3,2,1,0:T(8,128)(2,1)S(1)}, bf16[4,5,48,768]{3,2,1,0:T(8,128)(2,1)S(1)}, u32[]{:S(2)}, u32[]{:S(2)}) %collective-permute-start.8) | collective-permute-done | bytes 1474592 | tf_op jit(solution)/shard_map/conv_second/ppermute | solution.py:36
  66.4 1.1 collective-permute-start.13
  67.5 2.7 %collective-permute-start.14 = (bf16[4,4,48,768]{3,2,1,0:T(8,128)(2,1)S(1)}, bf16[4,4,48,768]{3,2,1,0:T(8,128)(2,1)}, u32[]{:S(2)}, u32[]{:S(2)}) collective-permute-start(bf16[4,4,48,768]{3,2,1,0:T(8,128)(2,1)S(1)} %fusion.11.g0), channel_id=1, source_target_pairs={{0,33},{1,0},{2,35},{3,2},{4,37},{5,4},{6,39},{7,6},{8,41},{9,8},{... | collective-permute-start | bytes 3538952 | tf_op jit(solution)/shard_map/qkv_second/ppermute | solution.py:36
  70.3 1.0 reshape.44.refs_2_
  71.3 2.1 %slice.158 = bf16[2,5,48,768]{3,2,1,0:T(8,128)(2,1)} slice(bf16[4,5,48,768]{3,2,1,0:T(8,128)(2,1)} %collective-permute-done.7.refs_4_), slice={[0:2], [0:5], [0:48], [0:768]} | slice | bytes 1474560 | tf_op jit(solution)/shard_map/slice | solution.py:379
  74.4 3.2 %collective-permute-start.10 = (bf16[2,5,48,768]{3,2,1,0:T(8,128)(2,1)}, bf16[2,5,48,768]{3,2,1,0:T(8,128)(2,1)S(1)}, u32[]{:S(2)}, u32[]{:S(2)}) collective-permute-start(bf16[2,5,48,768]{3,2,1,0:T(8,128)(2,1)} %slice.159), channel_id=1, source_target_pairs={{0,33},{1,0},{2,35},{3,2},{4,37},{5,4},{6,39},{7,6},{8,41},{9,8},{... | collective-permute-start | bytes 2211848 | tf_op jit(solution)/shard_map/conv_far/ppermute | solution.py:36
  77.6 1.2 fusion.14.refs_0_.table
  78.9 11.0 %conv_kernel.2.refs_3_.ma = bf16[12,48,512]{2,1,0:T(8,128)(2,1)} custom-call(s32[50]{0:T(128)} %fusion.14.refs_0_.table, bf16[6,768,512]{2,1,0:T(8,128)(2,1)} %acts_kernel.1.refs_1_, f32[16,48,1]{2,1,0:T(8,128)} %reshape.44.refs_2_, bf16[4,5,48,768]{3,2,1,0:T(8,128)(2,1)} %copy-done.3, bf16[4,5,48,768]{3,2,1,0:T(8,128)(2,1)} %collective-permute-done.7.refs_4_, ...), custom_call_target="tpu_custom_call" | custom-call | flops 4499999744 | bytes 8000000 | tf_op jit(solution)/shard_map/conv_kernel/pallas_call | solution.py:331
  90.0 2.0 slice.165
  92.0 1.1 slice.166
  93.1 3.3 %collective-permute-start.16 = (bf16[2,4,48,768]{3,2,1,0:T(8,128)(2,1)S(1)}, bf16[2,4,48,768]{3,2,1,0:T(8,128)(2,1)}, u32[]{:S(2)}, u32[]{:S(2)}) collective-permute-start(bf16[2,4,48,768]{3,2,1,0:T(8,128)(2,1)S(1)} %slice.166), channel_id=1, source_target_pairs={{0,33},{1,0},{2,35},{3,2},{4,37},{5,4},{6,39},{7,6},{8,41},{9,8},{... | collective-permute-start | bytes 1769480 | tf_op jit(solution)/shard_map/qkv_far/ppermute | solution.py:36
  98.1 6.6 %conv_kernel.3.mb = bf16[4,48,512]{2,1,0:T(8,128)(2,1)} custom-call(s32[50]{0:T(128)} %fusion.14.refs_0_.table, bf16[6,768,512]{2,1,0:T(8,128)(2,1)} %acts_kernel.1.refs_1_, f32[16,48,1]{2,1,0:T(8,128)} %reshape.44.refs_2_, bf16[12,48,512]{2,1,0:T(8,128)(2,1)} %conv_kernel.2.refs_3_.ma, bf16[2,5,48,768]{3,2,1,0:T(8,128)(2,1)} %copy-done.10, ...), custom_call_target="tpu_custom_call" | custom-call | flops 1500000000 | bytes 8000000 | tf_op jit(solution)/shard_map/conv_kernel/pallas_call | solution.py:331
  105.4 1.0 collective-permute-done.12.tb
  107.2 8.5 %project_kernel.1 = (bf16[4,2,192,256]{3,2,1,0:T(8,128)(2,1)}, bf16[4,192,256]{2,1,0:T(8,128)(2,1)}, bf16[16,48,768]{2,1,0:T(8,128)(2,1)}, bf16[2,16,48,512]{3,2,1,0:T(8,128)(2,1)}) custom-call(s32[50]{0:T(128)} %fusion.14.refs_0_.table, bf16[12,48,512]{2,1,0:T(8,128)(2,1)} %conv_kernel.2.refs_3_.ma, bf16[4,48,512]{2,1,0:T(8,128)(2,1)} %conv_kernel.3.mb, ...), custom_call_target="tpu_custom_call" | custom-call | flops 1800000000 | bytes 8000000 | tf_op jit(solution)/shard_map/project_kernel/pallas_call | solution.py:331
  115.7 1.3 slice_bitcast_fusion.8
  117.0 3.5 %collective-permute-start.17 = (bf16[2,192,256]{2,1,0:T(8,128)(2,1)S(1)}, bf16[2,192,256]{2,1,0:T(8,128)(2,1)S(1)}, u32[]{:S(2)}, u32[]{:S(2)}) collective-permute-start(bf16[2,192,256]{2,1,0:T(8,128)(2,1)S(1)} %get-tuple-element.22), channel_id=1, source_target_pairs={{0,4},{1,5},{2,20},{3,21},{4,8},{5,9},{6,24},{7,25},{8,12},{9,13},... | collective-permute-start | bytes 589832 | tf_op jit(solution)/shard_map/keys_z/ppermute | solution.py:36
  120.5 4.6 %collective-permute-start.24 = (bf16[2,192,256]{2,1,0:T(8,128)(2,1)S(1)}, bf16[2,192,256]{2,1,0:T(8,128)(2,1)S(1)}, u32[]{:S(2)}, u32[]{:S(2)}) collective-permute-start(bf16[2,192,256]{2,1,0:T(8,128)(2,1)S(1)} %get-tuple-element.20), channel_id=1, source_target_pairs={{0,8},{1,9},{2,24},{3,25},{4,12},{5,13},{6,28},{7,29},{8,0},{9,1},... | collective-permute-start | bytes 589832 | tf_op jit(solution)/shard_map/keys_z/ppermute | solution.py:36
  125.8 2.6 %collective-permute-start.22 = (bf16[2,192,256]{2,1,0:T(8,128)(2,1)S(1)}, bf16[2,192,256]{2,1,0:T(8,128)(2,1)S(1)}, u32[]{:S(2)}, u32[]{:S(2)}) collective-permute-start(bf16[2,192,256]{2,1,0:T(8,128)(2,1)S(1)} %get-tuple-element.19), channel_id=1, source_target_pairs={{0,12},{1,13},{2,28},{3,29},{4,0},{5,1},{6,16},{7,17},{8,4},{9,5},... | collective-permute-start | bytes 589832 | tf_op jit(solution)/shard_map/keys_z/ppermute | solution.py:36
  128.5 4.7 %collective-permute-done.17 = bf16[2,192,256]{2,1,0:T(8,128)(2,1)S(1)} collective-permute-done((bf16[2,192,256]{2,1,0:T(8,128)(2,1)S(1)}, bf16[2,192,256]{2,1,0:T(8,128)(2,1)S(1)}, u32[]{:S(2)}, u32[]{:S(2)}) %collective-permute-start.17) | collective-permute-done | bytes 196640 | tf_op jit(solution)/shard_map/keys_z/ppermute | solution.py:36
  133.2 4.0 %collective-permute-done.24 = bf16[2,192,256]{2,1,0:T(8,128)(2,1)S(1)} collective-permute-done((bf16[2,192,256]{2,1,0:T(8,128)(2,1)S(1)}, bf16[2,192,256]{2,1,0:T(8,128)(2,1)S(1)}, u32[]{:S(2)}, u32[]{:S(2)}) %collective-permute-start.24) | collective-permute-done | bytes 196640 | tf_op jit(solution)/shard_map/keys_z/ppermute | solution.py:36
  137.2 2.9 %collective-permute-done.22 = bf16[2,192,256]{2,1,0:T(8,128)(2,1)S(1)} collective-permute-done((bf16[2,192,256]{2,1,0:T(8,128)(2,1)S(1)}, bf16[2,192,256]{2,1,0:T(8,128)(2,1)S(1)}, u32[]{:S(2)}, u32[]{:S(2)}) %collective-permute-start.22) | collective-permute-done | bytes 196640 | tf_op jit(solution)/shard_map/keys_z/ppermute | solution.py:36
  141.6 3.4 %collective-permute-start.18 = (bf16[192,256]{1,0:T(8,128)(2,1)S(1)}, bf16[192,256]{1,0:T(8,128)(2,1)S(1)}, u32[]{:S(2)}, u32[]{:S(2)}) collective-permute-start(bf16[192,256]{1,0:T(8,128)(2,1)S(1)} %get-tuple-element.29), channel_id=1, source_target_pairs={{0,4},{1,5},{2,20},{3,21},{4,8},{5,9},{6,24},{7,25},{8,12},{9,13},... | collective-permute-start | bytes 294920 | tf_op jit(solution)/shard_map/queries_z/ppermute | solution.py:36
  145.1 1.1 collective-permute-start.19
  146.8 5.1 %collective-permute-start.21 = (bf16[192,256]{1,0:T(8,128)(2,1)S(1)}, bf16[192,256]{1,0:T(8,128)(2,1)S(1)}, u32[]{:S(2)}, u32[]{:S(2)}) collective-permute-start(bf16[192,256]{1,0:T(8,128)(2,1)S(1)} %get-tuple-element.30), channel_id=1, source_target_pairs={{0,8},{1,9},{2,24},{3,25},{4,12},{5,13},{6,28},{7,29},{8,0},{9,1},... | collective-permute-start | bytes 294920 | tf_op jit(solution)/shard_map/queries_z/ppermute | solution.py:36
  151.9 2.7 %collective-permute-start.27 = (bf16[4,2,192,256]{3,2,1,0:T(8,128)(2,1)S(1)}, bf16[4,2,192,256]{3,2,1,0:T(8,128)(2,1)S(1)}, u32[]{:S(2)}, u32[]{:S(2)}) collective-permute-start(bf16[4,2,192,256]{3,2,1,0:T(8,128)(2,1)S(1)} %pad_maximum_fusion.g0), channel_id=1, source_target_pairs={{0,16},{1,17},{2,18},{3,19},{4,20},{5,21},{6,22},{7,23},{8,24},{9,... | collective-permute-start | bytes 2359304 | tf_op jit(solution)/shard_map/keys_core/ppermute | solution.py:36
  160.7 1.0 broadcast_add_fusion.1
  164.2 8.7 %attend_kernel.1 = (f32[4,256,128]{2,1,0:T(8,128)}, f32[4,256,128]{2,1,0:T(8,128)}, f32[4,256,192]{2,1,0:T(8,128)}) custom-call(s32[50]{0:T(128)} %fusion.14.refs_0_.table, f32[4]{0:T(128)} %factor.3, bf16[4,192,256]{2,1,0:T(8,128)(2,1)} %pad_maximum_fusion.2.queries, bf16[4,2,192,256]{3,2,1,0:T(8,128)(2,1)} %copy-done.9, bf16[4,2,192,256]{3,2,1,0:T(8,128)(2,1)} %copy-done.24), custom_call_target="tpu_custom_call" | custom-call | flops 1600000000 | bytes 8000000 | tf_op jit(solution)/shard_map/attend_kernel/pallas_call | solution.py:331
  172.9 9.4 %finish_kernel.1 = bf16[4,192,256]{2,1,0:T(8,128)(2,1)} custom-call(s32[50]{0:T(128)} %fusion.14.refs_0_.table, f32[4]{0:T(128)} %factor.3, bf16[4,192,256]{2,1,0:T(8,128)(2,1)} %pad_maximum_fusion.2.queries, bf16[4,2,192,256]{3,2,1,0:T(8,128)(2,1)} %copy-done.8, bf16[4,2,192,256]{3,2,1,0:T(8,128)(2,1)} %collective-permute-done.26.g1, ...), custom_call_target="tpu_custom_call" | custom-call | flops 1600000000 | bytes 8000000 | tf_op jit(solution)/shard_map/finish_kernel/pallas_call | solution.py:331
  182.3 1.1 slice_bitcast_fusion.10
  183.4 2.5 %collective-permute-start.28 = (bf16[192,256]{1,0:T(8,128)(2,1)S(1)}, bf16[192,256]{1,0:T(8,128)(2,1)S(1)}, u32[]{:S(2)}, u32[]{:S(2)}) collective-permute-start(bf16[192,256]{1,0:T(8,128)(2,1)S(1)} %get-tuple-element.28), channel_id=1, source_target_pairs={{0,4},{1,5},{2,8},{3,9},{4,16},{5,17},{6,20},{7,21},{8,12},{9,13},... | collective-permute-start | bytes 294920 | tf_op jit(solution)/shard_map/heads_back/ppermute | solution.py:36
  185.9 3.6 %collective-permute-start.29 = (bf16[192,256]{1,0:T(8,128)(2,1)S(1)}, bf16[192,256]{1,0:T(8,128)(2,1)S(1)}, u32[]{:S(2)}, u32[]{:S(2)}) collective-permute-start(bf16[192,256]{1,0:T(8,128)(2,1)S(1)} %get-tuple-element.27), channel_id=1, source_target_pairs={{0,12},{1,13},{2,0},{3,1},{4,28},{5,29},{6,24},{7,25},{8,4},{9,5},... | collective-permute-start | bytes 294920 | tf_op jit(solution)/shard_map/heads_back/ppermute | solution.py:36
  190.2 2.5 %collective-permute-start.31 = (bf16[192,256]{1,0:T(8,128)(2,1)S(1)}, bf16[192,256]{1,0:T(8,128)(2,1)S(1)}, u32[]{:S(2)}, u32[]{:S(2)}) collective-permute-start(bf16[192,256]{1,0:T(8,128)(2,1)S(1)} %get-tuple-element.25), channel_id=1, source_target_pairs={{0,8},{1,9},{2,4},{3,5},{4,20},{5,21},{6,16},{7,17},{8,0},{9,1},{1... | collective-permute-start | bytes 294920 | tf_op jit(solution)/shard_map/heads_back/ppermute | solution.py:36
  192.7 2.5 %base_kernel.1.base = bf16[256,1536]{1,0:T(8,128)(2,1)} custom-call(bf16[2,16,48,512]{3,2,1,0:T(8,128)(2,1)} %get-tuple-element.17.tokens), custom_call_target="tpu_custom_call" | custom-call | flops 1000000 | bytes 8000000 | tf_op jit(solution)/shard_map/base_kernel/pallas_call | solution.py:331
  195.3 6.1 %collective-permute-done.31.h3 = bf16[192,256]{1,0:T(8,128)(2,1)S(1)} collective-permute-done((bf16[192,256]{1,0:T(8,128)(2,1)S(1)}, bf16[192,256]{1,0:T(8,128)(2,1)S(1)}, u32[]{:S(2)}, u32[]{:S(2)}) %collective-permute-start.31) | collective-permute-done | bytes 98336 | tf_op jit(solution)/shard_map/heads_back/ppermute | solution.py:36
  202.1 3.8 %out_kernel.1 = bf16[256,1536]{1,0:T(8,128)(2,1)} custom-call(s32[50]{0:T(128)} %fusion.14.refs_0_.table, bf16[192,256]{1,0:T(8,128)(2,1)} %copy-done.17, bf16[192,256]{1,0:T(8,128)(2,1)} %copy-done.18, bf16[192,256]{1,0:T(8,128)(2,1)} %copy-done.19, bf16[192,256]{1,0:T(8,128)(2,1)} %copy-done.20, bf16[256,1536]{1,0:T(8,128)(2,1)} %base_kernel.1.base, ...), custom_call_target="tpu_custom_call" | custom-call | flops 600000000 | bytes 8000000 | tf_op jit(solution)/shard_map/out_kernel/pallas_call | solution.py:331
  (124 shorter events, 21.8 us)
Async XLA Ops:
  0.0 9.1 %copy-start.7 = (bf16[512,768]{1,0:T(8,128)(2,1)S(1)}, bf16[512,768]{1,0:T(8,128)(2,1)}, u32[]{:S(2)}) copy-start(bf16[512,768]{1,0:T(8,128)(2,1)} %param.8) | copy-start | bytes 2359300
  1.4 21.4 %collective-permute-start.3 = (bf16[9,48,768]{2,1,0:T(8,128)(2,1)S(1)}, bf16[9,48,768]{2,1,0:T(8,128)(2,1)S(1)}, u32[]{:S(2)}, u32[]{:S(2)}) collective-permute-start(bf16[9,48,768]{2,1,0:T(8,128)(2,1)S(1)} %pad_maximum_fusion.1), channel_id=1, source_target_pairs={{0,4},{1,5},{2,2},{3,3},{4,6},{5,7},{6,0},{7,1},{8,18},{9,19},{10,... | collective-permute-start | bytes 1990664 | tf_op jit(solution)/shard_map/weights_z/ppermute | solution.py:36
  9.7 5.9 %collective-permute-start.1 = (bf16[2,768]{1,0:T(2,128)(2,1)S(1)}, bf16[2,768]{1,0:T(2,128)(2,1)S(1)}, u32[]{:S(2)}, u32[]{:S(2)}) collective-permute-start(bf16[2,768]{1,0:T(2,128)(2,1)S(1)} %get-tuple-element.24), channel_id=1, source_target_pairs={{1,0},{2,1},{3,2},{4,3},{5,4},{6,5},{7,6},{8,7},{9,8},{10,9},{11,1... | collective-permute-start | bytes 9224 | tf_op jit(solution)/shard_map/ppermute | solution.py:363
  11.0 5.9 %collective-permute-start = (bf16[2,768]{1,0:T(2,128)(2,1)S(1)}, bf16[2,768]{1,0:T(2,128)(2,1)S(1)}, u32[]{:S(2)}, u32[]{:S(2)}) collective-permute-start(bf16[2,768]{1,0:T(2,128)(2,1)S(1)} %get-tuple-element.23), channel_id=1, source_target_pairs={{0,1},{1,2},{2,3},{3,4},{4,5},{5,6},{6,7},{7,8},{8,9},{9,10},{10,1... | collective-permute-start | bytes 9224 | tf_op jit(solution)/shard_map/ppermute | solution.py:362
  17.2 8.9 %copy-start.2 = (bf16[528,768]{1,0:T(8,128)(2,1)}, bf16[528,768]{1,0:T(8,128)(2,1)S(1)}, u32[]{:S(2)}) copy-start(bf16[528,768]{1,0:T(8,128)(2,1)S(1)} %maximum_maximum_fusion.own) | copy-start | bytes 2433028
  17.2 8.9 %collective-permute-start.2 = (bf16[528,768]{1,0:T(8,128)(2,1)S(1)}, bf16[528,768]{1,0:T(8,128)(2,1)S(1)}, u32[]{:S(2)}, u32[]{:S(2)}) collective-permute-start(bf16[528,768]{1,0:T(8,128)(2,1)S(1)} %maximum_maximum_fusion.own), channel_id=1, source_target_pairs={{0,16},{1,17},{2,18},{3,19},{4,20},{5,21},{6,22},{7,23},{8,24},{9,... | collective-permute-start | bytes 2433032 | tf_op jit(solution)/shard_map/acts_core/ppermute | solution.py:36
  22.8 20.3 %copy-start.12 = (bf16[9,48,768]{2,1,0:T(8,128)(2,1)}, bf16[9,48,768]{2,1,0:T(8,128)(2,1)S(1)}, u32[]{:S(2)}) copy-start(bf16[9,48,768]{2,1,0:T(8,128)(2,1)S(1)} %collective-permute-done.3) | copy-start | bytes 1990660
  22.8 12.5 %collective-permute-start.4 = (bf16[9,48,768]{2,1,0:T(8,128)(2,1)S(1)}, bf16[9,48,768]{2,1,0:T(8,128)(2,1)}, u32[]{:S(2)}, u32[]{:S(2)}) collective-permute-start(bf16[9,48,768]{2,1,0:T(8,128)(2,1)S(1)} %collective-permute-done.3), channel_id=1, source_target_pairs={{0,128},{1,129},{2,130},{3,131},{4,132},{5,133},{6,134},{7,135},{8... | collective-permute-start | bytes 1990664 | tf_op jit(solution)/shard_map/weights_first/ppermute | solution.py:36
  22.8 19.0 %collective-permute-start.5 = (bf16[9,48,768]{2,1,0:T(8,128)(2,1)S(1)}, bf16[9,48,768]{2,1,0:T(8,128)(2,1)S(1)}, u32[]{:S(2)}, u32[]{:S(2)}) collective-permute-start(bf16[9,48,768]{2,1,0:T(8,128)(2,1)S(1)} %collective-permute-done.3), channel_id=1, source_target_pairs={{0,192},{1,193},{2,194},{3,195},{4,196},{5,197},{6,198},{7,199},{8... | collective-permute-start | bytes 1990664 | tf_op jit(solution)/shard_map/weights_first/ppermute | solution.py:36
  25.7 16.1 %collective-permute-start.6 = (bf16[9,48,768]{2,1,0:T(8,128)(2,1)S(1)}, bf16[9,48,768]{2,1,0:T(8,128)(2,1)}, u32[]{:S(2)}, u32[]{:S(2)}) collective-permute-start(bf16[9,48,768]{2,1,0:T(8,128)(2,1)S(1)} %collective-permute-done.3), channel_id=1, source_target_pairs={{0,64},{1,65},{2,66},{3,67},{4,68},{5,69},{6,70},{7,71},{8,72},{9,... | collective-permute-start | bytes 1990664 | tf_op jit(solution)/shard_map/weights_first/ppermute | solution.py:36
  41.8 5.4 %copy-start.13 = (bf16[9,48,768]{2,1,0:T(8,128)(2,1)}, bf16[9,48,768]{2,1,0:T(8,128)(2,1)S(1)}, u32[]{:S(2)}) copy-start(bf16[9,48,768]{2,1,0:T(8,128)(2,1)S(1)} %collective-permute-done.5) | copy-start | bytes 1990660
  43.2 7.1 %copy-start.3 = (bf16[4,5,48,768]{3,2,1,0:T(8,128)(2,1)}, bf16[4,5,48,768]{3,2,1,0:T(8,128)(2,1)S(1)}, u32[]{:S(2)}) copy-start(bf16[4,5,48,768]{3,2,1,0:T(8,128)(2,1)S(1)} %fusion.7.refs_3_) | copy-start | bytes 4423684
  43.2 20.9 %collective-permute-start.8 = (bf16[4,5,48,768]{3,2,1,0:T(8,128)(2,1)S(1)}, bf16[4,5,48,768]{3,2,1,0:T(8,128)(2,1)S(1)}, u32[]{:S(2)}, u32[]{:S(2)}) collective-permute-start(bf16[4,5,48,768]{3,2,1,0:T(8,128)(2,1)S(1)} %fusion.7.refs_3_), channel_id=1, source_target_pairs={{0,33},{1,0},{2,35},{3,2},{4,37},{5,4},{6,39},{7,6},{8,41},{9,8},{... | collective-permute-start | bytes 4423688 | tf_op jit(solution)/shard_map/conv_second/ppermute | solution.py:36
  47.2 24.1 %collective-permute-start.7 = (bf16[4,5,48,768]{3,2,1,0:T(8,128)(2,1)S(1)}, bf16[4,5,48,768]{3,2,1,0:T(8,128)(2,1)}, u32[]{:S(2)}, u32[]{:S(2)}) collective-permute-start(bf16[4,5,48,768]{3,2,1,0:T(8,128)(2,1)S(1)} %fusion.7.refs_3_), channel_id=1, source_target_pairs={{0,1},{1,32},{2,3},{3,34},{4,5},{5,36},{6,7},{7,38},{8,9},{9,40},{... | collective-permute-start | bytes 4423688 | tf_op jit(solution)/shard_map/conv_second/ppermute | solution.py:36
  48.2 22.0 %copy-start.23 = (f32[1536]{0:T(1024)S(1)}, f32[1536]{0:T(1024)}, u32[]{:S(2)}) copy-start(f32[1536]{0:T(1024)} %param.10) | copy-start | bytes 18436
  66.3 8.1 %copy-start.5 = (bf16[4,4,48,768]{3,2,1,0:T(8,128)(2,1)}, bf16[4,4,48,768]{3,2,1,0:T(8,128)(2,1)S(1)}, u32[]{:S(2)}) copy-start(bf16[4,4,48,768]{3,2,1,0:T(8,128)(2,1)S(1)} %fusion.11.g0) | copy-start | bytes 3538948
  66.4 23.6 %collective-permute-start.13 = (bf16[4,4,48,768]{3,2,1,0:T(8,128)(2,1)S(1)}, bf16[4,4,48,768]{3,2,1,0:T(8,128)(2,1)}, u32[]{:S(2)}, u32[]{:S(2)}) collective-permute-start(bf16[4,4,48,768]{3,2,1,0:T(8,128)(2,1)S(1)} %fusion.11.g0), channel_id=1, source_target_pairs={{0,1},{1,32},{2,3},{3,34},{4,5},{5,36},{6,7},{7,38},{8,9},{9,40},{... | collective-permute-start | bytes 3538952 | tf_op jit(solution)/shard_map/qkv_second/ppermute | solution.py:36
  67.5 24.5 %collective-permute-start.14 = (bf16[4,4,48,768]{3,2,1,0:T(8,128)(2,1)S(1)}, bf16[4,4,48,768]{3,2,1,0:T(8,128)(2,1)}, u32[]{:S(2)}, u32[]{:S(2)}) collective-permute-start(bf16[4,4,48,768]{3,2,1,0:T(8,128)(2,1)S(1)} %fusion.11.g0), channel_id=1, source_target_pairs={{0,33},{1,0},{2,35},{3,2},{4,37},{5,4},{6,39},{7,6},{8,41},{9,8},{... | collective-permute-start | bytes 3538952 | tf_op jit(solution)/shard_map/qkv_second/ppermute | solution.py:36
  73.5 22.9 %collective-permute-start.9 = (bf16[2,5,48,768]{3,2,1,0:T(8,128)(2,1)}, bf16[2,5,48,768]{3,2,1,0:T(8,128)(2,1)S(1)}, u32[]{:S(2)}, u32[]{:S(2)}) collective-permute-start(bf16[2,5,48,768]{3,2,1,0:T(8,128)(2,1)} %slice.158), channel_id=1, source_target_pairs={{0,1},{1,32},{2,3},{3,34},{4,5},{5,36},{6,7},{7,38},{8,9},{9,40},{... | collective-permute-start | bytes 2211848 | tf_op jit(solution)/shard_map/conv_far/ppermute | solution.py:36
  74.4 22.0 %collective-permute-start.10 = (bf16[2,5,48,768]{3,2,1,0:T(8,128)(2,1)}, bf16[2,5,48,768]{3,2,1,0:T(8,128)(2,1)S(1)}, u32[]{:S(2)}, u32[]{:S(2)}) collective-permute-start(bf16[2,5,48,768]{3,2,1,0:T(8,128)(2,1)} %slice.159), channel_id=1, source_target_pairs={{0,33},{1,0},{2,35},{3,2},{4,37},{5,4},{6,39},{7,6},{8,41},{9,8},{... | collective-permute-start | bytes 2211848 | tf_op jit(solution)/shard_map/conv_far/ppermute | solution.py:36
  89.9 15.6 %collective-permute-start.11 = (bf16[12,48,512]{2,1,0:T(8,128)(2,1)}, bf16[12,48,512]{2,1,0:T(8,128)(2,1)}, u32[]{:S(2)}, u32[]{:S(2)}) collective-permute-start(bf16[12,48,512]{2,1,0:T(8,128)(2,1)} %conv_kernel.2.refs_3_.ma), channel_id=1, source_target_pairs={{0,16},{1,17},{2,18},{3,19},{4,20},{5,21},{6,22},{7,23},{8,24},{9,... | collective-permute-start | bytes 1769480 | tf_op jit(solution)/shard_map/pooled_core/ppermute | solution.py:36
  92.0 14.5 %collective-permute-start.15 = (bf16[2,4,48,768]{3,2,1,0:T(8,128)(2,1)}, bf16[2,4,48,768]{3,2,1,0:T(8,128)(2,1)}, u32[]{:S(2)}, u32[]{:S(2)}) collective-permute-start(bf16[2,4,48,768]{3,2,1,0:T(8,128)(2,1)} %slice.165), channel_id=1, source_target_pairs={{0,1},{1,32},{2,3},{3,34},{4,5},{5,36},{6,7},{7,38},{8,9},{9,40},{... | collective-permute-start | bytes 1769480 | tf_op jit(solution)/shard_map/qkv_far/ppermute | solution.py:36
  93.1 11.7 %copy-start.22 = (f32[1536]{0:T(1024)S(1)}, f32[1536]{0:T(1024)}, u32[]{:S(2)}) copy-start(f32[1536]{0:T(1024)} %param.11) | copy-start | bytes 18436
  93.1 13.4 %collective-permute-start.16 = (bf16[2,4,48,768]{3,2,1,0:T(8,128)(2,1)S(1)}, bf16[2,4,48,768]{3,2,1,0:T(8,128)(2,1)}, u32[]{:S(2)}, u32[]{:S(2)}) collective-permute-start(bf16[2,4,48,768]{3,2,1,0:T(8,128)(2,1)S(1)} %slice.166), channel_id=1, source_target_pairs={{0,33},{1,0},{2,35},{3,2},{4,37},{5,4},{6,39},{7,6},{8,41},{9,8},{... | collective-permute-start | bytes 1769480 | tf_op jit(solution)/shard_map/qkv_far/ppermute | solution.py:36
  104.7 1.7 collective-permute-start.12
  115.7 25.8 %copy-start.14 = (bf16[4,192,256]{2,1,0:T(8,128)(2,1)S(1)}, bf16[4,192,256]{2,1,0:T(8,128)(2,1)}, u32[]{:S(2)}) copy-start(bf16[4,192,256]{2,1,0:T(8,128)(2,1)} %get-tuple-element.12) | copy-start | bytes 1179652
  117.0 16.2 %collective-permute-start.17 = (bf16[2,192,256]{2,1,0:T(8,128)(2,1)S(1)}, bf16[2,192,256]{2,1,0:T(8,128)(2,1)S(1)}, u32[]{:S(2)}, u32[]{:S(2)}) collective-permute-start(bf16[2,192,256]{2,1,0:T(8,128)(2,1)S(1)} %get-tuple-element.22), channel_id=1, source_target_pairs={{0,4},{1,5},{2,20},{3,21},{4,8},{5,9},{6,24},{7,25},{8,12},{9,13},... | collective-permute-start | bytes 589832 | tf_op jit(solution)/shard_map/keys_z/ppermute | solution.py:36
  120.5 16.6 %collective-permute-start.24 = (bf16[2,192,256]{2,1,0:T(8,128)(2,1)S(1)}, bf16[2,192,256]{2,1,0:T(8,128)(2,1)S(1)}, u32[]{:S(2)}, u32[]{:S(2)}) collective-permute-start(bf16[2,192,256]{2,1,0:T(8,128)(2,1)S(1)} %get-tuple-element.20), channel_id=1, source_target_pairs={{0,8},{1,9},{2,24},{3,25},{4,12},{5,13},{6,28},{7,29},{8,0},{9,1},... | collective-permute-start | bytes 589832 | tf_op jit(solution)/shard_map/keys_z/ppermute | solution.py:36
  125.1 12.0 %collective-permute-start.23 = (bf16[2,192,256]{2,1,0:T(8,128)(2,1)S(1)}, bf16[2,192,256]{2,1,0:T(8,128)(2,1)S(1)}, u32[]{:S(2)}, u32[]{:S(2)}) collective-permute-start(bf16[2,192,256]{2,1,0:T(8,128)(2,1)S(1)} %get-tuple-element.21), channel_id=1, source_target_pairs={{0,0},{1,1},{2,16},{3,17},{4,4},{5,5},{6,20},{7,21},{8,8},{9,9},{1... | collective-permute-start | bytes 589832 | tf_op jit(solution)/shard_map/keys_z/ppermute | solution.py:36
  125.8 14.2 %collective-permute-start.22 = (bf16[2,192,256]{2,1,0:T(8,128)(2,1)S(1)}, bf16[2,192,256]{2,1,0:T(8,128)(2,1)S(1)}, u32[]{:S(2)}, u32[]{:S(2)}) collective-permute-start(bf16[2,192,256]{2,1,0:T(8,128)(2,1)S(1)} %get-tuple-element.19), channel_id=1, source_target_pairs={{0,12},{1,13},{2,28},{3,29},{4,0},{5,1},{6,16},{7,17},{8,4},{9,5},... | collective-permute-start | bytes 589832 | tf_op jit(solution)/shard_map/keys_z/ppermute | solution.py:36
  140.1 21.6 %copy-start.9 = (bf16[4,2,192,256]{3,2,1,0:T(8,128)(2,1)}, bf16[4,2,192,256]{3,2,1,0:T(8,128)(2,1)S(1)}, u32[]{:S(2)}) copy-start(bf16[4,2,192,256]{3,2,1,0:T(8,128)(2,1)S(1)} %pad_maximum_fusion.g0) | copy-start | bytes 2359300
  140.1 20.5 %collective-permute-start.25 = (bf16[4,2,192,256]{3,2,1,0:T(8,128)(2,1)S(1)}, bf16[4,2,192,256]{3,2,1,0:T(8,128)(2,1)S(1)}, u32[]{:S(2)}, u32[]{:S(2)}) collective-permute-start(bf16[4,2,192,256]{3,2,1,0:T(8,128)(2,1)S(1)} %pad_maximum_fusion.g0), channel_id=1, source_target_pairs={{0,1},{1,0},{2,3},{3,2},{4,5},{5,4},{6,7},{7,6},{8,9},{9,8},{10,11... | collective-permute-start | bytes 2359304 | tf_op jit(solution)/shard_map/keys_y/ppermute | solution.py:36
  141.5 20.7 %copy-start.1 = (bf16[16,48,768]{2,1,0:T(8,128)(2,1)S(1)}, bf16[16,48,768]{2,1,0:T(8,128)(2,1)}, u32[]{:S(2)}) copy-start(bf16[16,48,768]{2,1,0:T(8,128)(2,1)} %get-tuple-element.18.mine) | copy-start | bytes 3538948
  141.6 10.3 %collective-permute-start.18 = (bf16[192,256]{1,0:T(8,128)(2,1)S(1)}, bf16[192,256]{1,0:T(8,128)(2,1)S(1)}, u32[]{:S(2)}, u32[]{:S(2)}) collective-permute-start(bf16[192,256]{1,0:T(8,128)(2,1)S(1)} %get-tuple-element.29), channel_id=1, source_target_pairs={{0,4},{1,5},{2,20},{3,21},{4,8},{5,9},{6,24},{7,25},{8,12},{9,13},... | collective-permute-start | bytes 294920 | tf_op jit(solution)/shard_map/queries_z/ppermute | solution.py:36
  145.1 11.3 %collective-permute-start.19 = (bf16[192,256]{1,0:T(8,128)(2,1)S(1)}, bf16[192,256]{1,0:T(8,128)(2,1)S(1)}, u32[]{:S(2)}, u32[]{:S(2)}) collective-permute-start(bf16[192,256]{1,0:T(8,128)(2,1)S(1)} %get-tuple-element.32), channel_id=1, source_target_pairs={{0,12},{1,13},{2,28},{3,29},{4,0},{5,1},{6,16},{7,17},{8,4},{9,5},... | collective-permute-start | bytes 294920 | tf_op jit(solution)/shard_map/queries_z/ppermute | solution.py:36
  146.2 12.1 %collective-permute-start.20 = (bf16[192,256]{1,0:T(8,128)(2,1)S(1)}, bf16[192,256]{1,0:T(8,128)(2,1)S(1)}, u32[]{:S(2)}, u32[]{:S(2)}) collective-permute-start(bf16[192,256]{1,0:T(8,128)(2,1)S(1)} %get-tuple-element.31), channel_id=1, source_target_pairs={{0,0},{1,1},{2,16},{3,17},{4,4},{5,5},{6,20},{7,21},{8,8},{9,9},{1... | collective-permute-start | bytes 294920 | tf_op jit(solution)/shard_map/queries_z/ppermute | solution.py:36
  146.8 12.6 %collective-permute-start.21 = (bf16[192,256]{1,0:T(8,128)(2,1)S(1)}, bf16[192,256]{1,0:T(8,128)(2,1)S(1)}, u32[]{:S(2)}, u32[]{:S(2)}) collective-permute-start(bf16[192,256]{1,0:T(8,128)(2,1)S(1)} %get-tuple-element.30), channel_id=1, source_target_pairs={{0,8},{1,9},{2,24},{3,25},{4,12},{5,13},{6,28},{7,29},{8,0},{9,1},... | collective-permute-start | bytes 294920 | tf_op jit(solution)/shard_map/queries_z/ppermute | solution.py:36
  151.9 11.4 %collective-permute-start.27 = (bf16[4,2,192,256]{3,2,1,0:T(8,128)(2,1)S(1)}, bf16[4,2,192,256]{3,2,1,0:T(8,128)(2,1)S(1)}, u32[]{:S(2)}, u32[]{:S(2)}) collective-permute-start(bf16[4,2,192,256]{3,2,1,0:T(8,128)(2,1)S(1)} %pad_maximum_fusion.g0), channel_id=1, source_target_pairs={{0,16},{1,17},{2,18},{3,19},{4,20},{5,21},{6,22},{7,23},{8,24},{9,... | collective-permute-start | bytes 2359304 | tf_op jit(solution)/shard_map/keys_core/ppermute | solution.py:36
  161.7 11.2 %collective-permute-start.26 = (bf16[4,2,192,256]{3,2,1,0:T(8,128)(2,1)}, bf16[4,2,192,256]{3,2,1,0:T(8,128)(2,1)}, u32[]{:S(2)}, u32[]{:S(2)}) collective-permute-start(bf16[4,2,192,256]{3,2,1,0:T(8,128)(2,1)} %broadcast_add_fusion.1), channel_id=1, source_target_pairs={{0,16},{1,17},{2,18},{3,19},{4,20},{5,21},{6,22},{7,23},{8,24},{9,... | collective-permute-start | bytes 2359304 | tf_op jit(solution)/shard_map/keys_y_core/ppermute | solution.py:36
  162.4 32.9 %collective-permute-start.32 = (bf16[16,48,768]{2,1,0:T(8,128)(2,1)S(1)}, bf16[16,48,768]{2,1,0:T(8,128)(2,1)S(1)}, u32[]{:S(2)}, u32[]{:S(2)}) collective-permute-start(bf16[16,48,768]{2,1,0:T(8,128)(2,1)S(1)} %broadcast_add_fusion), channel_id=1, source_target_pairs={{0,16},{1,17},{2,18},{3,19},{4,20},{5,21},{6,22},{7,23},{8,24},{9,... | collective-permute-start | bytes 3538952 | tf_op jit(solution)/shard_map/out_core/ppermute | solution.py:36
  183.4 11.9 %collective-permute-start.28 = (bf16[192,256]{1,0:T(8,128)(2,1)S(1)}, bf16[192,256]{1,0:T(8,128)(2,1)S(1)}, u32[]{:S(2)}, u32[]{:S(2)}) collective-permute-start(bf16[192,256]{1,0:T(8,128)(2,1)S(1)} %get-tuple-element.28), channel_id=1, source_target_pairs={{0,4},{1,5},{2,8},{3,9},{4,16},{5,17},{6,20},{7,21},{8,12},{9,13},... | collective-permute-start | bytes 294920 | tf_op jit(solution)/shard_map/heads_back/ppermute | solution.py:36
  185.9 9.4 %collective-permute-start.29 = (bf16[192,256]{1,0:T(8,128)(2,1)S(1)}, bf16[192,256]{1,0:T(8,128)(2,1)S(1)}, u32[]{:S(2)}, u32[]{:S(2)}) collective-permute-start(bf16[192,256]{1,0:T(8,128)(2,1)S(1)} %get-tuple-element.27), channel_id=1, source_target_pairs={{0,12},{1,13},{2,0},{3,1},{4,28},{5,29},{6,24},{7,25},{8,4},{9,5},... | collective-permute-start | bytes 294920 | tf_op jit(solution)/shard_map/heads_back/ppermute | solution.py:36
  189.5 5.8 %collective-permute-start.30 = (bf16[192,256]{1,0:T(8,128)(2,1)S(1)}, bf16[192,256]{1,0:T(8,128)(2,1)S(1)}, u32[]{:S(2)}, u32[]{:S(2)}) collective-permute-start(bf16[192,256]{1,0:T(8,128)(2,1)S(1)} %get-tuple-element.26), channel_id=1, source_target_pairs={{0,0},{1,1},{2,12},{3,13},{4,24},{5,25},{6,28},{7,29},{8,8},{9,9},... | collective-permute-start | bytes 294920 | tf_op jit(solution)/shard_map/heads_back/ppermute | solution.py:36
  190.2 11.2 %collective-permute-start.31 = (bf16[192,256]{1,0:T(8,128)(2,1)S(1)}, bf16[192,256]{1,0:T(8,128)(2,1)S(1)}, u32[]{:S(2)}, u32[]{:S(2)}) collective-permute-start(bf16[192,256]{1,0:T(8,128)(2,1)S(1)} %get-tuple-element.25), channel_id=1, source_target_pairs={{0,8},{1,9},{2,4},{3,5},{4,20},{5,21},{6,16},{7,17},{8,0},{9,1},{1... | collective-permute-start | bytes 294920 | tf_op jit(solution)/shard_map/heads_back/ppermute | solution.py:36
  195.2 6.2 %copy-start.4 = (bf16[16,48,768]{2,1,0:T(8,128)(2,1)}, bf16[16,48,768]{2,1,0:T(8,128)(2,1)S(1)}, u32[]{:S(2)}) copy-start(bf16[16,48,768]{2,1,0:T(8,128)(2,1)S(1)} %collective-permute-done.32.theirs) | copy-start | bytes 3538948
  195.2 6.2 %copy-start.17 = (bf16[192,256]{1,0:T(8,128)(2,1)}, bf16[192,256]{1,0:T(8,128)(2,1)S(1)}, u32[]{:S(2)}) copy-start(bf16[192,256]{1,0:T(8,128)(2,1)S(1)} %collective-permute-done.28.h0) | copy-start | bytes 294916
  195.3 6.1 %copy-start.18 = (bf16[192,256]{1,0:T(8,128)(2,1)}, bf16[192,256]{1,0:T(8,128)(2,1)S(1)}, u32[]{:S(2)}) copy-start(bf16[192,256]{1,0:T(8,128)(2,1)S(1)} %collective-permute-done.29.h1) | copy-start | bytes 294916
  195.3 6.1 %copy-start.19 = (bf16[192,256]{1,0:T(8,128)(2,1)}, bf16[192,256]{1,0:T(8,128)(2,1)S(1)}, u32[]{:S(2)}) copy-start(bf16[192,256]{1,0:T(8,128)(2,1)S(1)} %collective-permute-done.30.h2) | copy-start | bytes 294916
  (11 other events, 13.4 us)
